TPU v7x, 256 devices: a whole 4x4x8 slice. The times are simulated.
256 devices in a mesh: bx: 8 (over z), by: 16 (over y, x), bz: 2 (over core).
Axes of the slice: x: 4, y: 4, z: 8, core: 2. Of those that a mesh axis runs over, the one named last changes fastest.
Arguments:
- velocity: float32 [2048, 3, 39304], P(('bx', 'by', 'bz')), may hold values from -5 to 5, as said below
- fraction: int32 [2048, 39304], P(('bx', 'by', 'bz')), may hold values from 0 to 256, as said below
- placement: int32 [8, 16, 2, 4], P('bx', None, 'bz'), may hold values from 0 to 15, as said below
Outputs:
- velocity_out: float32 [2048, 3, 32768], P(('bx', 'by', 'bz'))
- pressure: float32 [256, 512, 256], P('bx', 'by', 'bz')
Inputs may be any that keep to these rules, and one draw needn't show every extreme that they name: placement[x, b, z, k] is the owner code c of box k of the brick (x, b, z): that box lives on the device (x, c, z). The 4 codes of one brick are distinct. Each device holds at most 8 boxes, and in every line of fixed (x, z) some device holds exactly 8. `velocity`: slot s of the device (x, y, z) holds that device's s-th box in the order of (its brick's y index, k); ghost cells equal the neighbouring cells of the grid and are zero outside it; slots beyond the device's count of boxes are zero. `fraction`: same slots and ghost layers as velocity; 256 in regular cells, 32 to 255 in cut cells, zero outside the grid and in unused slots.
All inputs are finite; a program needn't handle non-finite values.
Results may differ from a plain program's by a relative error of at most 0.0003.
Values sent between devices are 32-bit elements; how exact they have to be, the bound alone decides.
No kernel may reach another device: no remote copies, remote signals or barrier semaphores. Data moves between devices by JAX's collectives and lax.ppermute only.
A program may use at most 128 MiB of HBM per device.

v0:
```python
import functools

import jax
import jax.numpy as jnp
from jax import lax
from jax.experimental import pallas as pl
from jax.experimental.pallas import tpu as pltpu
from jax.sharding import PartitionSpec as P

BOX = 32
ITERS = 4
PADDED = BOX + 2
PLANE = PADDED * PADDED
TILE = 128
WIDE = 10 * TILE
INNER = BOX * BOX
TILES = INNER // TILE
PER_TILE = TILE // BOX
ROWS = BOX * TILES
RETURN_ROWS = PADDED * TILES + 4 * TILES
STEP_DT = 0.25
SHIFT_WEIGHT = 0.5
LOWER_BOUND = 0.5 / 6.5
UPPER_BOUND = 2.0

VMEM_SPEC = pl.BlockSpec(memory_space=pltpu.VMEM)
SMEM_SPEC = pl.BlockSpec(memory_space=pltpu.SMEM)
ANY_SPEC = pl.BlockSpec(memory_space=pl.ANY)


def lane_index():
    return lax.broadcasted_iota(jnp.int32, (8, TILE), 1)


def inside_plane():
    flat = lax.broadcasted_iota(jnp.int32, (8, WIDE), 1)
    row = flat // PADDED
    col = flat % PADDED
    return (row >= 1) & (row <= BOX) & (col >= 1) & (col <= BOX)


def ahead(values, offset):
    return pltpu.roll(values, WIDE - offset, 1)


def behind(values, offset):
    return pltpu.roll(values, offset, 1)


def compact(values, offset, lanes):
    tiles = [values[:, t * TILE : (t + 1) * TILE] for t in range(WIDE // TILE)]
    out = []
    for q in range(TILES):
        pieces = []
        for r in range(PER_TILE):
            start = (q * PER_TILE + r + 1) * PADDED + 1 + offset
            index, lane = divmod(start, TILE)
            shift = (BOX * r - lane) % TILE
            piece = pltpu.roll(tiles[index], shift, 1) if shift else tiles[index]
            if lane + BOX > TILE:
                rest = pltpu.roll(tiles[index + 1], shift, 1) if shift else tiles[index + 1]
                piece = jnp.where(lanes < BOX * r + TILE - lane, piece, rest)
            pieces.append(piece)
        value = pieces[-1]
        for r in reversed(range(PER_TILE - 1)):
            value = jnp.where(lanes < BOX * (r + 1), pieces[r], value)
        out.append(value)
    return out


def aligned_plane(load, x, lanes):
    start = x * (PLANE // TILE) + (x * (PLANE % TILE)) // TILE
    amount = (x * (PLANE % TILE)) % TILE
    block = load(pl.multiple_of(start * TILE, TILE))
    tiles = [
        pltpu.roll(block[:, t * TILE : (t + 1) * TILE], TILE - amount, 1)
        for t in range(WIDE // TILE)
    ]
    keep = lanes < TILE - amount
    return [
        jnp.where(keep, tiles[t], tiles[t + 1]) if t + 1 < len(tiles) else tiles[t]
        for t in range(len(tiles))
    ]


def store_plane(ref, index, tiles):
    for t, tile in enumerate(tiles):
        ref[index + (slice(None), slice(t * TILE, (t + 1) * TILE))] = tile


def last_plane(ref_tail, out_ref, index):
    tail = ref_tail
    start = (PADDED - 1) * PLANE
    first = start // TILE * TILE
    span = PADDED * PLANE - first
    tail_block = jnp.concatenate([tail, jnp.zeros((8, WIDE - span), jnp.float32)], axis=1)
    out_ref[index] = pltpu.roll(tail_block, WIDE - (start - first), 1)


def put_rows(ref, x, tiles):
    for q, tile in enumerate(tiles):
        ref[pl.ds(x * TILES + q, 8, stride=ROWS), :] = tile


def send_rows(slots, rows_ref, out_ref, sem, count):
    copies = [
        pltpu.make_async_copy(
            rows_ref.at[pl.ds(pl.multiple_of(slots[d] * ROWS, ROWS), ROWS)],
            out_ref.at[d],
            sem.at[d],
        )
        for d in range(count)
    ]
    for copy in copies:
        copy.start()
    for copy in copies:
        copy.wait()


def volume_kernel(slots, fraction, planes, rows, packed, tail, sem, *, lanes_by):
    lanes = lane_index()

    def align(x):
        tiles = aligned_plane(
            lambda s: fraction[:, pl.ds(s, WIDE)].astype(jnp.float32) * (1.0 / 256.0), x, lanes
        )
        store_plane(planes, (x,), tiles)

    def body(x, carry):
        align(x)
        return carry

    lax.fori_loop(0, PADDED - 1, body, 0)
    start = (PADDED - 1) * PLANE
    first = start // TILE * TILE
    span = PADDED * PLANE - first
    tail[...] = jnp.zeros_like(tail)
    tail[:, 0:span] = fraction[:, first : PADDED * PLANE].astype(jnp.float32) * (1.0 / 256.0)
    planes[PADDED - 1] = ahead(tail[...], start - first)

    def pack(x, carry):
        put_rows(packed, x, compact(planes[x + 1], 0, lanes))
        return carry

    lax.fori_loop(0, BOX, pack, 0)
    send_rows(slots, packed, rows, sem, lanes_by)


def flux_kernel(slots, velocity, planes, masses, rows, field, tail, carry_ref, packed, sem, *, lanes_by):
    lanes = lane_index()
    inside = inside_plane()

    def align(x):
        for c in range(3):
            store_plane(field, (x, c), aligned_plane(lambda s: velocity[c, :, pl.ds(s, WIDE)], x, lanes))

    def align_body(x, carry):
        align(x)
        return carry

    lax.fori_loop(0, PADDED - 1, align_body, 0)
    start = (PADDED - 1) * PLANE
    first = start // TILE * TILE
    span = PADDED * PLANE - first
    tail[...] = jnp.zeros_like(tail)
    for c in range(3):
        tail[:, 0:span] = velocity[c, :, first : PADDED * PLANE]
        field[PADDED - 1, c] = ahead(tail[...], start - first)

    def face(volume, volume_ahead, here, there, heading):
        speed = 0.5 * (here[heading] + there[heading])
        flow = jnp.minimum(volume, volume_ahead) * speed
        upwind = speed > 0.0
        return [flow * jnp.where(upwind, here[c], there[c]) for c in range(3)] + [flow]

    def x_face(x):
        return face(
            planes[x], planes[x + 1], [field[x, c] for c in range(3)], [field[x + 1, c] for c in range(3)], 0
        )

    for c, value in enumerate(x_face(0)):
        carry_ref[c] = value
    for c in range(3):
        masses[0, c] = jnp.zeros((8, WIDE), jnp.float32)
        masses[PADDED - 1, c] = jnp.zeros((8, WIDE), jnp.float32)

    def step(x, carry):
        volume = planes[x]
        here = [field[x, c] for c in range(3)]
        upper = x_face(x)
        total = [upper[c] - carry_ref[c] for c in range(4)]
        for c in range(4):
            carry_ref[c] = upper[c]
        for heading, offset in ((1, PADDED), (2, 1)):
            faces = face(volume, ahead(volume, offset), here, [ahead(v, offset) for v in here], heading)
            total = [total[c] + faces[c] - behind(faces[c], offset) for c in range(4)]
        for c in range(3):
            masses[x, c] = jnp.where(inside, volume * here[c] - STEP_DT * total[c], 0.0)
        put_rows(packed, x - 1, compact(-total[3], 0, lanes))
        return carry

    lax.fori_loop(1, PADDED - 1, step, 0)
    send_rows(slots, packed, rows, sem, lanes_by)


def update_kernel(masses, planes, updated, apertures):
    lanes = lane_index()
    inside = inside_plane()

    def put(ref, index, tiles):
        for q, tile in enumerate(tiles):
            ref[index + (slice(None), slice(q * TILE, (q + 1) * TILE))] = tile

    def neighbours(here, below, above):
        total = here + below + above
        for offset in (PADDED, 1):
            total = total + ahead(here, offset) + behind(here, offset)
        return total

    def step(x, carry):
        volume = planes[x]
        weight = jnp.where(inside, volume, 0.0)
        below = jnp.where(inside & (x > 1), planes[x - 1], 0.0)
        above = jnp.where(inside & (x < BOX), planes[x + 1], 0.0)
        weights = neighbours(weight, below, above)
        inverse = 1.0 / jnp.where(weights > 0.0, weights, 1.0)
        cut = volume < 1.0
        for c in range(3):
            here = masses[x, c]
            spread = neighbours(here, masses[x - 1, c], masses[x + 1, c]) * inverse
            put(updated, (x - 1, c), compact(jnp.where(cut, spread, here), 0, lanes))
        put(apertures, (x - 1, 0), compact(jnp.minimum(volume, planes[x - 1]), 0, lanes))
        put(apertures, (x - 1, 1), compact(jnp.minimum(volume, planes[x + 1]), 0, lanes))
        for axis, offset in ((1, PADDED), (2, 1)):
            aperture = jnp.minimum(volume, ahead(volume, offset))
            put(apertures, (x - 1, 2 * axis), compact(aperture, -offset, lanes))
            put(apertures, (x - 1, 2 * axis + 1), compact(aperture, 0, lanes))
        return carry

    lax.fori_loop(1, PADDED - 1, step, 0)


STEP_X = 4


def correct_kernel(rows, updated, apertures, returned, out, boxes, sem):
    step = pl.program_id(0)
    lanes = lane_index()

    @pl.when(step == 0)
    def _():
        copies = [
            pltpu.make_async_copy(
                returned.at[rows[s]], boxes.at[pl.ds(s * RETURN_ROWS, RETURN_ROWS)], sem.at[s]
            )
            for s in range(8)
        ]
        for copy in copies:
            copy.start()
        for copy in copies:
            copy.wait()

    def tile_of(row):
        return boxes[pl.ds(row, 8, stride=RETURN_ROWS), :]

    base = step * STEP_X
    faces = [
        tile_of(PADDED * TILES + f * TILES + step) for f in range(4)
    ]

    for i in range(STEP_X):
        x = base + i
        below = [tile_of(x * TILES + q) for q in range(TILES)]
        here = [tile_of((x + 1) * TILES + q) for q in range(TILES)]
        above = [tile_of((x + 2) * TILES + q) for q in range(TILES)]
        y_low, y_high = [
            pltpu.roll(faces[f], (TILE - BOX * i) % TILE, 1) if i else faces[f] for f in (0, 1)
        ]
        z_low, z_high = faces[2], faces[3]
        quarter = [pltpu.roll(t, BOX, 1) for t in here]
        reverse = [pltpu.roll(t, TILE - BOX, 1) for t in here]
        for q in range(TILES):
            p = here[q]
            before = quarter[q - 1] if q else pltpu.roll(y_low, 0, 1)
            y_behind = jnp.where(lanes < BOX, before, quarter[q])
            after = reverse[q + 1] if q + 1 < TILES else pltpu.roll(y_high, TILE - BOX, 1)
            y_ahead = jnp.where(lanes < TILE - BOX, reverse[q], after)
            z_behind = pltpu.roll(p, 1, 1)
            z_ahead = pltpu.roll(p, TILE - 1, 1)
            for r in range(PER_TILE):
                source = BOX * i + PER_TILE * q + r
                low = pltpu.roll(z_low, (BOX * r - source) % TILE, 1)
                high = pltpu.roll(z_high, (BOX * r + BOX - 1 - source) % TILE, 1)
                z_behind = jnp.where(lanes == BOX * r, low, z_behind)
                z_ahead = jnp.where(lanes == BOX * r + BOX - 1, high, z_ahead)
            cut = slice(q * TILE, (q + 1) * TILE)
            around = ((below[q], above[q]), (y_behind, y_ahead), (z_behind, z_ahead))
            for c, (lower, upper) in enumerate(around):
                slope = 0.5 * (
                    apertures[i, 2 * c + 1, :, cut] * (upper - p)
                    + apertures[i, 2 * c, :, cut] * (p - lower)
                )
                out[c, :, i * INNER + q * TILE : i * INNER + (q + 1) * TILE] = updated[i, c, :, cut] - slope


def struct(*shape):
    return jax.ShapeDtypeStruct(shape, jnp.float32)


def volume_call(send_slot, fraction):
    lanes_by = send_slot.shape[0]
    return pl.pallas_call(
        functools.partial(volume_kernel, lanes_by=lanes_by),
        in_specs=[SMEM_SPEC, VMEM_SPEC],
        out_specs=[VMEM_SPEC, ANY_SPEC],
        out_shape=[struct(PADDED, 8, WIDE), struct(lanes_by, ROWS, TILE)],
        scratch_shapes=[
            pltpu.VMEM((8 * ROWS, TILE), jnp.float32),
            pltpu.VMEM((8, WIDE), jnp.float32),
            pltpu.SemaphoreType.DMA((lanes_by,)),
        ],
        name="volume_rows",
    )(send_slot, fraction)


def flux_call(send_slot, velocity, planes):
    lanes_by = send_slot.shape[0]
    return pl.pallas_call(
        functools.partial(flux_kernel, lanes_by=lanes_by),
        in_specs=[SMEM_SPEC, VMEM_SPEC, VMEM_SPEC],
        out_specs=[VMEM_SPEC, ANY_SPEC],
        out_shape=[struct(PADDED, 3, 8, WIDE), struct(lanes_by, ROWS, TILE)],
        scratch_shapes=[
            pltpu.VMEM((PADDED, 3, 8, WIDE), jnp.float32),
            pltpu.VMEM((8, WIDE), jnp.float32),
            pltpu.VMEM((4, 8, WIDE), jnp.float32),
            pltpu.VMEM((8 * ROWS, TILE), jnp.float32),
            pltpu.SemaphoreType.DMA((lanes_by,)),
        ],
        name="flux_rows",
    )(send_slot, velocity, planes)


def update_call(masses, planes):
    return pl.pallas_call(
        update_kernel,
        in_specs=[VMEM_SPEC, VMEM_SPEC],
        out_specs=[VMEM_SPEC, VMEM_SPEC],
        out_shape=[struct(BOX, 3, 8, INNER), struct(BOX, 6, 8, INNER)],
        name="updated",
    )(masses, planes)


def correct_call(slot_row, updated, apertures, returned):
    return pl.pallas_call(
        correct_kernel,
        grid=(BOX // STEP_X,),
        in_specs=[
            SMEM_SPEC,
            pl.BlockSpec((STEP_X, 3, 8, INNER), lambda i: (i, 0, 0, 0)),
            pl.BlockSpec((STEP_X, 6, 8, INNER), lambda i: (i, 0, 0, 0)),
            ANY_SPEC,
        ],
        out_specs=pl.BlockSpec((3, 8, STEP_X * INNER), lambda i: (0, 0, i)),
        out_shape=struct(3, 8, BOX * INNER),
        scratch_shapes=[
            pltpu.VMEM((8 * RETURN_ROWS, TILE), jnp.float32),
            pltpu.SemaphoreType.DMA((8,)),
        ],
        name="corrected",
    )(slot_row, updated, apertures, returned)


def extended(cells, sides, width):
    for axis, dim in sides:
        count = lax.axis_size(axis)
        ends = count - 1
        head = lax.slice_in_dim(cells, 0, width, axis=dim)
        tail = lax.slice_in_dim(cells, cells.shape[dim] - width, cells.shape[dim], axis=dim)
        cells = jnp.concatenate(
            [
                lax.ppermute(tail, axis, [(i, (i + 1) % count) for i in range(ends)]),
                cells,
                lax.ppermute(head, axis, [((i + 1) % count, i) for i in range(ends)]),
            ],
            axis=dim,
        )
    return cells


def sides(rimmed):
    return [
        (rimmed[2:, 1:-1, 1:-1], rimmed[:-2, 1:-1, 1:-1]),
        (rimmed[1:-1, 2:, 1:-1], rimmed[1:-1, :-2, 1:-1]),
        (rimmed[1:-1, 1:-1, 2:], rimmed[1:-1, 1:-1, :-2]),
    ]


def operator_parts(volume, volume_rimmed):
    apertures = []
    diagonal = SHIFT_WEIGHT * volume
    for upper_side, lower_side in sides(volume_rimmed):
        upper_ap = jnp.minimum(volume, upper_side)
        lower_ap = jnp.minimum(lower_side, volume)
        apertures.append((upper_ap, lower_ap))
        diagonal = diagonal + upper_ap + lower_ap
    return (apertures, diagonal)


def apply_operator(search, search_rimmed, apertures, diagonal):
    total = jnp.zeros_like(search)
    for (upper_side, lower_side), (upper_ap, lower_ap) in zip(sides(search_rimmed), apertures):
        total = total + upper_ap * upper_side + lower_ap * lower_side
    return diagonal * search - total


def to_brick(rows):
    count = rows.shape[0]
    cube = rows.reshape(count, BOX, TILES, PER_TILE, BOX)
    return cube.transpose(1, 2, 3, 0, 4).reshape(BOX, BOX, count * BOX)


def return_box(rimmed, k):
    low = k * BOX
    core = rimmed[:, 1:-1, low + 1 : low + 1 + BOX].reshape(PADDED * TILES, TILE)
    y_faces = [rimmed[1:-1, y, low + 1 : low + 1 + BOX] for y in (0, BOX + 1)]
    z_faces = [rimmed[1:-1, 1:-1, z] for z in (low, low + BOX + 1)]
    return jnp.concatenate([core] + [f.reshape(TILES, TILE) for f in y_faces + z_faces], axis=0)


def solve(source, volume):
    axes = (("bx", 0), ("by", 1), ("bz", 2))
    volume_rimmed = extended(volume, axes, 1)
    apertures, diagonal = operator_parts(volume, volume_rimmed)
    center = 0.5 * (UPPER_BOUND + LOWER_BOUND)
    halfwidth = 0.5 * (UPPER_BOUND - LOWER_BOUND)
    spread = center / halfwidth
    damping = 1.0 / spread
    pressure = jnp.zeros_like(source)
    residual = source
    search = residual / diagonal * (1.0 / center)
    for iteration in range(ITERS):
        pressure = pressure + search
        if iteration < ITERS - 1:
            residual = residual - apply_operator(search, extended(search, axes, 1), apertures, diagonal)
            damping_next = 1.0 / (2.0 * spread - damping)
            search = damping_next * damping * search + 2.0 * damping_next / halfwidth * (
                residual / diagonal
            )
            damping = damping_next
    return pressure, extended(pressure, axes, 1)


def routing(placement, capacity):
    lanes = lax.axis_size("by")
    own_index = lax.axis_index("by")
    table = placement[0, :, 0, :]
    per_brick = table.shape[1]
    entries = lanes * per_brick
    owners = table.reshape(entries)
    onehot = (owners[:, None] == jnp.arange(lanes, dtype=jnp.int32)[None, :]).astype(jnp.int32)
    ranks = jnp.sum((jnp.cumsum(onehot, axis=0) - onehot) * onehot, axis=1)
    matches = (table == own_index).astype(jnp.int32)
    send_slot = jnp.sum(matches * ranks.reshape(lanes, per_brick), axis=1)
    slot_match = (
        (owners == own_index)[:, None]
        & (ranks[:, None] == jnp.arange(capacity, dtype=jnp.int32)[None, :])
    ).astype(jnp.int32)
    row_value = jnp.arange(entries, dtype=jnp.int32) // per_brick
    slot_row = jnp.sum(slot_match * row_value[:, None], axis=0)
    brick_table = lax.dynamic_index_in_dim(table, own_index, 0, keepdims=False)
    all_rows = jnp.arange(lanes, dtype=jnp.int32)
    box_of_row = jnp.sum(
        (brick_table[None, :] == all_rows[:, None]).astype(jnp.int32)
        * jnp.arange(per_brick, dtype=jnp.int32)[None, :],
        axis=1,
    )
    return send_slot, slot_row, brick_table, box_of_row


def exchange(rows):
    return lax.all_to_all(rows, "by", split_axis=0, concat_axis=0, tiled=True)


def local(velocity, fraction, placement):
    send_slot, slot_row, brick_table, box_of_row = routing(placement, velocity.shape[0])
    planes, volume_rows = volume_call(send_slot, fraction)
    volume_recv = exchange(volume_rows)
    masses, source_rows = flux_call(send_slot, jnp.swapaxes(velocity, 0, 1), planes)
    source_recv = exchange(source_rows)
    updated, apertures = update_call(masses, planes)
    volume = to_brick(jnp.take(volume_recv, brick_table, axis=0))
    source = to_brick(jnp.take(source_recv, brick_table, axis=0))
    pressure, rimmed = solve(source, volume)
    boxes = jnp.stack([return_box(rimmed, k) for k in range(placement.shape[3])])
    returned = exchange(jnp.take(boxes, box_of_row, axis=0))
    corrected = correct_call(slot_row, updated, apertures, returned)
    return (jnp.swapaxes(corrected, 0, 1), pressure)


def solution(mesh):
    in_specs = (
        P(("bx", "by", "bz"), None, None),
        P(("bx", "by", "bz"), None),
        P("bx", None, "bz", None),
    )
    out_specs = (P(("bx", "by", "bz"), None, None), P("bx", "by", "bz"))
    return jax.shard_map(local, mesh=mesh, in_specs=in_specs, out_specs=out_specs, check_vma=False)
```

profile of v0, /device:TPU:98, one launch (start us, length us, event | category | flops | bytes accessed | tf_op | source)
XLA Modules:
  0.0 329.7 jit_solution(17425488084394787022)
XLA Ops:
  3.2 10.3 %volume_rows.1 = (f32[34,8,1280]{2,1,0:T(8,128)}, f32[16,256,128]{2,1,0:T(8,128)}) custom-call(s32[16]{0:T(128)} %select_reduce_fusion.3.slots, s32[8,39304]{1,0:T(8,128)} %fraction.1), custom_call_target="tpu_custom_call" | custom-call | tf_op jit(solution)/shard_map/volume_rows/pallas_call | solution.py:312
  13.6 7.5 %all-to-all-start.1 = ((f32[16,256,128]{2,1,0:T(8,128)}), f32[16,256,128]{2,1,0:T(8,128)S(1)}, u32[]{:S(2)}, u32[]{:S(2)}) async-start(f32[16,256,128]{2,1,0:T(8,128)} %get-tuple-element.14), calls=%async_computation.1 | async-start | bytes 4194304 | tf_op jit(solution)/shard_map/all_to_all | solution.py:482
  21.1 24.0 %flux_rows.1 = (f32[34,3,8,1280]{3,2,1,0:T(8,128)}, f32[16,256,128]{2,1,0:T(8,128)}) custom-call(s32[16]{0:T(128)} %select_reduce_fusion.3.slots, f32[3,8,39304]{2,1,0:T(8,128)} %bitcast.29, f32[34,8,1280]{2,1,0:T(8,128)} %get-tuple-element.9.planes), custom_call_target="tpu_custom_call" | custom-call | tf_op jit(solution)/shard_map/flux_rows/pallas_call | solution.py:328
  45.1 3.1 all-to-all-done.1
  48.2 8.9 %all-to-all-start = ((f32[16,256,128]{2,1,0:T(8,128)}), f32[16,256,128]{2,1,0:T(8,128)}, u32[]{:S(2)}, u32[]{:S(2)}) async-start(f32[16,256,128]{2,1,0:T(8,128)} %get-tuple-element.13), calls=%async_computation | async-start | bytes 4194304 | tf_op jit(solution)/shard_map/all_to_all | solution.py:482
  57.9 25.7 %all-to-all-done = f32[16,256,128]{2,1,0:T(8,128)} async-done(((f32[16,256,128]{2,1,0:T(8,128)}), f32[16,256,128]{2,1,0:T(8,128)}, u32[]{:S(2)}, u32[]{:S(2)}) %all-to-all-start) | async-done | bytes 2097184 | tf_op jit(solution)/shard_map/all_to_all | solution.py:482
  83.6 2.2 gather_fusion.1
  86.7 2.2 reshape.84
  89.0 3.4 %copy.82 = f32[4,32,8,4,32]{4,0,3,2,1:T(4,128)S(1)} copy(f32[4,32,8,4,32]{4,3,2,1,0:T(4,128)} %reshape.84) | data formatting | bytes 1048576 | tf_op jit(solution)/shard_map/reshape | solution.py:419
  92.5 5.0 %collective-permute-start.1 = (f32[1,32,128]{2,1,0:T(8,128)S(1)}, f32[1,32,128]{2,1,0:T(8,128)S(1)}, u32[]{:S(2)}, u32[]{:S(2)}) collective-permute-start(f32[1,32,128]{2,1,0:T(8,128)S(1)} %slice.256), channel_id=1, source_target_pairs={{0,32},{32,64},{64,96},{96,128},{128,160},{160,192},{192,224},{1,3... | collective-permute-start | bytes 49160 | tf_op jit(solution)/shard_map/ppermute | solution.py:382
  98.5 1.9 collective-permute-start
  100.5 4.8 %collective-permute-done = f32[1,32,128]{2,1,0:T(8,128)S(1)} collective-permute-done((f32[1,32,128]{2,1,0:T(8,128)S(1)}, f32[1,32,128]{2,1,0:T(8,128)S(1)}, u32[]{:S(2)}, u32[]{:S(2)}) %collective-permute-start) | collective-permute-done | bytes 16416 | tf_op jit(solution)/shard_map/ppermute | solution.py:384
  105.4 5.7 %collective-permute-start.2 = (f32[34,1,128]{2,1,0:T(1,128)S(1)}, f32[34,1,128]{2,1,0:T(1,128)S(1)}, u32[]{:S(2)}, u32[]{:S(2)}) collective-permute-start(f32[34,1,128]{2,1,0:T(1,128)S(1)} %get-tuple-element.57), channel_id=1, source_target_pairs={{2,0},{4,2},{6,4},{8,6},{10,8},{12,10},{14,12},{16,14},{18,16},{20... | collective-permute-start | bytes 52232 | tf_op jit(solution)/shard_map/ppermute | solution.py:384
  111.0 1.9 collective-permute-start.3
  113.0 3.7 %collective-permute-done.3 = f32[34,1,128]{2,1,0:T(1,128)S(1)} collective-permute-done((f32[34,1,128]{2,1,0:T(1,128)S(1)}, f32[34,1,128]{2,1,0:T(1,128)S(1)}, u32[]{:S(2)}, u32[]{:S(2)}) %collective-permute-start.3) | collective-permute-done | bytes 17440 | tf_op jit(solution)/shard_map/ppermute | solution.py:382
  120.3 2.1 reshape.82
  122.4 3.1 copy.83
  125.5 2.4 reshape.83
  129.5 1.9 collective-permute-start.7
  131.4 3.9 %collective-permute-start.6 = (f32[1,32,128]{2,1,0:T(8,128)S(1)}, f32[1,32,128]{2,1,0:T(8,128)S(1)}, u32[]{:S(2)}, u32[]{:S(2)}) collective-permute-start(f32[1,32,128]{2,1,0:T(8,128)S(1)} %get-tuple-element.66), channel_id=1, source_target_pairs={{32,0},{64,32},{96,64},{128,96},{160,128},{192,160},{224,192},{33,... | collective-permute-start | bytes 49160 | tf_op jit(solution)/shard_map/ppermute | solution.py:384
  135.3 2.9 collective-permute-done.6
  138.3 1.9 collective-permute-start.9
  140.2 4.1 %collective-permute-start.8 = (f32[34,1,128]{2,1,0:T(1,128)S(1)}, f32[34,1,128]{2,1,0:T(1,128)S(1)}, u32[]{:S(2)}, u32[]{:S(2)}) collective-permute-start(f32[34,1,128]{2,1,0:T(1,128)S(1)} %get-tuple-element.56), channel_id=1, source_target_pairs={{2,0},{4,2},{6,4},{8,6},{10,8},{12,10},{14,12},{16,14},{18,16},{20... | collective-permute-start | bytes 52232 | tf_op jit(solution)/shard_map/ppermute | solution.py:384
  144.3 1.5 collective-permute-done.8
  146.0 1.3 fusion.57
  147.3 1.5 copy.66
  150.0 1.5 copy.68
  151.5 3.0 collective-permute-start.11
  157.0 6.7 %multiply_add_fusion.1 = (f32[32,32,128]{2,1,0:T(8,128)S(1)}, f32[32,32,128]{2,1,0:T(8,128)}) fusion(f32[32,32,128]{2,1,0:T(8,128)S(1)} %reshape.83, f32[32,32,128]{2,1,0:T(8,128)S(1)} %reshape.85, f32[34,32,128]{2,1,0:T(8,128)S(1)} %constant_dynamic-update-slice_fusion, f32[34,1,128]{2,1,0:T(1,128)} %copy-done.5, ...), kind=kLoop, calls=%fused_computation.133 | loop fusion | flops 7864320 | bytes 3332160 | tf_op jit(solution)/shard_map/add | solution.py:447
  163.7 1.9 collective-permute-start.13
  165.7 3.9 %collective-permute-start.12 = (f32[1,32,128]{2,1,0:T(8,128)S(1)}, f32[1,32,128]{2,1,0:T(8,128)S(1)}, u32[]{:S(2)}, u32[]{:S(2)}) collective-permute-start(f32[1,32,128]{2,1,0:T(8,128)S(1)} %get-tuple-element.64), channel_id=1, source_target_pairs={{32,0},{64,32},{96,64},{128,96},{160,128},{192,160},{224,192},{33,... | collective-permute-start | bytes 49160 | tf_op jit(solution)/shard_map/ppermute | solution.py:384
  169.6 2.9 collective-permute-done.12
  172.5 4.2 %collective-permute-start.15 = (f32[34,1,128]{2,1,0:T(1,128)S(1)}, f32[34,1,128]{2,1,0:T(1,128)S(1)}, u32[]{:S(2)}, u32[]{:S(2)}) collective-permute-start(f32[34,1,128]{2,1,0:T(1,128)S(1)} %get-tuple-element.53), channel_id=1, source_target_pairs={{0,2},{2,4},{4,6},{6,8},{8,10},{10,12},{12,14},{14,16},{16,18},{18... | collective-permute-start | bytes 52232 | tf_op jit(solution)/shard_map/ppermute | solution.py:382
  176.7 1.9 collective-permute-start.14
  178.7 5.8 %collective-permute-done.14 = f32[34,1,128]{2,1,0:T(1,128)S(1)} collective-permute-done((f32[34,1,128]{2,1,0:T(1,128)S(1)}, f32[34,1,128]{2,1,0:T(1,128)S(1)}, u32[]{:S(2)}, u32[]{:S(2)}) %collective-permute-start.14) | collective-permute-done | bytes 17440 | tf_op jit(solution)/shard_map/ppermute | solution.py:384
  186.5 2.1 copy.70
  188.6 2.1 copy.72
  190.6 1.9 collective-permute-start.17
  194.4 1.6 collective-permute-done.16
  195.9 1.9 copy.71
  197.9 1.9 copy.73
  199.8 4.3 %multiply_add_fusion = f32[32,32,128]{2,1,0:T(8,128)S(1)} fusion(f32[32,32,128]{2,1,0:T(8,128)} %get-tuple-element.32, f32[32,32,128]{2,1,0:T(8,128)S(1)} %reshape.83, f32[34,1,128]{2,1,0:T(1,128)} %copy-done.11, f32[1,32,128]{2,1,0:T(8,128)} %copy-done.9, f32[32,32,128]{2,1,0:T(8,128)S(1)} %get-tuple-element.31, f32[1,32,128]{2,1,0:T(8,128)} %copy-done.8, ...), kind=kLoop, calls=%fused_computation.132 | loop fusion | flops 8388608 | bytes 3332160 | tf_op jit(solution)/shard_map/add | solution.py:447
  204.2 1.9 collective-permute-start.19
  206.1 3.9 %collective-permute-start.18 = (f32[1,32,128]{2,1,0:T(8,128)S(1)}, f32[1,32,128]{2,1,0:T(8,128)S(1)}, u32[]{:S(2)}, u32[]{:S(2)}) collective-permute-start(f32[1,32,128]{2,1,0:T(8,128)S(1)} %get-tuple-element.62), channel_id=1, source_target_pairs={{32,0},{64,32},{96,64},{128,96},{160,128},{192,160},{224,192},{33,... | collective-permute-start | bytes 49160 | tf_op jit(solution)/shard_map/ppermute | solution.py:384
  210.5 2.4 collective-permute-done.18
  213.0 3.9 %collective-permute-start.21 = (f32[34,1,128]{2,1,0:T(1,128)S(1)}, f32[34,1,128]{2,1,0:T(1,128)S(1)}, u32[]{:S(2)}, u32[]{:S(2)}) collective-permute-start(f32[34,1,128]{2,1,0:T(1,128)S(1)} %get-tuple-element.51), channel_id=1, source_target_pairs={{0,2},{2,4},{4,6},{6,8},{8,10},{10,12},{12,14},{14,16},{16,18},{18... | collective-permute-start | bytes 52232 | tf_op jit(solution)/shard_map/ppermute | solution.py:382
  216.9 1.9 collective-permute-start.20
  218.9 3.8 %collective-permute-done.20 = f32[34,1,128]{2,1,0:T(1,128)S(1)} collective-permute-done((f32[34,1,128]{2,1,0:T(1,128)S(1)}, f32[34,1,128]{2,1,0:T(1,128)S(1)}, u32[]{:S(2)}, u32[]{:S(2)}) %collective-permute-start.20) | collective-permute-done | bytes 17440 | tf_op jit(solution)/shard_map/ppermute | solution.py:384
  224.0 1.5 copy.74
  225.5 1.5 copy.76
  229.6 1.8 collective-permute-done.22
  233.8 8.3 %fusion.7 = f32[32,32,128]{2,1,0:T(8,128)S(1)} fusion(f32[34,34,1]{2,1,0:T(8,128)} %copy.77, f32[34,1,128]{2,1,0:T(1,128)} %copy-done.17, f32[34,1,128]{2,1,0:T(1,128)} %copy-done.16, f32[1,32,128]{2,1,0:T(8,128)} %copy-done.13, f32[32,32,128]{2,1,0:T(8,128)} %copy-done.3, f32[1,32,128]{2,1,0:T(8,128)} %copy-done.12, f32[34,34,1]{2,1,0:T(8,128)} %copy.75, ...), kind=kLoop, calls=%fused_computation.27 | loop fusion | flops 13107200 | bytes 3933280 | tf_op jit(solution)/shard_map/add | solution.py:443
  242.1 1.9 collective-permute-start.24
  244.0 3.9 %collective-permute-start.25 = (f32[1,32,128]{2,1,0:T(8,128)S(1)}, f32[1,32,128]{2,1,0:T(8,128)S(1)}, u32[]{:S(2)}, u32[]{:S(2)}) collective-permute-start(f32[1,32,128]{2,1,0:T(8,128)S(1)} %get-tuple-element.60), channel_id=1, source_target_pairs={{32,0},{64,32},{96,64},{128,96},{160,128},{192,160},{224,192},{33,... | collective-permute-start | bytes 49160 | tf_op jit(solution)/shard_map/ppermute | solution.py:384
  247.9 1.7 slice_reduce_fusion.5
  250.9 1.9 collective-permute-start.27
  252.8 4.1 %collective-permute-start.26 = (f32[34,1,128]{2,1,0:T(1,128)S(1)}, f32[34,1,128]{2,1,0:T(1,128)S(1)}, u32[]{:S(2)}, u32[]{:S(2)}) collective-permute-start(f32[34,1,128]{2,1,0:T(1,128)S(1)} %get-tuple-element.50), channel_id=1, source_target_pairs={{0,2},{2,4},{4,6},{6,8},{8,10},{10,12},{12,14},{14,16},{16,18},{18... | collective-permute-start | bytes 52232 | tf_op jit(solution)/shard_map/ppermute | solution.py:382
  260.5 1.3 collective-permute-start.29
  261.8 3.0 collective-permute-start.28
  266.6 1.7 broadcast_select_fusion
  268.3 11.2 %all-to-all-start.2 = ((f32[16,304,128]{2,1,0:T(8,128)}), f32[16,304,128]{2,1,0:T(8,128)S(1)}, u32[]{:S(2)}, u32[]{:S(2)}) async-start(f32[16,304,128]{2,1,0:T(8,128)} %broadcast_select_fusion), calls=%async_computation.2 | async-start | bytes 4980736 | tf_op jit(solution)/shard_map/all_to_all | solution.py:482
  279.5 37.0 %updated.1 = (f32[32,3,8,1024]{3,2,1,0:T(8,128)}, f32[32,6,8,1024]{3,2,1,0:T(8,128)}) custom-call(f32[34,3,8,1280]{3,2,1,0:T(8,128)} %get-tuple-element.10.masses, f32[34,8,1280]{2,1,0:T(8,128)} %get-tuple-element.9.planes), custom_call_target="tpu_custom_call" | custom-call | tf_op jit(solution)/shard_map/updated/pallas_call | solution.py:345
  317.2 1.5 copy-done.2
  318.7 10.9 %corrected.1 = f32[3,8,32768]{2,1,0:T(8,128)} custom-call(s32[8]{0:T(128)} %select_reduce_fusion.1.rows, f32[32,3,8,1024]{3,2,1,0:T(8,128)} %get-tuple-element.11.updated, f32[32,6,8,1024]{3,2,1,0:T(8,128)} %get-tuple-element.12.apertures, f32[16,304,128]{2,1,0:T(8,128)} %copy-done.2), custom_call_target="tpu_custom_call" | custom-call | tf_op jit(solution)/shard_map/corrected/pallas_call | solution.py:355
  (176 shorter events, 32.2 us)
Async XLA Ops:
  13.6 34.6 %all-to-all-start.1 = ((f32[16,256,128]{2,1,0:T(8,128)}), f32[16,256,128]{2,1,0:T(8,128)S(1)}, u32[]{:S(2)}, u32[]{:S(2)}) async-start(f32[16,256,128]{2,1,0:T(8,128)} %get-tuple-element.14), calls=%async_computation.1 | async-start | bytes 4194304 | tf_op jit(solution)/shard_map/all_to_all | solution.py:482
  45.0 12.1 %copy-start.20 = (s32[1,16,1,4]{1,3,2,0:T(4,128)S(1)}, s32[1,16,1,4]{1,3,2,0:T(4,128)}, u32[]{:S(2)}) copy-start(s32[1,16,1,4]{1,3,2,0:T(4,128)} %param.7) | copy-start | bytes 772
  48.2 35.4 %all-to-all-start = ((f32[16,256,128]{2,1,0:T(8,128)}), f32[16,256,128]{2,1,0:T(8,128)}, u32[]{:S(2)}, u32[]{:S(2)}) async-start(f32[16,256,128]{2,1,0:T(8,128)} %get-tuple-element.13), calls=%async_computation | async-start | bytes 4194304 | tf_op jit(solution)/shard_map/all_to_all | solution.py:482
  92.5 8.0 %collective-permute-start.1 = (f32[1,32,128]{2,1,0:T(8,128)S(1)}, f32[1,32,128]{2,1,0:T(8,128)S(1)}, u32[]{:S(2)}, u32[]{:S(2)}) collective-permute-start(f32[1,32,128]{2,1,0:T(8,128)S(1)} %slice.256), channel_id=1, source_target_pairs={{0,32},{32,64},{64,96},{96,128},{128,160},{160,192},{192,224},{1,3... | collective-permute-start | bytes 49160 | tf_op jit(solution)/shard_map/ppermute | solution.py:382
  98.5 6.8 %collective-permute-start = (f32[1,32,128]{2,1,0:T(8,128)S(1)}, f32[1,32,128]{2,1,0:T(8,128)S(1)}, u32[]{:S(2)}, u32[]{:S(2)}) collective-permute-start(f32[1,32,128]{2,1,0:T(8,128)S(1)} %slice.253), channel_id=1, source_target_pairs={{32,0},{64,32},{96,64},{128,96},{160,128},{192,160},{224,192},{33,... | collective-permute-start | bytes 49160 | tf_op jit(solution)/shard_map/ppermute | solution.py:384
  100.4 28.3 %copy-start.6 = (f32[1,32,128]{2,1,0:T(8,128)}, f32[1,32,128]{2,1,0:T(8,128)S(1)}, u32[]{:S(2)}) copy-start(f32[1,32,128]{2,1,0:T(8,128)S(1)} %collective-permute-done.1) | copy-start | bytes 49156
  105.3 23.4 %copy-start.7 = (f32[1,32,128]{2,1,0:T(8,128)}, f32[1,32,128]{2,1,0:T(8,128)S(1)}, u32[]{:S(2)}) copy-start(f32[1,32,128]{2,1,0:T(8,128)S(1)} %collective-permute-done) | copy-start | bytes 49156
  105.4 7.6 %collective-permute-start.2 = (f32[34,1,128]{2,1,0:T(1,128)S(1)}, f32[34,1,128]{2,1,0:T(1,128)S(1)}, u32[]{:S(2)}, u32[]{:S(2)}) collective-permute-start(f32[34,1,128]{2,1,0:T(1,128)S(1)} %get-tuple-element.57), channel_id=1, source_target_pairs={{2,0},{4,2},{6,4},{8,6},{10,8},{12,10},{14,12},{16,14},{18,16},{20... | collective-permute-start | bytes 52232 | tf_op jit(solution)/shard_map/ppermute | solution.py:384
  111.0 5.6 %collective-permute-start.3 = (f32[34,1,128]{2,1,0:T(1,128)S(1)}, f32[34,1,128]{2,1,0:T(1,128)S(1)}, u32[]{:S(2)}, u32[]{:S(2)}) collective-permute-start(f32[34,1,128]{2,1,0:T(1,128)S(1)} %get-tuple-element.58), channel_id=1, source_target_pairs={{0,2},{2,4},{4,6},{6,8},{8,10},{10,12},{12,14},{14,16},{16,18},{18... | collective-permute-start | bytes 52232 | tf_op jit(solution)/shard_map/ppermute | solution.py:382
  116.7 12.1 %copy-start.5 = (f32[34,1,128]{2,1,0:T(1,128)}, f32[34,1,128]{2,1,0:T(1,128)S(1)}, u32[]{:S(2)}) copy-start(f32[34,1,128]{2,1,0:T(1,128)S(1)} %collective-permute-done.3) | copy-start | bytes 52228
  117.4 10.6 %collective-permute-start.5 = (f32[34,34,1]{1,0,2:T(8,128)S(1)}, f32[34,34,1]{1,0,2:T(8,128)S(1)}, u32[]{:S(2)}, u32[]{:S(2)}) collective-permute-start(f32[34,34,1]{1,0,2:T(8,128)S(1)} %copy.64), channel_id=1, source_target_pairs={{0,1},{2,3},{4,5},{6,7},{8,9},{10,11},{12,13},{14,15},{16,17},{18,... | collective-permute-start | bytes 13880 | tf_op jit(solution)/shard_map/ppermute | solution.py:382
  119.0 9.3 %collective-permute-start.4 = (f32[34,34,1]{1,0,2:T(8,128)S(1)}, f32[34,34,1]{1,0,2:T(8,128)S(1)}, u32[]{:S(2)}, u32[]{:S(2)}) collective-permute-start(f32[34,34,1]{1,0,2:T(8,128)S(1)} %copy.62), channel_id=1, source_target_pairs={{1,0},{3,2},{5,4},{7,6},{9,8},{11,10},{13,12},{15,14},{17,16},{19,... | collective-permute-start | bytes 13880 | tf_op jit(solution)/shard_map/ppermute | solution.py:384
  128.0 71.8 %copy-start.1 = (f32[32,32,128]{2,1,0:T(8,128)}, f32[32,32,128]{2,1,0:T(8,128)S(1)}, u32[]{:S(2)}) copy-start(f32[32,32,128]{2,1,0:T(8,128)S(1)} %reshape.83) | copy-start | bytes 1572868
  129.4 16.4 %copy-start.4 = (f32[32,32,128]{2,1,0:T(8,128)}, f32[32,32,128]{2,1,0:T(8,128)S(1)}, u32[]{:S(2)}) copy-start(f32[32,32,128]{2,1,0:T(8,128)S(1)} %divide_multiply_fusion) | copy-start | bytes 1572868
  129.5 5.9 %collective-permute-start.7 = (f32[1,32,128]{2,1,0:T(8,128)S(1)}, f32[1,32,128]{2,1,0:T(8,128)S(1)}, u32[]{:S(2)}, u32[]{:S(2)}) collective-permute-start(f32[1,32,128]{2,1,0:T(8,128)S(1)} %get-tuple-element.65), channel_id=1, source_target_pairs={{0,32},{32,64},{64,96},{96,128},{128,160},{160,192},{192,224},{1,3... | collective-permute-start | bytes 49160 | tf_op jit(solution)/shard_map/ppermute | solution.py:382
  131.4 6.9 %collective-permute-start.6 = (f32[1,32,128]{2,1,0:T(8,128)S(1)}, f32[1,32,128]{2,1,0:T(8,128)S(1)}, u32[]{:S(2)}, u32[]{:S(2)}) collective-permute-start(f32[1,32,128]{2,1,0:T(8,128)S(1)} %get-tuple-element.66), channel_id=1, source_target_pairs={{32,0},{64,32},{96,64},{128,96},{160,128},{192,160},{224,192},{33,... | collective-permute-start | bytes 49160 | tf_op jit(solution)/shard_map/ppermute | solution.py:384
  135.3 13.4 %copy-start.14 = (f32[1,32,128]{2,1,0:T(8,128)}, f32[1,32,128]{2,1,0:T(8,128)S(1)}, u32[]{:S(2)}) copy-start(f32[1,32,128]{2,1,0:T(8,128)S(1)} %collective-permute-done.7) | copy-start | bytes 49156
  138.3 10.5 %copy-start.15 = (f32[1,32,128]{2,1,0:T(8,128)}, f32[1,32,128]{2,1,0:T(8,128)S(1)}, u32[]{:S(2)}) copy-start(f32[1,32,128]{2,1,0:T(8,128)S(1)} %collective-permute-done.6) | copy-start | bytes 49156
  138.3 6.0 %collective-permute-start.9 = (f32[34,1,128]{2,1,0:T(1,128)S(1)}, f32[34,1,128]{2,1,0:T(1,128)S(1)}, u32[]{:S(2)}, u32[]{:S(2)}) collective-permute-start(f32[34,1,128]{2,1,0:T(1,128)S(1)} %get-tuple-element.55), channel_id=1, source_target_pairs={{0,2},{2,4},{4,6},{6,8},{8,10},{10,12},{12,14},{14,16},{16,18},{18... | collective-permute-start | bytes 52232 | tf_op jit(solution)/shard_map/ppermute | solution.py:382
  140.2 5.6 %collective-permute-start.8 = (f32[34,1,128]{2,1,0:T(1,128)S(1)}, f32[34,1,128]{2,1,0:T(1,128)S(1)}, u32[]{:S(2)}, u32[]{:S(2)}) collective-permute-start(f32[34,1,128]{2,1,0:T(1,128)S(1)} %get-tuple-element.56), channel_id=1, source_target_pairs={{2,0},{4,2},{6,4},{8,6},{10,8},{12,10},{14,12},{16,14},{18,16},{20... | collective-permute-start | bytes 52232 | tf_op jit(solution)/shard_map/ppermute | solution.py:384
  144.3 7.2 %copy-start.18 = (f32[34,1,128]{2,1,0:T(1,128)}, f32[34,1,128]{2,1,0:T(1,128)S(1)}, u32[]{:S(2)}) copy-start(f32[34,1,128]{2,1,0:T(1,128)S(1)} %collective-permute-done.9) | copy-start | bytes 52228
  145.9 5.6 %copy-start.19 = (f32[34,1,128]{2,1,0:T(1,128)}, f32[34,1,128]{2,1,0:T(1,128)S(1)}, u32[]{:S(2)}) copy-start(f32[34,1,128]{2,1,0:T(1,128)S(1)} %collective-permute-done.8) | copy-start | bytes 52228
  148.7 5.8 %collective-permute-start.10 = (f32[34,34,1]{1,0,2:T(8,128)S(1)}, f32[34,34,1]{1,0,2:T(8,128)S(1)}, u32[]{:S(2)}, u32[]{:S(2)}) collective-permute-start(f32[34,34,1]{1,0,2:T(8,128)S(1)} %copy.66), channel_id=1, source_target_pairs={{1,0},{3,2},{5,4},{7,6},{9,8},{11,10},{13,12},{15,14},{17,16},{19,... | collective-permute-start | bytes 13880 | tf_op jit(solution)/shard_map/ppermute | solution.py:384
  151.5 4.3 %collective-permute-start.11 = (f32[34,34,1]{1,0,2:T(8,128)S(1)}, f32[34,34,1]{1,0,2:T(8,128)S(1)}, u32[]{:S(2)}, u32[]{:S(2)}) collective-permute-start(f32[34,34,1]{1,0,2:T(8,128)S(1)} %copy.68), channel_id=1, source_target_pairs={{0,1},{2,3},{4,5},{6,7},{8,9},{10,11},{12,13},{14,15},{16,17},{18,... | collective-permute-start | bytes 13880 | tf_op jit(solution)/shard_map/ppermute | solution.py:382
  163.7 5.9 %collective-permute-start.13 = (f32[1,32,128]{2,1,0:T(8,128)S(1)}, f32[1,32,128]{2,1,0:T(8,128)S(1)}, u32[]{:S(2)}, u32[]{:S(2)}) collective-permute-start(f32[1,32,128]{2,1,0:T(8,128)S(1)} %get-tuple-element.63), channel_id=1, source_target_pairs={{0,32},{32,64},{64,96},{96,128},{128,160},{160,192},{192,224},{1,3... | collective-permute-start | bytes 49160 | tf_op jit(solution)/shard_map/ppermute | solution.py:382
  165.7 6.8 %collective-permute-start.12 = (f32[1,32,128]{2,1,0:T(8,128)S(1)}, f32[1,32,128]{2,1,0:T(8,128)S(1)}, u32[]{:S(2)}, u32[]{:S(2)}) collective-permute-start(f32[1,32,128]{2,1,0:T(8,128)S(1)} %get-tuple-element.64), channel_id=1, source_target_pairs={{32,0},{64,32},{96,64},{128,96},{160,128},{192,160},{224,192},{33,... | collective-permute-start | bytes 49160 | tf_op jit(solution)/shard_map/ppermute | solution.py:384
  169.6 14.9 %copy-start.8 = (f32[1,32,128]{2,1,0:T(8,128)}, f32[1,32,128]{2,1,0:T(8,128)S(1)}, u32[]{:S(2)}) copy-start(f32[1,32,128]{2,1,0:T(8,128)S(1)} %collective-permute-done.13) | copy-start | bytes 49156
  172.5 12.0 %copy-start.9 = (f32[1,32,128]{2,1,0:T(8,128)}, f32[1,32,128]{2,1,0:T(8,128)S(1)}, u32[]{:S(2)}) copy-start(f32[1,32,128]{2,1,0:T(8,128)S(1)} %collective-permute-done.12) | copy-start | bytes 49156
  172.5 6.1 %collective-permute-start.15 = (f32[34,1,128]{2,1,0:T(1,128)S(1)}, f32[34,1,128]{2,1,0:T(1,128)S(1)}, u32[]{:S(2)}, u32[]{:S(2)}) collective-permute-start(f32[34,1,128]{2,1,0:T(1,128)S(1)} %get-tuple-element.53), channel_id=1, source_target_pairs={{0,2},{2,4},{4,6},{6,8},{8,10},{10,12},{12,14},{14,16},{16,18},{18... | collective-permute-start | bytes 52232 | tf_op jit(solution)/shard_map/ppermute | solution.py:382
  176.7 7.8 %collective-permute-start.14 = (f32[34,1,128]{2,1,0:T(1,128)S(1)}, f32[34,1,128]{2,1,0:T(1,128)S(1)}, u32[]{:S(2)}, u32[]{:S(2)}) collective-permute-start(f32[34,1,128]{2,1,0:T(1,128)S(1)} %get-tuple-element.54), channel_id=1, source_target_pairs={{2,0},{4,2},{6,4},{8,6},{10,8},{12,10},{14,12},{16,14},{18,16},{20... | collective-permute-start | bytes 52232 | tf_op jit(solution)/shard_map/ppermute | solution.py:384
  178.7 5.8 %copy-start.10 = (f32[34,1,128]{2,1,0:T(1,128)}, f32[34,1,128]{2,1,0:T(1,128)S(1)}, u32[]{:S(2)}) copy-start(f32[34,1,128]{2,1,0:T(1,128)S(1)} %collective-permute-done.15) | copy-start | bytes 52228
  184.5 0.6 copy-start.11
  190.6 7.2 %collective-permute-start.17 = (f32[34,34,1]{1,0,2:T(8,128)}, f32[34,34,1]{1,0,2:T(8,128)}, u32[]{:S(2)}, u32[]{:S(2)}) collective-permute-start(f32[34,34,1]{1,0,2:T(8,128)} %copy.72), channel_id=1, source_target_pairs={{0,1},{2,3},{4,5},{6,7},{8,9},{10,11},{12,13},{14,15},{16,17},{18,... | collective-permute-start | bytes 13880 | tf_op jit(solution)/shard_map/ppermute | solution.py:382
  192.5 3.4 %collective-permute-start.16 = (f32[34,34,1]{1,0,2:T(8,128)}, f32[34,34,1]{1,0,2:T(8,128)}, u32[]{:S(2)}, u32[]{:S(2)}) collective-permute-start(f32[34,34,1]{1,0,2:T(8,128)} %copy.70), channel_id=1, source_target_pairs={{1,0},{3,2},{5,4},{7,6},{9,8},{11,10},{13,12},{15,14},{17,16},{19,... | collective-permute-start | bytes 13880 | tf_op jit(solution)/shard_map/ppermute | solution.py:384
  199.8 10.2 %copy-start.22 = (s32[16]{0:T(128)S(1)}, s32[16]{0:T(128)}, u32[]{:S(2)}) copy-start(s32[16]{0:T(128)} %select_reduce_fusion.2) | copy-start | bytes 196
  204.1 18.5 %copy-start.3 = (f32[32,32,128]{2,1,0:T(8,128)}, f32[32,32,128]{2,1,0:T(8,128)S(1)}, u32[]{:S(2)}) copy-start(f32[32,32,128]{2,1,0:T(8,128)S(1)} %multiply_add_fusion) | copy-start | bytes 1572868
  204.2 6.4 %collective-permute-start.19 = (f32[1,32,128]{2,1,0:T(8,128)S(1)}, f32[1,32,128]{2,1,0:T(8,128)S(1)}, u32[]{:S(2)}, u32[]{:S(2)}) collective-permute-start(f32[1,32,128]{2,1,0:T(8,128)S(1)} %get-tuple-element.61), channel_id=1, source_target_pairs={{0,32},{32,64},{64,96},{96,128},{128,160},{160,192},{192,224},{1,3... | collective-permute-start | bytes 49160 | tf_op jit(solution)/shard_map/ppermute | solution.py:382
  206.1 6.8 %collective-permute-start.18 = (f32[1,32,128]{2,1,0:T(8,128)S(1)}, f32[1,32,128]{2,1,0:T(8,128)S(1)}, u32[]{:S(2)}, u32[]{:S(2)}) collective-permute-start(f32[1,32,128]{2,1,0:T(8,128)S(1)} %get-tuple-element.62), channel_id=1, source_target_pairs={{32,0},{64,32},{96,64},{128,96},{160,128},{192,160},{224,192},{33,... | collective-permute-start | bytes 49160 | tf_op jit(solution)/shard_map/ppermute | solution.py:384
  210.5 15.0 %copy-start.12 = (f32[1,32,128]{2,1,0:T(8,128)}, f32[1,32,128]{2,1,0:T(8,128)S(1)}, u32[]{:S(2)}) copy-start(f32[1,32,128]{2,1,0:T(8,128)S(1)} %collective-permute-done.19) | copy-start | bytes 49156
  212.9 12.6 %copy-start.13 = (f32[1,32,128]{2,1,0:T(8,128)}, f32[1,32,128]{2,1,0:T(8,128)S(1)}, u32[]{:S(2)}) copy-start(f32[1,32,128]{2,1,0:T(8,128)S(1)} %collective-permute-done.18) | copy-start | bytes 49156
  213.0 5.9 %collective-permute-start.21 = (f32[34,1,128]{2,1,0:T(1,128)S(1)}, f32[34,1,128]{2,1,0:T(1,128)S(1)}, u32[]{:S(2)}, u32[]{:S(2)}) collective-permute-start(f32[34,1,128]{2,1,0:T(1,128)S(1)} %get-tuple-element.51), channel_id=1, source_target_pairs={{0,2},{2,4},{4,6},{6,8},{8,10},{10,12},{12,14},{14,16},{16,18},{18... | collective-permute-start | bytes 52232 | tf_op jit(solution)/shard_map/ppermute | solution.py:382
  216.9 5.8 %collective-permute-start.20 = (f32[34,1,128]{2,1,0:T(1,128)S(1)}, f32[34,1,128]{2,1,0:T(1,128)S(1)}, u32[]{:S(2)}, u32[]{:S(2)}) collective-permute-start(f32[34,1,128]{2,1,0:T(1,128)S(1)} %get-tuple-element.52), channel_id=1, source_target_pairs={{2,0},{4,2},{6,4},{8,6},{10,8},{12,10},{14,12},{16,14},{18,16},{20... | collective-permute-start | bytes 52232 | tf_op jit(solution)/shard_map/ppermute | solution.py:384
  218.8 8.1 %copy-start.16 = (f32[34,1,128]{2,1,0:T(1,128)}, f32[34,1,128]{2,1,0:T(1,128)S(1)}, u32[]{:S(2)}) copy-start(f32[34,1,128]{2,1,0:T(1,128)S(1)} %collective-permute-done.21) | copy-start | bytes 52228
  222.7 4.3 %copy-start.17 = (f32[34,1,128]{2,1,0:T(1,128)}, f32[34,1,128]{2,1,0:T(1,128)S(1)}, u32[]{:S(2)}) copy-start(f32[34,1,128]{2,1,0:T(1,128)S(1)} %collective-permute-done.20) | copy-start | bytes 52228
  227.0 5.6 %collective-permute-start.23 = (f32[34,34,1]{1,0,2:T(8,128)S(1)}, f32[34,34,1]{1,0,2:T(8,128)S(1)}, u32[]{:S(2)}, u32[]{:S(2)}) collective-permute-start(f32[34,34,1]{1,0,2:T(8,128)S(1)} %copy.76), channel_id=1, source_target_pairs={{0,1},{2,3},{4,5},{6,7},{8,9},{10,11},{12,13},{14,15},{16,17},{18,... | collective-permute-start | bytes 13880 | tf_op jit(solution)/shard_map/ppermute | solution.py:382
  228.3 3.1 collective-permute-start.22
  242.1 17.4 %copy-start = (f32[32,32,128]{2,1,0:T(8,128)}, f32[32,32,128]{2,1,0:T(8,128)S(1)}, u32[]{:S(2)}) copy-start(f32[32,32,128]{2,1,0:T(8,128)S(1)} %fusion.7) | copy-start | bytes 1572868
  242.1 8.0 %collective-permute-start.24 = (f32[1,32,128]{2,1,0:T(8,128)S(1)}, f32[1,32,128]{2,1,0:T(8,128)S(1)}, u32[]{:S(2)}, u32[]{:S(2)}) collective-permute-start(f32[1,32,128]{2,1,0:T(8,128)S(1)} %get-tuple-element.59), channel_id=1, source_target_pairs={{0,32},{32,64},{64,96},{96,128},{128,160},{160,192},{192,224},{1,3... | collective-permute-start | bytes 49160 | tf_op jit(solution)/shard_map/ppermute | solution.py:382
  244.0 6.8 %collective-permute-start.25 = (f32[1,32,128]{2,1,0:T(8,128)S(1)}, f32[1,32,128]{2,1,0:T(8,128)S(1)}, u32[]{:S(2)}, u32[]{:S(2)}) collective-permute-start(f32[1,32,128]{2,1,0:T(8,128)S(1)} %get-tuple-element.60), channel_id=1, source_target_pairs={{32,0},{64,32},{96,64},{128,96},{160,128},{192,160},{224,192},{33,... | collective-permute-start | bytes 49160 | tf_op jit(solution)/shard_map/ppermute | solution.py:384
  250.9 7.4 %collective-permute-start.27 = (f32[34,1,128]{2,1,0:T(1,128)S(1)}, f32[34,1,128]{2,1,0:T(1,128)S(1)}, u32[]{:S(2)}, u32[]{:S(2)}) collective-permute-start(f32[34,1,128]{2,1,0:T(1,128)S(1)} %get-tuple-element.49), channel_id=1, source_target_pairs={{2,0},{4,2},{6,4},{8,6},{10,8},{12,10},{14,12},{16,14},{18,16},{20... | collective-permute-start | bytes 52232 | tf_op jit(solution)/shard_map/ppermute | solution.py:384
  252.8 5.6 %collective-permute-start.26 = (f32[34,1,128]{2,1,0:T(1,128)S(1)}, f32[34,1,128]{2,1,0:T(1,128)S(1)}, u32[]{:S(2)}, u32[]{:S(2)}) collective-permute-start(f32[34,1,128]{2,1,0:T(1,128)S(1)} %get-tuple-element.50), channel_id=1, source_target_pairs={{0,2},{2,4},{4,6},{6,8},{8,10},{10,12},{12,14},{14,16},{16,18},{18... | collective-permute-start | bytes 52232 | tf_op jit(solution)/shard_map/ppermute | solution.py:382
  260.5 4.5 %collective-permute-start.29 = (f32[34,34,1]{1,0,2:T(8,128)S(1)}, f32[34,34,1]{1,0,2:T(8,128)S(1)}, u32[]{:S(2)}, u32[]{:S(2)}) collective-permute-start(f32[34,34,1]{1,0,2:T(8,128)S(1)} %copy.79), channel_id=1, source_target_pairs={{1,0},{3,2},{5,4},{7,6},{9,8},{11,10},{13,12},{15,14},{17,16},{19,... | collective-permute-start | bytes 13880 | tf_op jit(solution)/shard_map/ppermute | solution.py:384
  261.8 3.9 %collective-permute-start.28 = (f32[34,34,1]{1,0,2:T(8,128)S(1)}, f32[34,34,1]{1,0,2:T(8,128)S(1)}, u32[]{:S(2)}, u32[]{:S(2)}) collective-permute-start(f32[34,34,1]{1,0,2:T(8,128)S(1)} %copy.78), channel_id=1, source_target_pairs={{0,1},{2,3},{4,5},{6,7},{8,9},{10,11},{12,13},{14,15},{16,17},{18,... | collective-permute-start | bytes 13880 | tf_op jit(solution)/shard_map/ppermute | solution.py:382
  265.9 0.7 copy-start.21
  268.3 48.9 %all-to-all-start.2 = ((f32[16,304,128]{2,1,0:T(8,128)}), f32[16,304,128]{2,1,0:T(8,128)S(1)}, u32[]{:S(2)}, u32[]{:S(2)}) async-start(f32[16,304,128]{2,1,0:T(8,128)} %broadcast_select_fusion), calls=%async_computation.2 | async-start | bytes 4980736 | tf_op jit(solution)/shard_map/all_to_all | solution.py:482
  317.2 1.5 copy-start.2
where the time goes:
time: 335 us; the launch traced here: 330 us
  starting transfers between devices  106 us (32%)
  Pallas kernels  82.2 us (25%)
  waiting for transfers between devices  61.5 us (18%)
  local copies, waits for them, and re-layouts  51.2 us (15%)
  other arithmetic  26.6 us (8%)
    ppermute x15, starting transfers between devices, extended(): lax.ppermute(head, axis, [((i + 1) % count, i) for i in range(ends)])  39.6 us
    ppermute x15, starting transfers between devices, extended(): lax.ppermute(tail, axis, [(i, (i + 1) % count) for i in range(ends)])  39.3 us
    pallas_call x1, Pallas kernels, update_call(): pl.pallas_call(update_kernel, in_specs=[VMEM_SPEC, VMEM_SPEC], out_specs=...  37 us
    all_to_all x3, waiting for transfers between devices, exchange(): return lax.all_to_all(rows, 'by', split_axis=0, concat_axis=0, tiled=True)  28.8 us
    ppermute x15, waiting for transfers between devices, extended(): lax.ppermute(head, axis, [((i + 1) % count, i) for i in range(ends)])  28.3 us
    all_to_all x3, starting transfers between devices, exchange(): return lax.all_to_all(rows, 'by', split_axis=0, concat_axis=0, tiled=True)  27.6 us
    pallas_call x1, Pallas kernels, flux_call(): pl.pallas_call(functools.partial(flux_kernel, lanes_by=lanes_by), in_spec...  24 us
    add x2, other arithmetic, solve(): damping_next * damping * search  11.1 us
  transfers between devices with their start and end apart: 33, of which 15 were waited for; matrix products, arithmetic and copies ran while one was open for 6% of the time, Pallas kernels for 19%

commit v1 on v0

--- a/solution.py
+++ b/solution.py
@@ -371,84 +371,364 @@
     )(slot_row, updated, apertures, returned)
 
 
-def extended(cells, sides, width):
-    for axis, dim in sides:
-        count = lax.axis_size(axis)
-        ends = count - 1
-        head = lax.slice_in_dim(cells, 0, width, axis=dim)
-        tail = lax.slice_in_dim(cells, cells.shape[dim] - width, cells.shape[dim], axis=dim)
-        cells = jnp.concatenate(
-            [
-                lax.ppermute(tail, axis, [(i, (i + 1) % count) for i in range(ends)]),
-                cells,
-                lax.ppermute(head, axis, [((i + 1) % count, i) for i in range(ends)]),
-            ],
-            axis=dim,
+HALO = 5
+SIDE = 8
+EXT = BOX + 2 * HALO
+ROWS_Y = BOX + 2 * SIDE
+SLOT = 8
+GROUP = TILE // SLOT
+GROUPS = BOX // GROUP + 2
+
+
+def wide_lane():
+    return lax.broadcasted_iota(jnp.int32, (ROWS_Y, TILE), 1)
+
+
+def assemble_kernel(table, side, recv, brick, first, last, strip, strip_first, strip_last, boxes, sem, *, count):
+    lanes = lane_index()
+    copies = [
+        pltpu.make_async_copy(recv.at[table[k]], boxes.at[k], sem.at[k]) for k in range(count)
+    ]
+    for copy in copies:
+        copy.start()
+    for copy in copies:
+        copy.wait()
+    strip[...] = jnp.zeros_like(strip)
+    lanes_brick = lax.broadcasted_iota(jnp.int32, (BOX, TILE), 1)
+    source_lane = jnp.where(side[0] == 0, TILE - SLOT, 0)
+
+    def step(x, carry):
+        rows = [boxes[k, pl.ds(x * TILES, TILES), :] for k in range(count)]
+        for r in range(PER_TILE):
+            value = None
+            for k in reversed(range(count)):
+                shift = (BOX * (k - r)) % TILE
+                piece = pltpu.roll(rows[k], shift, 1) if shift else rows[k]
+                value = piece if value is None else jnp.where(lanes < BOX * (k + 1), piece, value)
+            brick[pl.ds(x * BOX + r, TILES, stride=PER_TILE), :] = value
+        plane = brick[pl.ds(x * BOX, BOX), :]
+        group = x // GROUP
+        lane = (x % GROUP) * SLOT
+        moved = pltpu.roll(plane, (lane - source_lane + TILE) % TILE, 1)
+        strip[group] = jnp.where(lanes_brick // SLOT == x % GROUP, moved, strip[group])
+        return carry
+
+    lax.fori_loop(0, BOX, step, 0)
+    first[...] = brick[0 : HALO * BOX, :]
+    last[...] = brick[(BOX - HALO) * BOX : BOX * BOX, :]
+    strip_first[...] = strip[0]
+    strip_last[...] = strip[BOX // GROUP - 1]
+
+
+def solve_kernel(box_of_row, side, *refs, count, lanes_by):
+    volume_in, source_in = refs[0:8], refs[8:16]
+    pressure, rows = refs[16:18]
+    scratch = refs[18:]
+    (vol, ax, ayu, ayl, azu, azl, diag, inv, res, sa, sb, total) = scratch[0:12]
+    (hvol, hres, hsa, hsb, htotal, hcoef, edge, turned, packed, sem) = scratch[12:]
+    lane = wide_lane()
+    at_top = side[0] == 0
+    edge_lane = jnp.where(at_top, TILE - 1, 0)
+    slot_lane = jnp.where(at_top, 0, SLOT - 1)
+    up_lane = jnp.where(at_top, TILE - 1, -1)
+    low_lane = jnp.where(at_top, -1, 0)
+    open_up = (lane % SLOT == SLOT - 1) & (low_lane == 0)
+    open_low = (lane % SLOT == 0) & (up_lane >= 0)
+
+    def main(ref, x):
+        return ref[pl.ds(pl.multiple_of(x * ROWS_Y, 8), ROWS_Y), :]
+
+    def put(ref, x, value):
+        ref[pl.ds(pl.multiple_of(x * ROWS_Y, 8), ROWS_Y), :] = value
+
+    def fill(ext, strips, parts):
+        brick, x_lo, x_hi, middle, z_lo, z_hi, y_lo, y_hi = parts
+
+        def rows_of(x):
+            ext[pl.ds(pl.multiple_of(x * ROWS_Y, 8), SIDE), :] = y_lo[x]
+            ext[pl.ds(pl.multiple_of(x * ROWS_Y + SIDE + BOX, 8), SIDE), :] = y_hi[x]
+
+        def body(i, carry):
+            ext[pl.ds(pl.multiple_of((i + HALO) * ROWS_Y + SIDE, 8), BOX), :] = brick[
+                pl.ds(pl.multiple_of(i * BOX, 8), BOX), :
+            ]
+            rows_of(i + HALO)
+            return carry
+
+        lax.fori_loop(0, BOX, body, 0)
+        for i in range(HALO):
+            for x, part in ((i, x_lo), (HALO + BOX + i, x_hi)):
+                ext[x * ROWS_Y + SIDE : x * ROWS_Y + SIDE + BOX, :] = part[i * BOX : (i + 1) * BOX, :]
+                rows_of(x)
+        pieces = [z_lo[...]] + [middle[g] for g in range(GROUPS - 2)] + [z_hi[...]]
+        for g, piece in enumerate(pieces):
+            strips[g, 0:SIDE] = y_lo[EXT + g]
+            strips[g, SIDE : SIDE + BOX] = piece
+            strips[g, SIDE + BOX : ROWS_Y] = y_hi[EXT + g]
+
+    fill(vol, hvol, volume_in)
+    fill(res, hres, source_in)
+
+    def place(x):
+        return (x + GROUP - HALO) // GROUP, (x + GROUP - HALO) % GROUP * SLOT + slot_lane
+
+    def strip_value(strips, x):
+        group, where = place(x)
+        return pltpu.roll(strips[group], (edge_lane - where + TILE) % TILE, 1)
+
+    def gather_edge(ref):
+        def body(x, carry):
+            group, where = place(x)
+            moved = pltpu.roll(main(ref, x), (where - edge_lane + TILE) % TILE, 1)
+            edge[group] = jnp.where(lane == where, moved, edge[group])
+            return carry
+
+        lax.fori_loop(1, EXT - 1, body, 0)
+
+    def y_up(value):
+        return pltpu.roll(value, ROWS_Y - 1, 0)
+
+    def y_down(value):
+        return pltpu.roll(value, 1, 0)
+
+    def z_sides(value, outside):
+        up = jnp.where(lane == up_lane, outside, pltpu.roll(value, TILE - 1, 1))
+        down = jnp.where(lane == low_lane, outside, pltpu.roll(value, 1, 1))
+        return up, down
+
+    def strip_sides(strips, g):
+        here = strips[g]
+        following = strips[min(g + 1, GROUPS - 1)]
+        previous = strips[max(g - 1, 0)]
+        x_up = jnp.where(
+            lane >= TILE - SLOT, pltpu.roll(following, TILE - SLOT, 1), pltpu.roll(here, TILE - SLOT, 1)
         )
-    return cells
-
-
-def sides(rimmed):
-    return [
-        (rimmed[2:, 1:-1, 1:-1], rimmed[:-2, 1:-1, 1:-1]),
-        (rimmed[1:-1, 2:, 1:-1], rimmed[1:-1, :-2, 1:-1]),
-        (rimmed[1:-1, 1:-1, 2:], rimmed[1:-1, 1:-1, :-2]),
-    ]
-
-
-def operator_parts(volume, volume_rimmed):
-    apertures = []
-    diagonal = SHIFT_WEIGHT * volume
-    for upper_side, lower_side in sides(volume_rimmed):
-        upper_ap = jnp.minimum(volume, upper_side)
-        lower_ap = jnp.minimum(lower_side, volume)
-        apertures.append((upper_ap, lower_ap))
-        diagonal = diagonal + upper_ap + lower_ap
-    return (apertures, diagonal)
-
-
-def apply_operator(search, search_rimmed, apertures, diagonal):
-    total = jnp.zeros_like(search)
-    for (upper_side, lower_side), (upper_ap, lower_ap) in zip(sides(search_rimmed), apertures):
-        total = total + upper_ap * upper_side + lower_ap * lower_side
-    return diagonal * search - total
-
-
-def to_brick(rows):
-    count = rows.shape[0]
-    cube = rows.reshape(count, BOX, TILES, PER_TILE, BOX)
-    return cube.transpose(1, 2, 3, 0, 4).reshape(BOX, BOX, count * BOX)
-
-
-def return_box(rimmed, k):
-    low = k * BOX
-    core = rimmed[:, 1:-1, low + 1 : low + 1 + BOX].reshape(PADDED * TILES, TILE)
-    y_faces = [rimmed[1:-1, y, low + 1 : low + 1 + BOX] for y in (0, BOX + 1)]
-    z_faces = [rimmed[1:-1, 1:-1, z] for z in (low, low + BOX + 1)]
-    return jnp.concatenate([core] + [f.reshape(TILES, TILE) for f in y_faces + z_faces], axis=0)
-
-
-def solve(source, volume):
-    axes = (("bx", 0), ("by", 1), ("bz", 2))
-    volume_rimmed = extended(volume, axes, 1)
-    apertures, diagonal = operator_parts(volume, volume_rimmed)
+        x_down = jnp.where(lane < SLOT, pltpu.roll(previous, SLOT, 1), pltpu.roll(here, SLOT, 1))
+        z_up = jnp.where(open_up, edge[g], pltpu.roll(here, TILE - 1, 1))
+        z_down = jnp.where(open_low, edge[g], pltpu.roll(here, 1, 1))
+        return x_up, x_down, y_up(here), y_down(here), z_up, z_down
+
+    edge[...] = jnp.zeros_like(edge)
+    gather_edge(vol)
+    zero = jnp.zeros((ROWS_Y, TILE), jnp.float32)
     center = 0.5 * (UPPER_BOUND + LOWER_BOUND)
     halfwidth = 0.5 * (UPPER_BOUND - LOWER_BOUND)
     spread = center / halfwidth
     damping = 1.0 / spread
-    pressure = jnp.zeros_like(source)
-    residual = source
-    search = residual / diagonal * (1.0 / center)
-    for iteration in range(ITERS):
-        pressure = pressure + search
-        if iteration < ITERS - 1:
-            residual = residual - apply_operator(search, extended(search, axes, 1), apertures, diagonal)
-            damping_next = 1.0 / (2.0 * spread - damping)
-            search = damping_next * damping * search + 2.0 * damping_next / halfwidth * (
-                residual / diagonal
-            )
-            damping = damping_next
-    return pressure, extended(pressure, axes, 1)
+    for ref in (sa, sb):
+        put(ref, 0, zero)
+        put(ref, EXT - 1, zero)
+    put(ax, 0, jnp.minimum(main(vol, 0), main(vol, 1)))
+
+    def inverse_of(value):
+        return jnp.where(value > 0.0, 1.0 / jnp.where(value > 0.0, value, 1.0), 0.0)
+
+    def prepare(x, carry):
+        v = main(vol, x)
+        upper = jnp.minimum(v, main(vol, x + 1))
+        z_up, z_down = z_sides(v, strip_value(hvol, x))
+        z_up = jnp.where((lane == TILE - 1) & (lane != up_lane), 0.0, z_up)
+        z_down = jnp.where((lane == 0) & (lane != low_lane), 0.0, z_down)
+        parts = [jnp.minimum(v, n) for n in (y_up(v), y_down(v), z_up, z_down)]
+        whole = SHIFT_WEIGHT * v + upper + main(ax, x - 1) + parts[0] + parts[1] + parts[2] + parts[3]
+        scale = inverse_of(whole)
+        put(ax, x, upper)
+        for ref, value in zip((ayu, ayl, azu, azl, diag, inv), parts + [whole, scale]):
+            put(ref, x, value)
+        search = (main(res, x) * scale) * (1.0 / center)
+        put(sa, x, search)
+        put(total, x, search)
+        return carry
+
+    lax.fori_loop(1, EXT - 1, prepare, 0)
+    for g in range(GROUPS):
+        v = hvol[g]
+        parts = [jnp.minimum(v, n) for n in strip_sides(hvol, g)]
+        whole = SHIFT_WEIGHT * v
+        for value in parts:
+            whole = whole + value
+        scale = inverse_of(whole)
+        for i, value in enumerate(parts + [whole, scale]):
+            hcoef[i, g] = value
+        search = (hres[g] * scale) * (1.0 / center)
+        hsa[g] = search
+        htotal[g] = search
+
+    now, then, hnow, hthen = sa, sb, hsa, hsb
+    for iteration in range(ITERS - 1):
+        damping_next = 1.0 / (2.0 * spread - damping)
+        keep = damping_next * damping
+        push = 2.0 * damping_next / halfwidth
+        damping = damping_next
+        gather_edge(now)
+
+        def iterate(x, carry, now=now, then=then, hnow=hnow, keep=keep, push=push):
+            s = main(now, x)
+            z_up, z_down = z_sides(s, strip_value(hnow, x))
+            flow = main(ax, x) * main(now, x + 1) + main(ax, x - 1) * main(now, x - 1)
+            flow = flow + (main(ayu, x) * y_up(s) + main(ayl, x) * y_down(s))
+            flow = flow + (main(azu, x) * z_up + main(azl, x) * z_down)
+            residual = main(res, x) - (main(diag, x) * s - flow)
+            put(res, x, residual)
+            search = keep * s + push * (residual * main(inv, x))
+            put(then, x, search)
+            put(total, x, main(total, x) + search)
+            return carry
+
+        lax.fori_loop(1, EXT - 1, iterate, 0)
+        for g in range(GROUPS):
+            s = hnow[g]
+            flow = zero
+            for i, value in enumerate(strip_sides(hnow, g)):
+                flow = flow + hcoef[i, g] * value
+            residual = hres[g] - (hcoef[6, g] * s - flow)
+            hres[g] = residual
+            search = keep * s + push * (residual * hcoef[7, g])
+            hthen[g] = search
+            htotal[g] = htotal[g] + search
+        now, then, hnow, hthen = then, now, hthen, hnow
+
+    lanes = lane_index()
+
+    def spread_boxes(pieces, row):
+        for k in range(count):
+            value = None
+            for r in reversed(range(PER_TILE)):
+                shift = (BOX * (r - k)) % TILE
+                piece = pltpu.roll(pieces[r], shift, 1) if shift else pieces[r]
+                value = piece if value is None else jnp.where(lanes < BOX * (r + 1), piece, value)
+            packed[pl.ds(pl.multiple_of(k * RETURN_ROWS + row, 8), TILES), :] = value
+
+    def core(i, carry):
+        base = (i + HALO - 1) * ROWS_Y + SIDE
+        pieces = [total[pl.ds(base + r, TILES, stride=PER_TILE), :] for r in range(PER_TILE)]
+        spread_boxes(pieces, i * TILES)
+        return carry
+
+    lax.fori_loop(0, PADDED, core, 0)
+
+    def output(i, carry):
+        pressure[i] = total[pl.ds(pl.multiple_of((i + HALO) * ROWS_Y + SIDE, 8), BOX), :]
+        return carry
+
+    lax.fori_loop(0, BOX, output, 0)
+    for f, y in enumerate((SIDE - 1, SIDE + BOX)):
+        pieces = [
+            total[pl.ds((HALO + r) * ROWS_Y + y, TILES, stride=PER_TILE * ROWS_Y), :]
+            for r in range(PER_TILE)
+        ]
+        spread_boxes(pieces, PADDED * TILES + f * TILES)
+    z_row = PADDED * TILES + 2 * TILES
+    for k in (0, count - 1):
+        packed[k * RETURN_ROWS + z_row : k * RETURN_ROWS + z_row + 2 * TILES, :] = jnp.zeros(
+            (2 * TILES, TILE), jnp.float32
+        )
+    for block in range(TILES):
+        for r in range(PER_TILE):
+            start = (HALO + PER_TILE * block + r) * ROWS_Y + SIDE
+            turned[r * BOX : (r + 1) * BOX, :] = total[start : start + BOX, :]
+        flat = turned[...].T
+        for k in range(count):
+            low = k * RETURN_ROWS + z_row + block
+            if k:
+                packed[low : low + 1, :] = flat[BOX * k - 1 : BOX * k, :]
+            if k < count - 1:
+                packed[low + TILES : low + TILES + 1, :] = flat[BOX * k + BOX : BOX * k + BOX + 1, :]
+    half = GROUP // PER_TILE
+    row4 = lax.broadcasted_iota(jnp.int32, (half, TILE), 1)
+    box = jnp.where(at_top, count - 1, 0)
+    target = box * RETURN_ROWS + z_row + jnp.where(at_top, TILES, 0)
+    for g in range(1, GROUPS - 1):
+        turned[0:BOX, :] = htotal[g, SIDE : SIDE + BOX]
+        turned[BOX:TILE, :] = jnp.zeros((TILE - BOX, TILE), jnp.float32)
+        flat = turned[...].T
+        turned[...] = flat
+        value = None
+        for r in range(PER_TILE):
+            piece = turned[pl.ds(SLOT * r + slot_lane, half, stride=SLOT * PER_TILE), :]
+            piece = pltpu.roll(piece, BOX * r, 1) if r else piece
+            value = piece if value is None else jnp.where(row4 // BOX == r, piece, value)
+        packed[pl.ds(target + (g - 1) * half, half), :] = value
+    copies = [
+        pltpu.make_async_copy(
+            packed.at[pl.ds(pl.multiple_of(box_of_row[d] * RETURN_ROWS, 8), RETURN_ROWS)],
+            rows.at[d],
+            sem.at[d],
+        )
+        for d in range(lanes_by)
+    ]
+    for copy in copies:
+        copy.start()
+    for copy in copies:
+        copy.wait()
+
+
+def assemble_call(table, side, recv):
+    count = table.shape[0]
+    return pl.pallas_call(
+        functools.partial(assemble_kernel, count=count),
+        in_specs=[SMEM_SPEC, SMEM_SPEC, ANY_SPEC],
+        out_specs=[VMEM_SPEC] * 6,
+        out_shape=[
+            struct(BOX * BOX, TILE),
+            struct(HALO * BOX, TILE),
+            struct(HALO * BOX, TILE),
+            struct(BOX // GROUP, BOX, TILE),
+            struct(BOX, TILE),
+            struct(BOX, TILE),
+        ],
+        scratch_shapes=[
+            pltpu.VMEM((count, ROWS, TILE), jnp.float32),
+            pltpu.SemaphoreType.DMA((count,)),
+        ],
+        name="brick",
+    )(table, side, recv)
+
+
+def halo(parts):
+    brick, first, last, strip, strip_first, strip_last = parts
+    nx, ny = lax.axis_size("bx"), lax.axis_size("by")
+    nz = lax.axis_size("bz")
+    middle = lax.ppermute(strip, "bz", [(i, nz - 1 - i) for i in range(nz)])
+    up = [(i, i + 1) for i in range(nx - 1)]
+    down = [(j, i) for i, j in up]
+    cross_up = [(i * nz + z, j * nz + nz - 1 - z) for i, j in up for z in range(nz)]
+    cross_down = [(i * nz + z, j * nz + nz - 1 - z) for i, j in down for z in range(nz)]
+    x_lo = lax.ppermute(last, "bx", up)
+    x_hi = lax.ppermute(first, "bx", down)
+    z_lo = lax.ppermute(strip_last, ("bx", "bz"), cross_up)
+    z_hi = lax.ppermute(strip_first, ("bx", "bz"), cross_down)
+    cubes = [v.reshape(-1, BOX, TILE) for v in (x_lo, brick, x_hi, z_lo, middle, z_hi)]
+
+    def edge(start):
+        return jnp.concatenate([v[:, start : start + SIDE] for v in cubes], axis=0)
+
+    y_up = [(i, i + 1) for i in range(ny - 1)]
+    y_lo = lax.ppermute(edge(BOX - SIDE), "by", y_up)
+    y_hi = lax.ppermute(edge(0), "by", [(j, i) for i, j in y_up])
+    return brick, x_lo, x_hi, middle, z_lo, z_hi, y_lo, y_hi
+
+
+def solve_call(box_of_row, side, count, volume, source):
+    lanes_by = box_of_row.shape[0]
+    wide = pltpu.VMEM((EXT * ROWS_Y, TILE), jnp.float32)
+    narrow = pltpu.VMEM((GROUPS, ROWS_Y, TILE), jnp.float32)
+    return pl.pallas_call(
+        functools.partial(solve_kernel, count=count, lanes_by=lanes_by),
+        in_specs=[SMEM_SPEC, SMEM_SPEC] + [VMEM_SPEC] * 16,
+        out_specs=[VMEM_SPEC, ANY_SPEC],
+        out_shape=[struct(BOX, BOX, count * BOX), struct(lanes_by, RETURN_ROWS, TILE)],
+        scratch_shapes=[wide] * 12
+        + [narrow] * 5
+        + [
+            pltpu.VMEM((8, GROUPS, ROWS_Y, TILE), jnp.float32),
+            narrow,
+            pltpu.VMEM((TILE, TILE), jnp.float32),
+            pltpu.VMEM((count * RETURN_ROWS, TILE), jnp.float32),
+            pltpu.SemaphoreType.DMA((lanes_by,)),
+        ],
+        name="solve",
+    )(box_of_row, side, *volume, *source)
 
 
 def routing(placement, capacity):
@@ -489,11 +769,11 @@
     masses, source_rows = flux_call(send_slot, jnp.swapaxes(velocity, 0, 1), planes)
     source_recv = exchange(source_rows)
     updated, apertures = update_call(masses, planes)
-    volume = to_brick(jnp.take(volume_recv, brick_table, axis=0))
-    source = to_brick(jnp.take(source_recv, brick_table, axis=0))
-    pressure, rimmed = solve(source, volume)
-    boxes = jnp.stack([return_box(rimmed, k) for k in range(placement.shape[3])])
-    returned = exchange(jnp.take(boxes, box_of_row, axis=0))
+    side = lax.axis_index("bz").reshape(1)
+    volume = halo(assemble_call(brick_table, side, volume_recv))
+    source = halo(assemble_call(brick_table, side, source_recv))
+    pressure, rows = solve_call(box_of_row, side, placement.shape[3], volume, source)
+    returned = exchange(rows)
     corrected = correct_call(slot_row, updated, apertures, returned)
     return (jnp.swapaxes(corrected, 0, 1), pressure)
 

time: 335 us -> 227 us (0.68); the launches traced: 330 us -> 226 us
  Pallas kernels: 82.2 us -> 134 us
  waiting for transfers between devices: 61.5 us -> 13.8 us
  local copies, waits for them, and re-layouts: 51.2 us -> 8.6 us
  starting transfers between devices: 106 us -> 65.6 us
  other arithmetic: 26.6 us -> 2.89 us
    pallas_call x0 -> x3, Pallas kernels: none -> 52.2 us  [the longest x1 37 us: solve_call(): pl.pallas_call(functools.partial(solve_kernel, count=count, lanes_by=lane...]
    ppermute x30 -> x14, starting transfers between devices: 78.9 us -> 40.3 us  [the longest x2 9.81 us: halo(): x_lo = lax.ppermute(last, 'bx', up)]
    ppermute x30 -> x14, waiting for transfers between devices: 32.7 us -> 5.57 us  [the longest x2 3.56 us: halo(): y_lo = lax.ppermute(edge(BOX - SIDE), 'by', y_up)]
    all_to_all x3, waiting for transfers between devices: 28.8 us -> 8.27 us  [exchange(): return lax.all_to_all(rows, 'by', split_axis=0, concat_axis=0, tiled=True)]
    add x3 -> x0, other arithmetic: 19.3 us -> none  [the longest x2 11.1 us: solve(): damping_next * damping * search]
    slice x28 -> x0, local copies, waits for them, and re-layouts: 18.8 us -> none  [the longest x11 9.74 us: extended(): head = lax.slice_in_dim(cells, 0, width, axis=dim)]
    reshape x10 -> x0, local copies, waits for them, and re-layouts: 14.8 us -> none  [the longest x4 10.8 us: to_brick(): cube = rows.reshape(count, BOX, TILES, PER_TILE, BOX)]
    ppermute x8 -> x0, local copies, waits for them, and re-layouts: 9.44 us -> none  [the longest x4 4.74 us: extended(): lax.ppermute(head, axis, [((i + 1) % count, i) for i in range(ends)])]
  transfers between devices with their start and end apart: 33 -> 17, of which waited for: 15 -> 5; matrix products, arithmetic and copies ran while one was open for 6% -> 2% of each run, Pallas kernels for 19% -> 34%
where the time goes in v1:
time: 227 us; the launch traced here: 226 us
  Pallas kernels  134 us (59%)
  starting transfers between devices  65.6 us (29%)
  waiting for transfers between devices  13.8 us (6%)
  local copies, waits for them, and re-layouts  8.6 us (4%)
  other arithmetic  2.89 us (1%)
    pallas_call x1, Pallas kernels, update_call(): pl.pallas_call(update_kernel, in_specs=[VMEM_SPEC, VMEM_SPEC], out_specs=...  37 us
    pallas_call x1, Pallas kernels, solve_call(): pl.pallas_call(functools.partial(solve_kernel, count=count, lanes_by=lane...  37 us
    all_to_all x3, starting transfers between devices, exchange(): return lax.all_to_all(rows, 'by', split_axis=0, concat_axis=0, tiled=True)  25.2 us
    pallas_call x1, Pallas kernels, flux_call(): pl.pallas_call(functools.partial(flux_kernel, lanes_by=lanes_by), in_spec...  24 us
    pallas_call x2, Pallas kernels, assemble_call(): pl.pallas_call(functools.partial(assemble_kernel, count=count), in_specs=...  15.3 us
    pallas_call x1, Pallas kernels, correct_call(): pl.pallas_call(correct_kernel, grid=(BOX // STEP_X,), in_specs=[SMEM_SPEC...  10.7 us
    pallas_call x1, Pallas kernels, volume_call(): pl.pallas_call(functools.partial(volume_kernel, lanes_by=lanes_by), in_sp...  10.3 us
    ppermute x2, starting transfers between devices, halo(): x_lo = lax.ppermute(last, 'bx', up)  9.81 us
  transfers between devices with their start and end apart: 17, of which 5 were waited for; matrix products, arithmetic and copies ran while one was open for 2% of the time, Pallas kernels for 34%

profile of v1, /device:TPU:98, one launch (start us, length us, event | category | flops | bytes accessed | tf_op | source)
XLA Modules:
  0.0 226.3 jit_solution(13611934304428709156)
XLA Ops:
  0.6 0.8 copy.9
  1.4 0.1 reshape_squeeze.3
  1.5 0.1 fusion
  1.6 0.1 reduce_window_sum.11
  1.7 0.2 select_reduce_fusion
  1.8 0.1 reshape.65
  1.9 0.1 copy.10
  2.0 1.2 select_reduce_fusion.3.slots
  3.2 10.3 %volume_rows.1 = (f32[34,8,1280]{2,1,0:T(8,128)}, f32[16,256,128]{2,1,0:T(8,128)}) custom-call(s32[16]{0:T(128)} %select_reduce_fusion.3.slots, s32[8,39304]{1,0:T(8,128)} %fraction.1), custom_call_target="tpu_custom_call" | custom-call | tf_op jit(solution)/shard_map/volume_rows/pallas_call | solution.py:312
  13.6 7.5 %all-to-all-start = ((f32[16,256,128]{2,1,0:T(8,128)}), f32[16,256,128]{2,1,0:T(8,128)S(1)}, u32[]{:S(2)}, u32[]{:S(2)}) async-start(f32[16,256,128]{2,1,0:T(8,128)} %get-tuple-element.26), calls=%async_computation | async-start | bytes 4194304 | tf_op jit(solution)/shard_map/all_to_all | solution.py:762
  21.1 24.0 %flux_rows.1 = (f32[34,3,8,1280]{3,2,1,0:T(8,128)}, f32[16,256,128]{2,1,0:T(8,128)}) custom-call(s32[16]{0:T(128)} %select_reduce_fusion.3.slots, f32[3,8,39304]{2,1,0:T(8,128)} %bitcast.19, f32[34,8,1280]{2,1,0:T(8,128)} %get-tuple-element.22.planes), custom_call_target="tpu_custom_call" | custom-call | tf_op jit(solution)/shard_map/flux_rows/pallas_call | solution.py:328
  45.1 0.0 copy-start.17
  45.1 3.1 %all-to-all-done.recv = f32[16,256,128]{2,1,0:T(8,128)S(1)} async-done(((f32[16,256,128]{2,1,0:T(8,128)}), f32[16,256,128]{2,1,0:T(8,128)S(1)}, u32[]{:S(2)}, u32[]{:S(2)}) %all-to-all-start) | async-done | bytes 2097184 | tf_op jit(solution)/shard_map/all_to_all | solution.py:762
  48.2 1.3 copy-done.2
  49.5 8.3 %all-to-all-start.1 = ((f32[16,256,128]{2,1,0:T(8,128)}), f32[16,256,128]{2,1,0:T(8,128)S(1)}, u32[]{:S(2)}, u32[]{:S(2)}) async-start(f32[16,256,128]{2,1,0:T(8,128)} %get-tuple-element.33), calls=%async_computation.1 | async-start | bytes 4194304 | tf_op jit(solution)/shard_map/all_to_all | solution.py:762
  57.8 0.7 dynamic-slice_reduce_fusion.table
  58.4 7.6 %brick.2 = (f32[1024,128]{1,0:T(8,128)}, f32[160,128]{1,0:T(8,128)}, f32[160,128]{1,0:T(8,128)}, f32[2,32,128]{2,1,0:T(8,128)}, f32[32,128]{1,0:T(8,128)}, /*index=5*/f32[32,128]{1,0:T(8,128)}) custom-call(s32[4]{0:T(128)} %dynamic-slice_reduce_fusion.table, s32[1]{0:T(128)} %bitcast.2.side, f32[16,256,128]{2,1,0:T(8,128)} %copy-done.2), custom_call_target="tpu_custom_call" | custom-call | tf_op jit(solution)/shard_map/brick/pallas_call | solution.py:668
  66.1 5.0 %collective-permute-start = (f32[160,128]{1,0:T(8,128)}, f32[160,128]{1,0:T(8,128)S(1)}, u32[]{:S(2)}, u32[]{:S(2)}) collective-permute-start(f32[160,128]{1,0:T(8,128)} %get-tuple-element.28), channel_id=1, source_target_pairs={{0,32},{32,64},{64,96},{96,128},{128,160},{160,192},{192,224},{1,3... | collective-permute-start | bytes 245768 | tf_op jit(solution)/shard_map/ppermute | solution.py:697
  71.1 1.9 collective-permute-start.3
  73.1 3.6 %collective-permute-start.4 = (f32[32,128]{1,0:T(8,128)}, f32[32,128]{1,0:T(8,128)S(1)}, u32[]{:S(2)}, u32[]{:S(2)}) collective-permute-start(f32[32,128]{1,0:T(8,128)} %get-tuple-element.32), channel_id=1, source_target_pairs={{32,1},{33,0},{64,33},{65,32},{96,65},{97,64},{128,97},{129,96},{1... | collective-permute-start | bytes 49160 | tf_op jit(solution)/shard_map/ppermute | solution.py:700
  76.7 0.1 collective-permute-start.2
  76.8 2.3 %collective-permute-start.1 = (f32[160,128]{1,0:T(8,128)}, f32[160,128]{1,0:T(8,128)S(1)}, u32[]{:S(2)}, u32[]{:S(2)}) collective-permute-start(f32[160,128]{1,0:T(8,128)} %get-tuple-element.29), channel_id=1, source_target_pairs={{32,0},{64,32},{96,64},{128,96},{160,128},{192,160},{224,192},{33,... | collective-permute-start | bytes 245768 | tf_op jit(solution)/shard_map/ppermute | solution.py:698
  79.1 5.2 %all-to-all-done.1.recv = f32[16,256,128]{2,1,0:T(8,128)S(1)} async-done(((f32[16,256,128]{2,1,0:T(8,128)}), f32[16,256,128]{2,1,0:T(8,128)S(1)}, u32[]{:S(2)}, u32[]{:S(2)}) %all-to-all-start.1) | async-done | bytes 2097184 | tf_op jit(solution)/shard_map/all_to_all | solution.py:762
  84.3 1.3 copy-done.1
  85.6 7.6 %brick.3 = (f32[1024,128]{1,0:T(8,128)}, f32[160,128]{1,0:T(8,128)}, f32[160,128]{1,0:T(8,128)}, f32[2,32,128]{2,1,0:T(8,128)}, f32[32,128]{1,0:T(8,128)}, /*index=5*/f32[32,128]{1,0:T(8,128)}) custom-call(s32[4]{0:T(128)} %dynamic-slice_reduce_fusion.table, s32[1]{0:T(128)} %bitcast.2.side, f32[16,256,128]{2,1,0:T(8,128)} %copy-done.1), custom_call_target="tpu_custom_call" | custom-call | tf_op jit(solution)/shard_map/brick/pallas_call | solution.py:668
  93.2 0.0 collective-permute-done.refs_1_
  93.2 0.0 copy-start.7
  93.3 3.5 %collective-permute-start.10 = (f32[32,128]{1,0:T(8,128)}, f32[32,128]{1,0:T(8,128)S(1)}, u32[]{:S(2)}, u32[]{:S(2)}) collective-permute-start(f32[32,128]{1,0:T(8,128)} %get-tuple-element.38), channel_id=1, source_target_pairs={{0,33},{1,32},{32,65},{33,64},{64,97},{65,96},{96,129},{97,128},{1... | collective-permute-start | bytes 49160 | tf_op jit(solution)/shard_map/ppermute | solution.py:699
  96.8 1.0 slice_dynamic-update-slice_fusion.2
  97.8 0.0 collective-permute-done.1.refs_2_
  97.8 0.0 copy-start.8
  97.8 2.1 collective-permute-start.11
  99.9 0.0 collective-permute-done.3.refs_4_
  99.9 1.6 collective-permute-start.9
  101.5 0.0 collective-permute-done.2.refs_3_
  101.5 4.8 %collective-permute-start.7 = (f32[160,128]{1,0:T(8,128)}, f32[160,128]{1,0:T(8,128)S(1)}, u32[]{:S(2)}, u32[]{:S(2)}) collective-permute-start(f32[160,128]{1,0:T(8,128)} %get-tuple-element.35), channel_id=1, source_target_pairs={{0,32},{32,64},{64,96},{96,128},{128,160},{160,192},{192,224},{1,3... | collective-permute-start | bytes 245768 | tf_op jit(solution)/shard_map/ppermute | solution.py:697
  106.3 0.0 collective-permute-done.4.refs_5_
  106.3 1.9 collective-permute-start.8
  108.3 0.7 collective-permute-done.7.refs_9_
  108.9 5.7 %collective-permute-start.6 = (f32[46,8,128]{2,1,0:T(8,128)S(1)}, f32[46,8,128]{2,1,0:T(8,128)S(1)}, u32[]{:S(2)}, u32[]{:S(2)}) collective-permute-start(f32[46,8,128]{2,1,0:T(8,128)S(1)} %get-tuple-element.62), channel_id=1, source_target_pairs={{2,0},{4,2},{6,4},{8,6},{10,8},{12,10},{14,12},{16,14},{18,16},{20... | collective-permute-start | bytes 565256 | tf_op jit(solution)/shard_map/ppermute | solution.py:708
  114.7 1.0 slice_dynamic-update-slice_fusion
  115.6 0.0 collective-permute-done.8.refs_10_
  115.7 1.9 collective-permute-start.5
  117.6 0.0 collective-permute-done.10.refs_12_
  117.6 0.0 collective-permute-done.9.refs_11_
  117.7 0.0 collective-permute-done.11.refs_13_
  117.7 0.0 copy-start.16
  117.7 3.9 %collective-permute-start.13 = (f32[46,8,128]{2,1,0:T(8,128)S(1)}, f32[46,8,128]{2,1,0:T(8,128)S(1)}, u32[]{:S(2)}, u32[]{:S(2)}) collective-permute-start(f32[46,8,128]{2,1,0:T(8,128)S(1)} %get-tuple-element.58), channel_id=1, source_target_pairs={{2,0},{4,2},{6,4},{8,6},{10,8},{12,10},{14,12},{16,14},{18,16},{20... | collective-permute-start | bytes 565256 | tf_op jit(solution)/shard_map/ppermute | solution.py:708
  121.6 1.9 collective-permute-start.12
  123.6 0.6 select_reduce_fusion.2.box_of_row
  124.2 0.0 collective-permute-done.6.refs_7_
  124.2 0.0 collective-permute-done.5.refs_6_
  124.2 1.3 collective-permute-done.13.refs_15_
  125.6 3.6 %collective-permute-done.12.refs_14_ = f32[46,8,128]{2,1,0:T(8,128)S(1)} collective-permute-done((f32[46,8,128]{2,1,0:T(8,128)S(1)}, f32[46,8,128]{2,1,0:T(8,128)S(1)}, u32[]{:S(2)}, u32[]{:S(2)}) %collective-permute-start.12) | collective-permute-done | bytes 188448 | tf_op jit(solution)/shard_map/ppermute | solution.py:707
  129.1 0.0 copy-done.7
  129.1 0.0 copy-done.13
  129.2 0.7 copy-done.6
  129.9 37.0 %solve.1 = (f32[32,32,128]{2,1,0:T(8,128)}, f32[16,304,128]{2,1,0:T(8,128)}) custom-call(s32[16]{0:T(128)} %select_reduce_fusion.2.box_of_row, s32[1]{0:T(128)} %bitcast.2.side, f32[1024,128]{1,0:T(8,128)} %get-tuple-element.27.refs_0_, f32[160,128]{1,0:T(8,128)} %copy-done.7, f32[160,128]{1,0:T(8,128)} %copy-done.8, f32[2,32,128]{2,1,0:T(8,128)} %copy-done.11, ...), custom_call_target="tpu_custom_call" | custom-call | tf_op jit(solution)/shard_map/solve/pallas_call | solution.py:716
  166.9 9.5 %all-to-all-start.2 = ((f32[16,304,128]{2,1,0:T(8,128)}), f32[16,304,128]{2,1,0:T(8,128)S(1)}, u32[]{:S(2)}, u32[]{:S(2)}) async-start(f32[16,304,128]{2,1,0:T(8,128)} %get-tuple-element.40), calls=%async_computation.2 | async-start | bytes 4980736 | tf_op jit(solution)/shard_map/all_to_all | solution.py:762
  176.4 37.0 %updated.1 = (f32[32,3,8,1024]{3,2,1,0:T(8,128)}, f32[32,6,8,1024]{3,2,1,0:T(8,128)}) custom-call(f32[34,3,8,1280]{3,2,1,0:T(8,128)} %get-tuple-element.23.masses, f32[34,8,1280]{2,1,0:T(8,128)} %get-tuple-element.22.planes), custom_call_target="tpu_custom_call" | custom-call | tf_op jit(solution)/shard_map/updated/pallas_call | solution.py:345
  213.4 0.7 select_reduce_fusion.1.rows
  214.1 0.0 all-to-all-done.2.returned
  214.1 1.5 copy-done
  215.6 10.7 %corrected.1 = f32[3,8,32768]{2,1,0:T(8,128)} custom-call(s32[8]{0:T(128)} %select_reduce_fusion.1.rows, f32[32,3,8,1024]{3,2,1,0:T(8,128)} %get-tuple-element.24.updated, f32[32,6,8,1024]{3,2,1,0:T(8,128)} %get-tuple-element.25.apertures, f32[16,304,128]{2,1,0:T(8,128)} %copy-done), custom_call_target="tpu_custom_call" | custom-call | tf_op jit(solution)/shard_map/corrected/pallas_call | solution.py:355
  (40 shorter events, 0.1 us)
Async XLA Ops:
  13.6 34.6 %all-to-all-start = ((f32[16,256,128]{2,1,0:T(8,128)}), f32[16,256,128]{2,1,0:T(8,128)S(1)}, u32[]{:S(2)}, u32[]{:S(2)}) async-start(f32[16,256,128]{2,1,0:T(8,128)} %get-tuple-element.26), calls=%async_computation | async-start | bytes 4194304 | tf_op jit(solution)/shard_map/all_to_all | solution.py:762
  45.1 12.7 %copy-start.17 = (s32[1,16,1,4]{1,3,2,0:T(4,128)S(1)}, s32[1,16,1,4]{1,3,2,0:T(4,128)}, u32[]{:S(2)}) copy-start(s32[1,16,1,4]{1,3,2,0:T(4,128)} %param.5) | copy-start | bytes 772
  48.2 1.3 copy-start.2
  49.5 34.8 %all-to-all-start.1 = ((f32[16,256,128]{2,1,0:T(8,128)}), f32[16,256,128]{2,1,0:T(8,128)S(1)}, u32[]{:S(2)}, u32[]{:S(2)}) async-start(f32[16,256,128]{2,1,0:T(8,128)} %get-tuple-element.33), calls=%async_computation.1 | async-start | bytes 4194304 | tf_op jit(solution)/shard_map/all_to_all | solution.py:762
  58.4 65.1 %copy-start.18 = (s32[4]{0:T(128)S(1)}, s32[4]{0:T(128)}, u32[]{:S(2)}) copy-start(s32[4]{0:T(128)} %dynamic-slice_reduce_fusion.table) | copy-start | bytes 52
  66.1 27.1 %collective-permute-start = (f32[160,128]{1,0:T(8,128)}, f32[160,128]{1,0:T(8,128)S(1)}, u32[]{:S(2)}, u32[]{:S(2)}) collective-permute-start(f32[160,128]{1,0:T(8,128)} %get-tuple-element.28), channel_id=1, source_target_pairs={{0,32},{32,64},{64,96},{96,128},{128,160},{160,192},{192,224},{1,3... | collective-permute-start | bytes 245768 | tf_op jit(solution)/shard_map/ppermute | solution.py:697
  71.1 28.7 %collective-permute-start.3 = (f32[32,128]{1,0:T(8,128)}, f32[32,128]{1,0:T(8,128)S(1)}, u32[]{:S(2)}, u32[]{:S(2)}) collective-permute-start(f32[32,128]{1,0:T(8,128)} %get-tuple-element.31), channel_id=1, source_target_pairs={{0,33},{1,32},{32,65},{33,64},{64,97},{65,96},{96,129},{97,128},{1... | collective-permute-start | bytes 49160 | tf_op jit(solution)/shard_map/ppermute | solution.py:699
  73.1 33.2 %collective-permute-start.4 = (f32[32,128]{1,0:T(8,128)}, f32[32,128]{1,0:T(8,128)S(1)}, u32[]{:S(2)}, u32[]{:S(2)}) collective-permute-start(f32[32,128]{1,0:T(8,128)} %get-tuple-element.32), channel_id=1, source_target_pairs={{32,1},{33,0},{64,33},{65,32},{96,65},{97,64},{128,97},{129,96},{1... | collective-permute-start | bytes 49160 | tf_op jit(solution)/shard_map/ppermute | solution.py:700
  76.7 24.8 %collective-permute-start.2 = (f32[2,32,128]{2,1,0:T(8,128)}, f32[2,32,128]{2,1,0:T(8,128)S(1)}, u32[]{:S(2)}, u32[]{:S(2)}) collective-permute-start(f32[2,32,128]{2,1,0:T(8,128)} %get-tuple-element.30), channel_id=1, source_target_pairs={{0,1},{1,0},{2,3},{3,2},{4,5},{5,4},{6,7},{7,6},{8,9},{9,8},{10,11... | collective-permute-start | bytes 98312 | tf_op jit(solution)/shard_map/ppermute | solution.py:692
  76.8 21.0 %collective-permute-start.1 = (f32[160,128]{1,0:T(8,128)}, f32[160,128]{1,0:T(8,128)S(1)}, u32[]{:S(2)}, u32[]{:S(2)}) collective-permute-start(f32[160,128]{1,0:T(8,128)} %get-tuple-element.29), channel_id=1, source_target_pairs={{32,0},{64,32},{96,64},{128,96},{160,128},{192,160},{224,192},{33,... | collective-permute-start | bytes 245768 | tf_op jit(solution)/shard_map/ppermute | solution.py:698
  84.3 1.3 copy-start.1
  93.2 35.9 %copy-start.7 = (f32[160,128]{1,0:T(8,128)}, f32[160,128]{1,0:T(8,128)S(1)}, u32[]{:S(2)}) copy-start(f32[160,128]{1,0:T(8,128)S(1)} %collective-permute-done.refs_1_) | copy-start | bytes 245764
  93.3 24.4 %collective-permute-start.10 = (f32[32,128]{1,0:T(8,128)}, f32[32,128]{1,0:T(8,128)S(1)}, u32[]{:S(2)}, u32[]{:S(2)}) collective-permute-start(f32[32,128]{1,0:T(8,128)} %get-tuple-element.38), channel_id=1, source_target_pairs={{0,33},{1,32},{32,65},{33,64},{64,97},{65,96},{96,129},{97,128},{1... | collective-permute-start | bytes 49160 | tf_op jit(solution)/shard_map/ppermute | solution.py:699
  97.8 31.3 %copy-start.8 = (f32[160,128]{1,0:T(8,128)}, f32[160,128]{1,0:T(8,128)S(1)}, u32[]{:S(2)}) copy-start(f32[160,128]{1,0:T(8,128)S(1)} %collective-permute-done.1.refs_2_) | copy-start | bytes 245764
  97.8 19.9 %collective-permute-start.11 = (f32[32,128]{1,0:T(8,128)}, f32[32,128]{1,0:T(8,128)S(1)}, u32[]{:S(2)}, u32[]{:S(2)}) collective-permute-start(f32[32,128]{1,0:T(8,128)} %get-tuple-element.39), channel_id=1, source_target_pairs={{32,1},{33,0},{64,33},{65,32},{96,65},{97,64},{128,97},{129,96},{1... | collective-permute-start | bytes 49160 | tf_op jit(solution)/shard_map/ppermute | solution.py:700
  99.9 29.2 %copy-start.13 = (f32[32,128]{1,0:T(8,128)}, f32[32,128]{1,0:T(8,128)S(1)}, u32[]{:S(2)}) copy-start(f32[32,128]{1,0:T(8,128)S(1)} %collective-permute-done.3.refs_4_) | copy-start | bytes 49156
  99.9 17.8 %collective-permute-start.9 = (f32[2,32,128]{2,1,0:T(8,128)}, f32[2,32,128]{2,1,0:T(8,128)S(1)}, u32[]{:S(2)}, u32[]{:S(2)}) collective-permute-start(f32[2,32,128]{2,1,0:T(8,128)} %get-tuple-element.37), channel_id=1, source_target_pairs={{0,1},{1,0},{2,3},{3,2},{4,5},{5,4},{6,7},{7,6},{8,9},{9,8},{10,11... | collective-permute-start | bytes 98312 | tf_op jit(solution)/shard_map/ppermute | solution.py:692
  101.5 27.6 %copy-start.11 = (f32[2,32,128]{2,1,0:T(8,128)}, f32[2,32,128]{2,1,0:T(8,128)S(1)}, u32[]{:S(2)}) copy-start(f32[2,32,128]{2,1,0:T(8,128)S(1)} %collective-permute-done.2.refs_3_) | copy-start | bytes 98308
  101.5 7.4 %collective-permute-start.7 = (f32[160,128]{1,0:T(8,128)}, f32[160,128]{1,0:T(8,128)S(1)}, u32[]{:S(2)}, u32[]{:S(2)}) collective-permute-start(f32[160,128]{1,0:T(8,128)} %get-tuple-element.35), channel_id=1, source_target_pairs={{0,32},{32,64},{64,96},{96,128},{128,160},{160,192},{192,224},{1,3... | collective-permute-start | bytes 245768 | tf_op jit(solution)/shard_map/ppermute | solution.py:697
  106.3 22.8 %copy-start.14 = (f32[32,128]{1,0:T(8,128)}, f32[32,128]{1,0:T(8,128)S(1)}, u32[]{:S(2)}) copy-start(f32[32,128]{1,0:T(8,128)S(1)} %collective-permute-done.4.refs_5_) | copy-start | bytes 49156
  106.3 9.3 %collective-permute-start.8 = (f32[160,128]{1,0:T(8,128)}, f32[160,128]{1,0:T(8,128)S(1)}, u32[]{:S(2)}, u32[]{:S(2)}) collective-permute-start(f32[160,128]{1,0:T(8,128)} %get-tuple-element.36), channel_id=1, source_target_pairs={{32,0},{64,32},{96,64},{128,96},{160,128},{192,160},{224,192},{33,... | collective-permute-start | bytes 245768 | tf_op jit(solution)/shard_map/ppermute | solution.py:698
  108.9 20.2 %copy-start.9 = (f32[160,128]{1,0:T(8,128)}, f32[160,128]{1,0:T(8,128)S(1)}, u32[]{:S(2)}) copy-start(f32[160,128]{1,0:T(8,128)S(1)} %collective-permute-done.7.refs_9_) | copy-start | bytes 245764
  108.9 15.3 %collective-permute-start.6 = (f32[46,8,128]{2,1,0:T(8,128)S(1)}, f32[46,8,128]{2,1,0:T(8,128)S(1)}, u32[]{:S(2)}, u32[]{:S(2)}) collective-permute-start(f32[46,8,128]{2,1,0:T(8,128)S(1)} %get-tuple-element.62), channel_id=1, source_target_pairs={{2,0},{4,2},{6,4},{8,6},{10,8},{12,10},{14,12},{16,14},{18,16},{20... | collective-permute-start | bytes 565256 | tf_op jit(solution)/shard_map/ppermute | solution.py:708
  115.7 13.5 %copy-start.10 = (f32[160,128]{1,0:T(8,128)}, f32[160,128]{1,0:T(8,128)S(1)}, u32[]{:S(2)}) copy-start(f32[160,128]{1,0:T(8,128)S(1)} %collective-permute-done.8.refs_10_) | copy-start | bytes 245764
  115.7 8.6 %collective-permute-start.5 = (f32[46,8,128]{2,1,0:T(8,128)S(1)}, f32[46,8,128]{2,1,0:T(8,128)S(1)}, u32[]{:S(2)}, u32[]{:S(2)}) collective-permute-start(f32[46,8,128]{2,1,0:T(8,128)S(1)} %get-tuple-element.63), channel_id=1, source_target_pairs={{0,2},{2,4},{4,6},{6,8},{8,10},{10,12},{12,14},{14,16},{16,18},{18... | collective-permute-start | bytes 565256 | tf_op jit(solution)/shard_map/ppermute | solution.py:707
  117.6 11.6 %copy-start.15 = (f32[32,128]{1,0:T(8,128)}, f32[32,128]{1,0:T(8,128)S(1)}, u32[]{:S(2)}) copy-start(f32[32,128]{1,0:T(8,128)S(1)} %collective-permute-done.10.refs_12_) | copy-start | bytes 49156
  117.7 11.5 %copy-start.12 = (f32[2,32,128]{2,1,0:T(8,128)}, f32[2,32,128]{2,1,0:T(8,128)S(1)}, u32[]{:S(2)}) copy-start(f32[2,32,128]{2,1,0:T(8,128)S(1)} %collective-permute-done.9.refs_11_) | copy-start | bytes 98308
  117.7 11.5 %copy-start.16 = (f32[32,128]{1,0:T(8,128)}, f32[32,128]{1,0:T(8,128)S(1)}, u32[]{:S(2)}) copy-start(f32[32,128]{1,0:T(8,128)S(1)} %collective-permute-done.11.refs_13_) | copy-start | bytes 49156
  117.7 7.9 %collective-permute-start.13 = (f32[46,8,128]{2,1,0:T(8,128)S(1)}, f32[46,8,128]{2,1,0:T(8,128)S(1)}, u32[]{:S(2)}, u32[]{:S(2)}) collective-permute-start(f32[46,8,128]{2,1,0:T(8,128)S(1)} %get-tuple-element.58), channel_id=1, source_target_pairs={{2,0},{4,2},{6,4},{8,6},{10,8},{12,10},{14,12},{16,14},{18,16},{20... | collective-permute-start | bytes 565256 | tf_op jit(solution)/shard_map/ppermute | solution.py:708
  121.6 7.5 %collective-permute-start.12 = (f32[46,8,128]{2,1,0:T(8,128)S(1)}, f32[46,8,128]{2,1,0:T(8,128)S(1)}, u32[]{:S(2)}, u32[]{:S(2)}) collective-permute-start(f32[46,8,128]{2,1,0:T(8,128)S(1)} %get-tuple-element.59), channel_id=1, source_target_pairs={{0,2},{2,4},{4,6},{6,8},{8,10},{10,12},{12,14},{14,16},{16,18},{18... | collective-permute-start | bytes 565256 | tf_op jit(solution)/shard_map/ppermute | solution.py:707
  124.2 5.0 %copy-start.3 = (f32[46,8,128]{2,1,0:T(8,128)}, f32[46,8,128]{2,1,0:T(8,128)S(1)}, u32[]{:S(2)}) copy-start(f32[46,8,128]{2,1,0:T(8,128)S(1)} %collective-permute-done.6.refs_7_) | copy-start | bytes 565252
  124.2 5.0 %copy-start.4 = (f32[46,8,128]{2,1,0:T(8,128)}, f32[46,8,128]{2,1,0:T(8,128)S(1)}, u32[]{:S(2)}) copy-start(f32[46,8,128]{2,1,0:T(8,128)S(1)} %collective-permute-done.5.refs_6_) | copy-start | bytes 565252
  125.6 3.7 %copy-start.5 = (f32[46,8,128]{2,1,0:T(8,128)}, f32[46,8,128]{2,1,0:T(8,128)S(1)}, u32[]{:S(2)}) copy-start(f32[46,8,128]{2,1,0:T(8,128)S(1)} %collective-permute-done.13.refs_15_) | copy-start | bytes 565252
  129.2 0.7 copy-start.6
  166.9 47.2 %all-to-all-start.2 = ((f32[16,304,128]{2,1,0:T(8,128)}), f32[16,304,128]{2,1,0:T(8,128)S(1)}, u32[]{:S(2)}, u32[]{:S(2)}) async-start(f32[16,304,128]{2,1,0:T(8,128)} %get-tuple-element.40), calls=%async_computation.2 | async-start | bytes 4980736 | tf_op jit(solution)/shard_map/all_to_all | solution.py:762
  214.1 1.5 copy-start

commit v2 on v1

--- a/solution.py
+++ b/solution.py
@@ -26,6 +26,7 @@
 VMEM_SPEC = pl.BlockSpec(memory_space=pltpu.VMEM)
 SMEM_SPEC = pl.BlockSpec(memory_space=pltpu.SMEM)
 ANY_SPEC = pl.BlockSpec(memory_space=pl.ANY)
+HBM_SPEC = pl.BlockSpec(memory_space=pltpu.HBM)
 
 
 def lane_index():
@@ -287,12 +288,10 @@
             y_ahead = jnp.where(lanes < TILE - BOX, reverse[q], after)
             z_behind = pltpu.roll(p, 1, 1)
             z_ahead = pltpu.roll(p, TILE - 1, 1)
-            for r in range(PER_TILE):
-                source = BOX * i + PER_TILE * q + r
-                low = pltpu.roll(z_low, (BOX * r - source) % TILE, 1)
-                high = pltpu.roll(z_high, (BOX * r + BOX - 1 - source) % TILE, 1)
-                z_behind = jnp.where(lanes == BOX * r, low, z_behind)
-                z_ahead = jnp.where(lanes == BOX * r + BOX - 1, high, z_ahead)
+            low = pltpu.roll(z_low, (TILE - TILES * i - q) % TILE, 1) if i + q else z_low
+            high = pltpu.roll(z_high, (BOX - 1 - TILES * i - q) % TILE, 1)
+            z_behind = jnp.where(lanes % BOX == 0, low, z_behind)
+            z_ahead = jnp.where(lanes % BOX == BOX - 1, high, z_ahead)
             cut = slice(q * TILE, (q + 1) * TILE)
             around = ((below[q], above[q]), (y_behind, y_ahead), (z_behind, z_ahead))
             for c, (lower, upper) in enumerate(around):
@@ -312,7 +311,7 @@
     return pl.pallas_call(
         functools.partial(volume_kernel, lanes_by=lanes_by),
         in_specs=[SMEM_SPEC, VMEM_SPEC],
-        out_specs=[VMEM_SPEC, ANY_SPEC],
+        out_specs=[VMEM_SPEC, HBM_SPEC],
         out_shape=[struct(PADDED, 8, WIDE), struct(lanes_by, ROWS, TILE)],
         scratch_shapes=[
             pltpu.VMEM((8 * ROWS, TILE), jnp.float32),
@@ -328,7 +327,7 @@
     return pl.pallas_call(
         functools.partial(flux_kernel, lanes_by=lanes_by),
         in_specs=[SMEM_SPEC, VMEM_SPEC, VMEM_SPEC],
-        out_specs=[VMEM_SPEC, ANY_SPEC],
+        out_specs=[VMEM_SPEC, HBM_SPEC],
         out_shape=[struct(PADDED, 3, 8, WIDE), struct(lanes_by, ROWS, TILE)],
         scratch_shapes=[
             pltpu.VMEM((PADDED, 3, 8, WIDE), jnp.float32),
@@ -367,8 +366,14 @@
             pltpu.VMEM((8 * RETURN_ROWS, TILE), jnp.float32),
             pltpu.SemaphoreType.DMA((8,)),
         ],
+        compiler_params=pltpu.CompilerParams(vmem_limit_bytes=14 << 20),
         name="corrected",
-    )(slot_row, updated, apertures, returned)
+    )(
+        slot_row,
+        pltpu.with_memory_space_constraint(updated, pltpu.HBM),
+        pltpu.with_memory_space_constraint(apertures, pltpu.HBM),
+        returned,
+    )
 
 
 HALO = 5
@@ -380,25 +385,30 @@
 GROUPS = BOX // GROUP + 2
 
 
-def wide_lane():
-    return lax.broadcasted_iota(jnp.int32, (ROWS_Y, TILE), 1)
-
-
-def assemble_kernel(table, side, recv, brick, first, last, strip, strip_first, strip_last, boxes, sem, *, count):
+def loop(start, stop, body, unroll):
+    def several(i, carry):
+        for j in range(unroll):
+            body(start + i * unroll + j)
+        return carry
+
+    lax.fori_loop(0, (stop - start) // unroll, several, 0)
+
+
+STEP_BRICK = 8
+
+
+def assemble_kernel(table, side, *refs, count):
+    boxes = refs[:count]
+    brick, first, last, strip, strip_first, strip_last = refs[count:]
+    step = pl.program_id(0)
+    steps = BOX // STEP_BRICK
     lanes = lane_index()
-    copies = [
-        pltpu.make_async_copy(recv.at[table[k]], boxes.at[k], sem.at[k]) for k in range(count)
-    ]
-    for copy in copies:
-        copy.start()
-    for copy in copies:
-        copy.wait()
-    strip[...] = jnp.zeros_like(strip)
     lanes_brick = lax.broadcasted_iota(jnp.int32, (BOX, TILE), 1)
     source_lane = jnp.where(side[0] == 0, TILE - SLOT, 0)
-
-    def step(x, carry):
-        rows = [boxes[k, pl.ds(x * TILES, TILES), :] for k in range(count)]
+    half = step % (GROUP // STEP_BRICK) * STEP_BRICK
+
+    for x in range(STEP_BRICK):
+        rows = [boxes[k][0, x * TILES : (x + 1) * TILES, :] for k in range(count)]
         for r in range(PER_TILE):
             value = None
             for k in reversed(range(count)):
@@ -406,27 +416,40 @@
                 piece = pltpu.roll(rows[k], shift, 1) if shift else rows[k]
                 value = piece if value is None else jnp.where(lanes < BOX * (k + 1), piece, value)
             brick[pl.ds(x * BOX + r, TILES, stride=PER_TILE), :] = value
-        plane = brick[pl.ds(x * BOX, BOX), :]
-        group = x // GROUP
-        lane = (x % GROUP) * SLOT
+    group = step // (GROUP // STEP_BRICK)
+    value = jnp.zeros((BOX, TILE), jnp.float32)
+    for x in range(STEP_BRICK):
+        lane = (half + x) * SLOT
+        plane = brick[x * BOX : (x + 1) * BOX, :]
         moved = pltpu.roll(plane, (lane - source_lane + TILE) % TILE, 1)
-        strip[group] = jnp.where(lanes_brick // SLOT == x % GROUP, moved, strip[group])
-        return carry
-
-    lax.fori_loop(0, BOX, step, 0)
-    first[...] = brick[0 : HALO * BOX, :]
-    last[...] = brick[(BOX - HALO) * BOX : BOX * BOX, :]
-    strip_first[...] = strip[0]
-    strip_last[...] = strip[BOX // GROUP - 1]
+        value = jnp.where(lanes_brick // SLOT == half + x, moved, value)
+
+    @pl.when(half == 0)
+    def _():
+        strip[group] = value
+
+    @pl.when(half != 0)
+    def _():
+        strip[group] = jnp.where(lanes_brick // SLOT >= half, value, strip[group])
+
+    @pl.when(step == 0)
+    def _():
+        first[...] = brick[0 : HALO * BOX, :]
+
+    @pl.when(step == steps - 1)
+    def _():
+        last[...] = brick[(STEP_BRICK - HALO) * BOX : STEP_BRICK * BOX, :]
+        strip_first[...] = strip[0]
+        strip_last[...] = strip[BOX // GROUP - 1]
 
 
 def solve_kernel(box_of_row, side, *refs, count, lanes_by):
     volume_in, source_in = refs[0:8], refs[8:16]
     pressure, rows = refs[16:18]
     scratch = refs[18:]
-    (vol, ax, ayu, ayl, azu, azl, diag, inv, res, sa, sb, total) = scratch[0:12]
-    (hvol, hres, hsa, hsb, htotal, hcoef, edge, turned, packed, sem) = scratch[12:]
-    lane = wide_lane()
+    (vol, ax, ay, azu, azl, diag, inv, res, sa, sb, total) = scratch[0:11]
+    (hvol, hres, hsa, hsb, htotal, edge_a, edge_b, hcoef, turned, packed, sem) = scratch[11:]
+    lane = lane_index()
     at_top = side[0] == 0
     edge_lane = jnp.where(at_top, TILE - 1, 0)
     slot_lane = jnp.where(at_top, 0, SLOT - 1)
@@ -434,159 +457,183 @@
     low_lane = jnp.where(at_top, -1, 0)
     open_up = (lane % SLOT == SLOT - 1) & (low_lane == 0)
     open_low = (lane % SLOT == 0) & (up_lane >= 0)
-
-    def main(ref, x):
-        return ref[pl.ds(pl.multiple_of(x * ROWS_Y, 8), ROWS_Y), :]
-
-    def put(ref, x, value):
-        ref[pl.ds(pl.multiple_of(x * ROWS_Y, 8), ROWS_Y), :] = value
+    row_tiles = range(ROWS_Y // 8)
+
+    def base(x):
+        return pl.multiple_of(x * ROWS_Y, 8)
+
+    def tile(ref, start, t, offset=0):
+        return ref[pl.ds(start + 8 * t + offset, 8), :]
+
+    def put(ref, start, t, value):
+        ref[pl.ds(start + 8 * t, 8), :] = value
+
+    def strip_base(g):
+        return g * ROWS_Y + 8
 
     def fill(ext, strips, parts):
         brick, x_lo, x_hi, middle, z_lo, z_hi, y_lo, y_hi = parts
 
         def rows_of(x):
-            ext[pl.ds(pl.multiple_of(x * ROWS_Y, 8), SIDE), :] = y_lo[x]
-            ext[pl.ds(pl.multiple_of(x * ROWS_Y + SIDE + BOX, 8), SIDE), :] = y_hi[x]
-
-        def body(i, carry):
-            ext[pl.ds(pl.multiple_of((i + HALO) * ROWS_Y + SIDE, 8), BOX), :] = brick[
-                pl.ds(pl.multiple_of(i * BOX, 8), BOX), :
-            ]
+            ext[pl.ds(base(x), SIDE), :] = y_lo[x]
+            ext[pl.ds(base(x) + SIDE + BOX, SIDE), :] = y_hi[x]
+
+        def body(i):
+            ext[pl.ds(base(i + HALO) + SIDE, BOX), :] = brick[pl.ds(pl.multiple_of(i * BOX, 8), BOX), :]
             rows_of(i + HALO)
-            return carry
-
-        lax.fori_loop(0, BOX, body, 0)
+
+        loop(0, BOX, body, 4)
         for i in range(HALO):
             for x, part in ((i, x_lo), (HALO + BOX + i, x_hi)):
                 ext[x * ROWS_Y + SIDE : x * ROWS_Y + SIDE + BOX, :] = part[i * BOX : (i + 1) * BOX, :]
                 rows_of(x)
         pieces = [z_lo[...]] + [middle[g] for g in range(GROUPS - 2)] + [z_hi[...]]
         for g, piece in enumerate(pieces):
-            strips[g, 0:SIDE] = y_lo[EXT + g]
-            strips[g, SIDE : SIDE + BOX] = piece
-            strips[g, SIDE + BOX : ROWS_Y] = y_hi[EXT + g]
+            start = strip_base(g)
+            strips[start : start + SIDE, :] = y_lo[EXT + g]
+            strips[start + SIDE : start + SIDE + BOX, :] = piece
+            strips[start + SIDE + BOX : start + ROWS_Y, :] = y_hi[EXT + g]
 
     fill(vol, hvol, volume_in)
     fill(res, hres, source_in)
+    guard = jnp.zeros((8, TILE), jnp.float32)
+    for ref in (hvol, hsa, hsb):
+        ref[0:8, :] = guard
+        ref[GROUPS * ROWS_Y + 8 : GROUPS * ROWS_Y + 16, :] = guard
+    for ref in (edge_a, edge_b):
+        ref[...] = jnp.zeros_like(ref)
 
     def place(x):
-        return (x + GROUP - HALO) // GROUP, (x + GROUP - HALO) % GROUP * SLOT + slot_lane
-
-    def strip_value(strips, x):
-        group, where = place(x)
-        return pltpu.roll(strips[group], (edge_lane - where + TILE) % TILE, 1)
-
-    def gather_edge(ref):
-        def body(x, carry):
-            group, where = place(x)
-            moved = pltpu.roll(main(ref, x), (where - edge_lane + TILE) % TILE, 1)
-            edge[group] = jnp.where(lane == where, moved, edge[group])
-            return carry
-
-        lax.fori_loop(1, EXT - 1, body, 0)
-
-    def y_up(value):
-        return pltpu.roll(value, ROWS_Y - 1, 0)
-
-    def y_down(value):
-        return pltpu.roll(value, 1, 0)
-
-    def z_sides(value, outside):
+        group = (x + GROUP - HALO) // GROUP
+        where = (x + GROUP - HALO) % GROUP * SLOT + slot_lane
+        return pl.multiple_of(group * ROWS_Y + 8, 8), where
+
+    def to_edge(edge, start, t, where, value):
+        moved = pltpu.roll(value, (where - edge_lane + TILE) % TILE, 1)
+        pltpu.store(edge.at[pl.ds(start + 8 * t, 8), :], moved, mask=lane == where)
+
+    def z_sides(value, strips, start, t, where):
+        outside = pltpu.roll(tile(strips, start, t), (edge_lane - where + TILE) % TILE, 1)
         up = jnp.where(lane == up_lane, outside, pltpu.roll(value, TILE - 1, 1))
         down = jnp.where(lane == low_lane, outside, pltpu.roll(value, 1, 1))
         return up, down
 
-    def strip_sides(strips, g):
-        here = strips[g]
-        following = strips[min(g + 1, GROUPS - 1)]
-        previous = strips[max(g - 1, 0)]
-        x_up = jnp.where(
-            lane >= TILE - SLOT, pltpu.roll(following, TILE - SLOT, 1), pltpu.roll(here, TILE - SLOT, 1)
-        )
-        x_down = jnp.where(lane < SLOT, pltpu.roll(previous, SLOT, 1), pltpu.roll(here, SLOT, 1))
-        z_up = jnp.where(open_up, edge[g], pltpu.roll(here, TILE - 1, 1))
-        z_down = jnp.where(open_low, edge[g], pltpu.roll(here, 1, 1))
-        return x_up, x_down, y_up(here), y_down(here), z_up, z_down
-
-    edge[...] = jnp.zeros_like(edge)
-    gather_edge(vol)
-    zero = jnp.zeros((ROWS_Y, TILE), jnp.float32)
+    def strip_sides(strips, edge, g, t):
+        here = tile(strips, strip_base(g), t)
+        following = tile(strips, strip_base(min(g + 1, GROUPS - 1)), t)
+        previous = tile(strips, strip_base(max(g - 1, 0)), t)
+        x_up = pltpu.roll(jnp.where(lane < SLOT, following, here), TILE - SLOT, 1)
+        x_down = pltpu.roll(jnp.where(lane >= TILE - SLOT, previous, here), SLOT, 1)
+        beyond = tile(edge, strip_base(g), t)
+        z_up = jnp.where(open_up, beyond, pltpu.roll(here, TILE - 1, 1))
+        z_down = jnp.where(open_low, beyond, pltpu.roll(here, 1, 1))
+        y_up = tile(strips, strip_base(g), t, 1)
+        y_down = tile(strips, strip_base(g), t, -1)
+        return x_up, x_down, y_up, y_down, z_up, z_down
+
+    def volume_edge(x):
+        start, where = place(x)
+        for t in row_tiles:
+            to_edge(edge_a, start, t, where, tile(vol, base(x), t))
+
+    loop(1, EXT - 1, volume_edge, 4)
     center = 0.5 * (UPPER_BOUND + LOWER_BOUND)
     halfwidth = 0.5 * (UPPER_BOUND - LOWER_BOUND)
     spread = center / halfwidth
     damping = 1.0 / spread
-    for ref in (sa, sb):
-        put(ref, 0, zero)
-        put(ref, EXT - 1, zero)
-    put(ax, 0, jnp.minimum(main(vol, 0), main(vol, 1)))
+    for t in row_tiles:
+        for ref in (sa, sb):
+            put(ref, 0, t, guard)
+            put(ref, (EXT - 1) * ROWS_Y, t, guard)
+        put(ax, 0, t, jnp.minimum(tile(vol, 0, t), tile(vol, ROWS_Y, t)))
+    put(ay, ROWS_Y - 8, 0, guard)
 
     def inverse_of(value):
         return jnp.where(value > 0.0, 1.0 / jnp.where(value > 0.0, value, 1.0), 0.0)
 
-    def prepare(x, carry):
-        v = main(vol, x)
-        upper = jnp.minimum(v, main(vol, x + 1))
-        z_up, z_down = z_sides(v, strip_value(hvol, x))
-        z_up = jnp.where((lane == TILE - 1) & (lane != up_lane), 0.0, z_up)
-        z_down = jnp.where((lane == 0) & (lane != low_lane), 0.0, z_down)
-        parts = [jnp.minimum(v, n) for n in (y_up(v), y_down(v), z_up, z_down)]
-        whole = SHIFT_WEIGHT * v + upper + main(ax, x - 1) + parts[0] + parts[1] + parts[2] + parts[3]
-        scale = inverse_of(whole)
-        put(ax, x, upper)
-        for ref, value in zip((ayu, ayl, azu, azl, diag, inv), parts + [whole, scale]):
-            put(ref, x, value)
-        search = (main(res, x) * scale) * (1.0 / center)
-        put(sa, x, search)
-        put(total, x, search)
-        return carry
-
-    lax.fori_loop(1, EXT - 1, prepare, 0)
+    closed_up = (lane == TILE - 1) & (lane != up_lane)
+    closed_low = (lane == 0) & (lane != low_lane)
+
+    def prepare(x):
+        here = base(x)
+        start, where = place(x)
+        for t in row_tiles:
+            v = tile(vol, here, t)
+            upper = jnp.minimum(v, tile(vol, here + ROWS_Y, t))
+            lower = jnp.minimum(v, tile(vol, here - ROWS_Y, t))
+            z_up, z_down = z_sides(v, hvol, start, t, where)
+            z_up = jnp.minimum(v, jnp.where(closed_up, 0.0, z_up))
+            z_down = jnp.minimum(v, jnp.where(closed_low, 0.0, z_down))
+            y_up = jnp.minimum(v, tile(vol, here, t, 1))
+            y_down = jnp.minimum(v, tile(vol, here, t, -1))
+            whole = SHIFT_WEIGHT * v + (upper + lower) + (y_up + y_down) + (z_up + z_down)
+            scale = inverse_of(whole)
+            for ref, value in ((ax, upper), (ay, y_up), (azu, z_up), (azl, z_down), (diag, whole), (inv, scale)):
+                put(ref, here, t, value)
+            search = (tile(res, here, t) * scale) * (1.0 / center)
+            put(sa, here, t, search)
+            put(total, here, t, search)
+            to_edge(edge_b, start, t, where, search)
+
+    loop(1, EXT - 1, prepare, 2)
     for g in range(GROUPS):
-        v = hvol[g]
-        parts = [jnp.minimum(v, n) for n in strip_sides(hvol, g)]
-        whole = SHIFT_WEIGHT * v
-        for value in parts:
-            whole = whole + value
-        scale = inverse_of(whole)
-        for i, value in enumerate(parts + [whole, scale]):
-            hcoef[i, g] = value
-        search = (hres[g] * scale) * (1.0 / center)
-        hsa[g] = search
-        htotal[g] = search
+        for t in row_tiles:
+            v = tile(hvol, strip_base(g), t)
+            parts = [jnp.minimum(v, n) for n in strip_sides(hvol, edge_a, g, t)]
+            whole = SHIFT_WEIGHT * v
+            for value in parts:
+                whole = whole + value
+            scale = inverse_of(whole)
+            for i, value in enumerate(parts + [whole, scale]):
+                hcoef[i, g * ROWS_Y + 8 * t : g * ROWS_Y + 8 * t + 8, :] = value
+            search = (tile(hres, strip_base(g), t) * scale) * (1.0 / center)
+            put(hsa, strip_base(g), t, search)
+            put(htotal, strip_base(g), t, search)
 
     now, then, hnow, hthen = sa, sb, hsa, hsb
+    edge, edge_next = edge_b, edge_a
     for iteration in range(ITERS - 1):
         damping_next = 1.0 / (2.0 * spread - damping)
         keep = damping_next * damping
         push = 2.0 * damping_next / halfwidth
         damping = damping_next
-        gather_edge(now)
-
-        def iterate(x, carry, now=now, then=then, hnow=hnow, keep=keep, push=push):
-            s = main(now, x)
-            z_up, z_down = z_sides(s, strip_value(hnow, x))
-            flow = main(ax, x) * main(now, x + 1) + main(ax, x - 1) * main(now, x - 1)
-            flow = flow + (main(ayu, x) * y_up(s) + main(ayl, x) * y_down(s))
-            flow = flow + (main(azu, x) * z_up + main(azl, x) * z_down)
-            residual = main(res, x) - (main(diag, x) * s - flow)
-            put(res, x, residual)
-            search = keep * s + push * (residual * main(inv, x))
-            put(then, x, search)
-            put(total, x, main(total, x) + search)
-            return carry
-
-        lax.fori_loop(1, EXT - 1, iterate, 0)
+
+        def iterate(x, now=now, then=then, hnow=hnow, edge_next=edge_next, keep=keep, push=push):
+            here = base(x)
+            start, where = place(x)
+            for t in row_tiles:
+                s = tile(now, here, t)
+                z_up, z_down = z_sides(s, hnow, start, t, where)
+                along_x = tile(ax, here, t) * tile(now, here + ROWS_Y, t)
+                along_x = along_x + tile(ax, here - ROWS_Y, t) * tile(now, here - ROWS_Y, t)
+                along_y = tile(ay, here, t) * tile(now, here, t, 1)
+                along_y = along_y + tile(ay, here, t, -1) * tile(now, here, t, -1)
+                along_z = tile(azu, here, t) * z_up + tile(azl, here, t) * z_down
+                flow = along_x + along_y + along_z
+                residual = tile(res, here, t) - (tile(diag, here, t) * s - flow)
+                put(res, here, t, residual)
+                search = keep * s + push * (residual * tile(inv, here, t))
+                put(then, here, t, search)
+                put(total, here, t, tile(total, here, t) + search)
+                if edge_next is not None:
+                    to_edge(edge_next, start, t, where, search)
+
+        if iteration == ITERS - 2:
+            iterate = functools.partial(iterate, edge_next=None)
+        loop(1, EXT - 1, iterate, 2)
         for g in range(GROUPS):
-            s = hnow[g]
-            flow = zero
-            for i, value in enumerate(strip_sides(hnow, g)):
-                flow = flow + hcoef[i, g] * value
-            residual = hres[g] - (hcoef[6, g] * s - flow)
-            hres[g] = residual
-            search = keep * s + push * (residual * hcoef[7, g])
-            hthen[g] = search
-            htotal[g] = htotal[g] + search
+            for t in row_tiles:
+                rows_here = slice(g * ROWS_Y + 8 * t, g * ROWS_Y + 8 * t + 8)
+                s = tile(hnow, strip_base(g), t)
+                parts = [hcoef[i, rows_here, :] * v for i, v in enumerate(strip_sides(hnow, edge, g, t))]
+                flow = (parts[0] + parts[1]) + (parts[2] + parts[3]) + (parts[4] + parts[5])
+                residual = tile(hres, strip_base(g), t) - (hcoef[6, rows_here, :] * s - flow)
+                put(hres, strip_base(g), t, residual)
+                search = keep * s + push * (residual * hcoef[7, rows_here, :])
+                put(hthen, strip_base(g), t, search)
+                put(htotal, strip_base(g), t, tile(htotal, strip_base(g), t) + search)
         now, then, hnow, hthen = then, now, hthen, hnow
+        edge, edge_next = edge_next, edge
 
     lanes = lane_index()
 
@@ -599,19 +646,17 @@
                 value = piece if value is None else jnp.where(lanes < BOX * (r + 1), piece, value)
             packed[pl.ds(pl.multiple_of(k * RETURN_ROWS + row, 8), TILES), :] = value
 
-    def core(i, carry):
-        base = (i + HALO - 1) * ROWS_Y + SIDE
-        pieces = [total[pl.ds(base + r, TILES, stride=PER_TILE), :] for r in range(PER_TILE)]
+    def core(i):
+        start = (i + HALO - 1) * ROWS_Y + SIDE
+        pieces = [total[pl.ds(start + r, TILES, stride=PER_TILE), :] for r in range(PER_TILE)]
         spread_boxes(pieces, i * TILES)
-        return carry
-
-    lax.fori_loop(0, PADDED, core, 0)
-
-    def output(i, carry):
-        pressure[i] = total[pl.ds(pl.multiple_of((i + HALO) * ROWS_Y + SIDE, 8), BOX), :]
-        return carry
-
-    lax.fori_loop(0, BOX, output, 0)
+
+    loop(0, PADDED, core, 2)
+
+    def output(i):
+        pressure[i] = total[pl.ds(base(i + HALO) + SIDE, BOX), :]
+
+    loop(0, BOX, output, 4)
     for f, y in enumerate((SIDE - 1, SIDE + BOX)):
         pieces = [
             total[pl.ds((HALO + r) * ROWS_Y + y, TILES, stride=PER_TILE * ROWS_Y), :]
@@ -624,9 +669,12 @@
             (2 * TILES, TILE), jnp.float32
         )
     for block in range(TILES):
-        for r in range(PER_TILE):
-            start = (HALO + PER_TILE * block + r) * ROWS_Y + SIDE
-            turned[r * BOX : (r + 1) * BOX, :] = total[start : start + BOX, :]
+        for i in range(PER_TILE):
+            for r in range(PER_TILE):
+                start = (HALO + PER_TILE * block + i) * ROWS_Y + SIDE + r
+                turned[BOX * r + TILES * i : BOX * r + TILES * (i + 1), :] = total[
+                    pl.ds(start, TILES, stride=PER_TILE), :
+                ]
         flat = turned[...].T
         for k in range(count):
             low = k * RETURN_ROWS + z_row + block
@@ -639,15 +687,17 @@
     box = jnp.where(at_top, count - 1, 0)
     target = box * RETURN_ROWS + z_row + jnp.where(at_top, TILES, 0)
     for g in range(1, GROUPS - 1):
-        turned[0:BOX, :] = htotal[g, SIDE : SIDE + BOX]
-        turned[BOX:TILE, :] = jnp.zeros((TILE - BOX, TILE), jnp.float32)
-        flat = turned[...].T
-        turned[...] = flat
+        turned[...] = jnp.zeros_like(turned)
+        for r in range(PER_TILE):
+            turned[BOX * r : BOX * r + TILES, :] = htotal[
+                pl.ds(strip_base(g) + SIDE + r, TILES, stride=PER_TILE), :
+            ]
+        turned[...] = turned[...].T
         value = None
-        for r in range(PER_TILE):
-            piece = turned[pl.ds(SLOT * r + slot_lane, half, stride=SLOT * PER_TILE), :]
-            piece = pltpu.roll(piece, BOX * r, 1) if r else piece
-            value = piece if value is None else jnp.where(row4 // BOX == r, piece, value)
+        for i in range(PER_TILE):
+            piece = turned[pl.ds(SLOT * i + slot_lane, half, stride=SLOT * PER_TILE), :]
+            piece = pltpu.roll(piece, TILES * i, 1) if i else piece
+            value = piece if value is None else jnp.where(row4 % BOX // TILES == i, piece, value)
         packed[pl.ds(target + (g - 1) * half, half), :] = value
     copies = [
         pltpu.make_async_copy(
@@ -665,24 +715,33 @@
 
 def assemble_call(table, side, recv):
     count = table.shape[0]
+    fixed = [
+        (HALO * BOX, TILE),
+        (HALO * BOX, TILE),
+        (BOX // GROUP, BOX, TILE),
+        (BOX, TILE),
+        (BOX, TILE),
+    ]
+
+    def box_spec(k):
+        return pl.BlockSpec((1, STEP_BRICK * TILES, TILE), lambda i, table, side: (table[k], i, 0))
+
+    def fixed_spec(shape):
+        return pl.BlockSpec(shape, lambda i, table, side: (0,) * len(shape))
+
     return pl.pallas_call(
         functools.partial(assemble_kernel, count=count),
-        in_specs=[SMEM_SPEC, SMEM_SPEC, ANY_SPEC],
-        out_specs=[VMEM_SPEC] * 6,
-        out_shape=[
-            struct(BOX * BOX, TILE),
-            struct(HALO * BOX, TILE),
-            struct(HALO * BOX, TILE),
-            struct(BOX // GROUP, BOX, TILE),
-            struct(BOX, TILE),
-            struct(BOX, TILE),
-        ],
-        scratch_shapes=[
-            pltpu.VMEM((count, ROWS, TILE), jnp.float32),
-            pltpu.SemaphoreType.DMA((count,)),
-        ],
+        grid_spec=pltpu.PrefetchScalarGridSpec(
+            num_scalar_prefetch=2,
+            grid=(BOX // STEP_BRICK,),
+            in_specs=[box_spec(k) for k in range(count)],
+            out_specs=[pl.BlockSpec((STEP_BRICK * BOX, TILE), lambda i, table, side: (i, 0))]
+            + [fixed_spec(shape) for shape in fixed],
+        ),
+        out_shape=[struct(BOX * BOX, TILE)] + [struct(*shape) for shape in fixed],
+        compiler_params=pltpu.CompilerParams(vmem_limit_bytes=6 << 20),
         name="brick",
-    )(table, side, recv)
+    )(table, side, *([recv] * count))
 
 
 def halo(parts):
@@ -712,21 +771,21 @@
 def solve_call(box_of_row, side, count, volume, source):
     lanes_by = box_of_row.shape[0]
     wide = pltpu.VMEM((EXT * ROWS_Y, TILE), jnp.float32)
-    narrow = pltpu.VMEM((GROUPS, ROWS_Y, TILE), jnp.float32)
+    narrow = pltpu.VMEM((GROUPS * ROWS_Y + 16, TILE), jnp.float32)
     return pl.pallas_call(
         functools.partial(solve_kernel, count=count, lanes_by=lanes_by),
         in_specs=[SMEM_SPEC, SMEM_SPEC] + [VMEM_SPEC] * 16,
-        out_specs=[VMEM_SPEC, ANY_SPEC],
+        out_specs=[VMEM_SPEC, HBM_SPEC],
         out_shape=[struct(BOX, BOX, count * BOX), struct(lanes_by, RETURN_ROWS, TILE)],
-        scratch_shapes=[wide] * 12
-        + [narrow] * 5
+        scratch_shapes=[wide] * 11
+        + [narrow] * 7
         + [
-            pltpu.VMEM((8, GROUPS, ROWS_Y, TILE), jnp.float32),
-            narrow,
+            pltpu.VMEM((8, GROUPS * ROWS_Y, TILE), jnp.float32),
             pltpu.VMEM((TILE, TILE), jnp.float32),
             pltpu.VMEM((count * RETURN_ROWS, TILE), jnp.float32),
             pltpu.SemaphoreType.DMA((lanes_by,)),
         ],
+        compiler_params=pltpu.CompilerParams(vmem_limit_bytes=26 << 20),
         name="solve",
     )(box_of_row, side, *volume, *source)
 
@@ -771,9 +830,10 @@
     updated, apertures = update_call(masses, planes)
     side = lax.axis_index("bz").reshape(1)
     volume = halo(assemble_call(brick_table, side, volume_recv))
+    source_recv, volume = lax.optimization_barrier((source_recv, volume))
     source = halo(assemble_call(brick_table, side, source_recv))
     pressure, rows = solve_call(box_of_row, side, placement.shape[3], volume, source)
-    returned = exchange(rows)
+    returned = exchange(pltpu.with_memory_space_constraint(rows, pltpu.HBM))
     corrected = correct_call(slot_row, updated, apertures, returned)
     return (jnp.swapaxes(corrected, 0, 1), pressure)
 

time: 227 us -> 202 us (0.89)
  Pallas kernels: 134 us -> 104 us
  waiting for transfers between devices: 13.8 us -> 21 us
    pallas_call x1, Pallas kernels: 37 us -> 19.9 us  [solve_call(): pl.pallas_call(functools.partial(solve_kernel, count=count, lanes_by=lane...]
    pallas_call x2, Pallas kernels: 15.3 us -> 3.27 us  [assemble_call(): pl.pallas_call(functools.partial(assemble_kernel, count=count), grid_spec...]
    ppermute x2, waiting for transfers between devices: 0.01 us -> 9.31 us  [halo(): x_hi = lax.ppermute(first, 'bx', down)]
    ppermute x2, starting transfers between devices: 9.66 us -> 4.05 us  [halo(): y_hi = lax.ppermute(edge(0), 'by', [(j, i) for i, j in y_up])]
    all_to_all x3, waiting for transfers between devices: 8.27 us -> 3.14 us  [exchange(): return lax.all_to_all(rows, 'by', split_axis=0, concat_axis=0, tiled=True)]
    ppermute x2, starting transfers between devices: 3.84 us -> 7.63 us  [halo(): y_lo = lax.ppermute(edge(BOX - SIDE), 'by', y_up)]
    ppermute x2, waiting for transfers between devices: 1.34 us -> 4.49 us  [halo(): y_hi = lax.ppermute(edge(0), 'by', [(j, i) for i, j in y_up])]
    unnamed x49 -> x19, local copies, waits for them, and re-layouts: 7.67 us -> 8.31 us
  transfers between devices with their start and end apart: 17 -> 17, of which waited for: 5 -> 7; matrix products, arithmetic and copies ran while one was open for 2% -> 2% of each run, Pallas kernels for 34% -> 31%
where the time goes in v2:
time: 202 us; the launch traced here: 201 us
  Pallas kernels  104 us (51%)
  starting transfers between devices  63.4 us (31%)
  waiting for transfers between devices  21 us (10%)
  local copies, waits for them, and re-layouts  9.35 us (5%)
    pallas_call x1, Pallas kernels, update_call(): pl.pallas_call(update_kernel, in_specs=[VMEM_SPEC, VMEM_SPEC], out_specs=...  37 us
    all_to_all x3, starting transfers between devices, exchange(): return lax.all_to_all(rows, 'by', split_axis=0, concat_axis=0, tiled=True)  27.2 us
    pallas_call x1, Pallas kernels, flux_call(): pl.pallas_call(functools.partial(flux_kernel, lanes_by=lanes_by), in_spec...  24 us
    pallas_call x1, Pallas kernels, solve_call(): pl.pallas_call(functools.partial(solve_kernel, count=count, lanes_by=lane...  19.9 us
    pallas_call x1, Pallas kernels, volume_call(): pl.pallas_call(functools.partial(volume_kernel, lanes_by=lanes_by), in_sp...  10.3 us
    pallas_call x1, Pallas kernels, correct_call(): pl.pallas_call(correct_kernel, grid=(BOX // STEP_X,), in_specs=[SMEM_SPEC...  9.95 us
    ppermute x2, waiting for transfers between devices, halo(): x_hi = lax.ppermute(first, 'bx', down)  9.31 us
    unnamed x19, local copies, waits for them, and re-layouts  8.31 us
  transfers between devices with their start and end apart: 17, of which 7 were waited for; matrix products, arithmetic and copies ran while one was open for 2% of the time, Pallas kernels for 31%

profile of v2, /device:TPU:98, one launch (start us, length us, event | category | flops | bytes accessed | tf_op | source)
XLA Modules:
  0.0 200.9 jit_solution(14001792742874683206)
XLA Ops:
  0.6 0.8 copy.9
  1.4 0.1 reshape_squeeze.3
  1.5 0.1 fusion
  1.6 0.1 reduce_window_sum.11
  1.7 0.2 select_reduce_fusion
  1.8 0.1 reshape.65
  1.9 0.1 copy.10
  2.0 1.2 select_reduce_fusion.3.slots
  3.2 10.3 %volume_rows.1 = (f32[34,8,1280]{2,1,0:T(8,128)}, f32[16,256,128]{2,1,0:T(8,128)}) custom-call(s32[16]{0:T(128)} %select_reduce_fusion.3.slots, s32[8,39304]{1,0:T(8,128)} %fraction.1), custom_call_target="tpu_custom_call" | custom-call | tf_op jit(solution)/shard_map/volume_rows/pallas_call | solution.py:311
  13.6 7.5 %all-to-all-start.1 = ((f32[16,256,128]{2,1,0:T(8,128)}), f32[16,256,128]{2,1,0:T(8,128)S(1)}, u32[]{:S(2)}, u32[]{:S(2)}) async-start(f32[16,256,128]{2,1,0:T(8,128)} %get-tuple-element.36), calls=%async_computation.1 | async-start | bytes 4194304 | tf_op jit(solution)/shard_map/all_to_all | solution.py:821
  21.1 24.0 %flux_rows.1 = (f32[34,3,8,1280]{3,2,1,0:T(8,128)}, f32[16,256,128]{2,1,0:T(8,128)}) custom-call(s32[16]{0:T(128)} %select_reduce_fusion.3.slots, f32[3,8,39304]{2,1,0:T(8,128)} %bitcast.29, f32[34,8,1280]{2,1,0:T(8,128)} %get-tuple-element.31.planes), custom_call_target="tpu_custom_call" | custom-call | tf_op jit(solution)/shard_map/flux_rows/pallas_call | solution.py:327
  45.0 0.0 copy-start.3
  45.1 3.1 %all-to-all-done.1.refs_0_.refs_1_.refs_2_.refs_3_ = f32[16,256,128]{2,1,0:T(8,128)S(1)} async-done(((f32[16,256,128]{2,1,0:T(8,128)}), f32[16,256,128]{2,1,0:T(8,128)S(1)}, u32[]{:S(2)}, u32[]{:S(2)}) %all-to-all-start.1) | async-done | bytes 2097184 | tf_op jit(solution)/shard_map/all_to_all | solution.py:821
  48.2 0.0 copy-start
  48.2 1.3 copy-done
  49.5 8.3 %all-to-all-start = ((f32[16,256,128]{2,1,0:T(8,128)}), f32[16,256,128]{2,1,0:T(8,128)S(1)}, u32[]{:S(2)}, u32[]{:S(2)}) async-start(f32[16,256,128]{2,1,0:T(8,128)} %get-tuple-element.35), calls=%async_computation | async-start | bytes 4194304 | tf_op jit(solution)/shard_map/all_to_all | solution.py:821
  57.8 0.0 copy-done.3
  57.8 0.2 dynamic-slice_reduce_fusion.table
  58.0 1.6 copy-done.1
  59.6 1.6 brick.2
  61.2 5.0 %collective-permute-start = (f32[160,128]{1,0:T(8,128)S(1)}, f32[160,128]{1,0:T(8,128)S(1)}, u32[]{:S(2)}, u32[]{:S(2)}) collective-permute-start(f32[160,128]{1,0:T(8,128)S(1)} %get-tuple-element.38), channel_id=1, source_target_pairs={{0,32},{32,64},{64,96},{96,128},{128,160},{160,192},{192,224},{1,3... | collective-permute-start | bytes 245768 | tf_op jit(solution)/shard_map/ppermute | solution.py:756
  66.2 1.9 collective-permute-start.3
  68.2 3.6 %collective-permute-start.4 = (f32[32,128]{1,0:T(8,128)S(1)}, f32[32,128]{1,0:T(8,128)S(1)}, u32[]{:S(2)}, u32[]{:S(2)}) collective-permute-start(f32[32,128]{1,0:T(8,128)S(1)} %get-tuple-element.42), channel_id=1, source_target_pairs={{32,1},{33,0},{64,33},{65,32},{96,65},{97,64},{128,97},{129,96},{1... | collective-permute-start | bytes 49160 | tf_op jit(solution)/shard_map/ppermute | solution.py:759
  71.8 0.1 collective-permute-start.2
  71.9 2.3 %collective-permute-start.1 = (f32[160,128]{1,0:T(8,128)S(1)}, f32[160,128]{1,0:T(8,128)S(1)}, u32[]{:S(2)}, u32[]{:S(2)}) collective-permute-start(f32[160,128]{1,0:T(8,128)S(1)} %get-tuple-element.39), channel_id=1, source_target_pairs={{32,0},{64,32},{96,64},{128,96},{160,128},{192,160},{224,192},{33,... | collective-permute-start | bytes 245768 | tf_op jit(solution)/shard_map/ppermute | solution.py:757
  74.2 0.0 collective-permute-done.refs_1_
  74.2 0.6 constant_dynamic-update-slice_fusion.9
  74.8 0.7 slice_dynamic-update-slice_fusion.2
  75.5 4.3 %collective-permute-done.1.refs_2_ = f32[160,128]{1,0:T(8,128)S(1)} collective-permute-done((f32[160,128]{1,0:T(8,128)S(1)}, f32[160,128]{1,0:T(8,128)S(1)}, u32[]{:S(2)}, u32[]{:S(2)}) %collective-permute-start.1) | collective-permute-done | bytes 81952 | tf_op jit(solution)/shard_map/ppermute | solution.py:757
  79.9 0.6 constant_dynamic-update-slice_fusion.8
  80.5 0.0 collective-permute-done.3.refs_4_
  80.5 0.6 constant_dynamic-update-slice_fusion.7
  81.1 0.0 collective-permute-done.2.refs_3_
  81.1 0.6 constant_dynamic-update-slice_fusion.6
  81.7 0.0 collective-permute-done.4.refs_5_
  81.7 0.6 constant_dynamic-update-slice_fusion.5
  82.3 2.1 %collective-permute-start.6 = (f32[46,8,128]{2,1,0:T(8,128)S(1)}, f32[46,8,128]{2,1,0:T(8,128)S(1)}, u32[]{:S(2)}, u32[]{:S(2)}) collective-permute-start(f32[46,8,128]{2,1,0:T(8,128)S(1)} %get-tuple-element.80), channel_id=1, source_target_pairs={{2,0},{4,2},{6,4},{8,6},{10,8},{12,10},{14,12},{16,14},{18,16},{20... | collective-permute-start | bytes 565256 | tf_op jit(solution)/shard_map/ppermute | solution.py:767
  84.4 3.7 %collective-permute-start.5 = (f32[46,8,128]{2,1,0:T(8,128)}, f32[46,8,128]{2,1,0:T(8,128)S(1)}, u32[]{:S(2)}, u32[]{:S(2)}) collective-permute-start(f32[46,8,128]{2,1,0:T(8,128)} %get-tuple-element.81), channel_id=1, source_target_pairs={{0,2},{2,4},{4,6},{6,8},{8,10},{10,12},{12,14},{14,16},{16,18},{18... | collective-permute-start | bytes 565256 | tf_op jit(solution)/shard_map/ppermute | solution.py:766
  88.1 0.0 all-to-all-done.refs_0_.refs_1_.refs_2_.refs_3_
  88.1 2.3 %collective-permute-done.6.refs_7_ = f32[46,8,128]{2,1,0:T(8,128)S(1)} collective-permute-done((f32[46,8,128]{2,1,0:T(8,128)S(1)}, f32[46,8,128]{2,1,0:T(8,128)S(1)}, u32[]{:S(2)}, u32[]{:S(2)}) %collective-permute-start.6) | collective-permute-done | bytes 188448 | tf_op jit(solution)/shard_map/ppermute | solution.py:767
  90.4 2.1 %collective-permute-done.5.refs_6_ = f32[46,8,128]{2,1,0:T(8,128)S(1)} collective-permute-done((f32[46,8,128]{2,1,0:T(8,128)}, f32[46,8,128]{2,1,0:T(8,128)S(1)}, u32[]{:S(2)}, u32[]{:S(2)}) %collective-permute-start.5) | collective-permute-done | bytes 188448 | tf_op jit(solution)/shard_map/ppermute | solution.py:766
  92.5 1.6 brick.3
  94.2 2.9 %collective-permute-start.7 = (f32[160,128]{1,0:T(8,128)S(1)}, f32[160,128]{1,0:T(8,128)S(1)}, u32[]{:S(2)}, u32[]{:S(2)}) collective-permute-start(f32[160,128]{1,0:T(8,128)S(1)} %get-tuple-element.53), channel_id=1, source_target_pairs={{0,32},{32,64},{64,96},{96,128},{128,160},{160,192},{192,224},{1,3... | collective-permute-start | bytes 245768 | tf_op jit(solution)/shard_map/ppermute | solution.py:756
  97.1 1.9 collective-permute-start.10
  99.1 3.6 %collective-permute-start.11 = (f32[32,128]{1,0:T(8,128)S(1)}, f32[32,128]{1,0:T(8,128)S(1)}, u32[]{:S(2)}, u32[]{:S(2)}) collective-permute-start(f32[32,128]{1,0:T(8,128)S(1)} %get-tuple-element.57), channel_id=1, source_target_pairs={{32,1},{33,0},{64,33},{65,32},{96,65},{97,64},{128,97},{129,96},{1... | collective-permute-start | bytes 49160 | tf_op jit(solution)/shard_map/ppermute | solution.py:759
  102.7 0.1 collective-permute-start.9
  102.8 2.9 %collective-permute-start.8 = (f32[160,128]{1,0:T(8,128)S(1)}, f32[160,128]{1,0:T(8,128)S(1)}, u32[]{:S(2)}, u32[]{:S(2)}) collective-permute-start(f32[160,128]{1,0:T(8,128)S(1)} %get-tuple-element.54), channel_id=1, source_target_pairs={{32,0},{64,32},{96,64},{128,96},{160,128},{192,160},{224,192},{33,... | collective-permute-start | bytes 245768 | tf_op jit(solution)/shard_map/ppermute | solution.py:757
  105.7 0.0 collective-permute-done.7.refs_9_
  105.8 5.0 %collective-permute-done.8.refs_10_ = f32[160,128]{1,0:T(8,128)S(1)} collective-permute-done((f32[160,128]{1,0:T(8,128)S(1)}, f32[160,128]{1,0:T(8,128)S(1)}, u32[]{:S(2)}, u32[]{:S(2)}) %collective-permute-start.8) | collective-permute-done | bytes 81952 | tf_op jit(solution)/shard_map/ppermute | solution.py:757
  110.7 0.0 collective-permute-done.10.refs_12_
  110.8 0.0 collective-permute-done.9.refs_11_
  110.8 0.0 collective-permute-done.11.refs_13_
  110.8 1.9 collective-permute-start.13
  112.7 3.9 %collective-permute-start.12 = (f32[46,8,128]{2,1,0:T(8,128)S(1)}, f32[46,8,128]{2,1,0:T(8,128)S(1)}, u32[]{:S(2)}, u32[]{:S(2)}) collective-permute-start(f32[46,8,128]{2,1,0:T(8,128)S(1)} %get-tuple-element.77), channel_id=1, source_target_pairs={{0,2},{2,4},{4,6},{6,8},{8,10},{10,12},{12,14},{14,16},{16,18},{18... | collective-permute-start | bytes 565256 | tf_op jit(solution)/shard_map/ppermute | solution.py:766
  116.7 0.1 select_reduce_fusion.2.box_of_row
  116.7 2.2 %collective-permute-done.13.refs_15_ = f32[46,8,128]{2,1,0:T(8,128)S(1)} collective-permute-done((f32[46,8,128]{2,1,0:T(8,128)S(1)}, f32[46,8,128]{2,1,0:T(8,128)S(1)}, u32[]{:S(2)}, u32[]{:S(2)}) %collective-permute-start.13) | collective-permute-done | bytes 188448 | tf_op jit(solution)/shard_map/ppermute | solution.py:767
  119.0 1.9 collective-permute-done.12.refs_14_
  120.9 19.9 %solve.1 = (f32[32,32,128]{2,1,0:T(8,128)}, f32[16,304,128]{2,1,0:T(8,128)}) custom-call(s32[16]{0:T(128)S(1)} %select_reduce_fusion.2.box_of_row, s32[1]{0:T(128)} %bitcast.2.side, f32[1024,128]{1,0:T(8,128)S(1)} %get-tuple-element.43.refs_0_, f32[160,128]{1,0:T(8,128)S(1)} %collective-permute-done.refs_1_, f32[160,128]{1,0:T(8,128)S(1)} %collective-permute-done.1.refs_2_, ...), custom_call_target="tpu_custom_call" | custom-call | tf_op jit(solution)/shard_map/solve/pallas_call | solution.py:775
  140.8 11.5 %all-to-all-start.2 = ((f32[16,304,128]{2,1,0:T(8,128)}), f32[16,304,128]{2,1,0:T(8,128)S(1)}, u32[]{:S(2)}, u32[]{:S(2)}) async-start(f32[16,304,128]{2,1,0:T(8,128)} %get-tuple-element.58), calls=%async_computation.2 | async-start | bytes 4980736 | tf_op jit(solution)/shard_map/all_to_all | solution.py:821
  152.3 37.0 %updated.1 = (f32[32,3,8,1024]{3,2,1,0:T(8,128)}, f32[32,6,8,1024]{3,2,1,0:T(8,128)}) custom-call(f32[34,3,8,1280]{3,2,1,0:T(8,128)} %get-tuple-element.32.masses, f32[34,8,1280]{2,1,0:T(8,128)} %get-tuple-element.31.planes), custom_call_target="tpu_custom_call" | custom-call | tf_op jit(solution)/shard_map/updated/pallas_call | solution.py:344
  189.3 0.1 select_reduce_fusion.1.rows
  189.5 0.0 all-to-all-done.2.returned
  189.5 1.5 copy-done.2
  191.0 10.0 %corrected.1 = f32[3,8,32768]{2,1,0:T(8,128)} custom-call(s32[8]{0:T(128)S(1)} %select_reduce_fusion.1.rows, f32[32,3,8,1024]{3,2,1,0:T(8,128)} %get-tuple-element.33.updated, f32[32,6,8,1024]{3,2,1,0:T(8,128)} %get-tuple-element.34.apertures, f32[16,304,128]{2,1,0:T(8,128)} %copy-done.2), custom_call_target="tpu_custom_call" | custom-call | tf_op jit(solution)/shard_map/corrected/pallas_call | solution.py:354
  (10 shorter events, 0.0 us)
Async XLA Ops:
  13.6 34.6 %all-to-all-start.1 = ((f32[16,256,128]{2,1,0:T(8,128)}), f32[16,256,128]{2,1,0:T(8,128)S(1)}, u32[]{:S(2)}, u32[]{:S(2)}) async-start(f32[16,256,128]{2,1,0:T(8,128)} %get-tuple-element.36), calls=%async_computation.1 | async-start | bytes 4194304 | tf_op jit(solution)/shard_map/all_to_all | solution.py:821
  45.0 12.7 %copy-start.3 = (s32[1,16,1,4]{1,3,2,0:T(4,128)S(1)}, s32[1,16,1,4]{1,3,2,0:T(4,128)}, u32[]{:S(2)}) copy-start(s32[1,16,1,4]{1,3,2,0:T(4,128)} %param.5) | copy-start | bytes 772
  48.2 1.3 copy-start
  49.5 38.6 %all-to-all-start = ((f32[16,256,128]{2,1,0:T(8,128)}), f32[16,256,128]{2,1,0:T(8,128)S(1)}, u32[]{:S(2)}, u32[]{:S(2)}) async-start(f32[16,256,128]{2,1,0:T(8,128)} %get-tuple-element.35), calls=%async_computation | async-start | bytes 4194304 | tf_op jit(solution)/shard_map/all_to_all | solution.py:821
  58.0 1.6 copy-start.1
  61.2 13.0 %collective-permute-start = (f32[160,128]{1,0:T(8,128)S(1)}, f32[160,128]{1,0:T(8,128)S(1)}, u32[]{:S(2)}, u32[]{:S(2)}) collective-permute-start(f32[160,128]{1,0:T(8,128)S(1)} %get-tuple-element.38), channel_id=1, source_target_pairs={{0,32},{32,64},{64,96},{96,128},{128,160},{160,192},{192,224},{1,3... | collective-permute-start | bytes 245768 | tf_op jit(solution)/shard_map/ppermute | solution.py:756
  66.2 14.2 %collective-permute-start.3 = (f32[32,128]{1,0:T(8,128)S(1)}, f32[32,128]{1,0:T(8,128)S(1)}, u32[]{:S(2)}, u32[]{:S(2)}) collective-permute-start(f32[32,128]{1,0:T(8,128)S(1)} %get-tuple-element.41), channel_id=1, source_target_pairs={{0,33},{1,32},{32,65},{33,64},{64,97},{65,96},{96,129},{97,128},{1... | collective-permute-start | bytes 49160 | tf_op jit(solution)/shard_map/ppermute | solution.py:758
  68.2 13.5 %collective-permute-start.4 = (f32[32,128]{1,0:T(8,128)S(1)}, f32[32,128]{1,0:T(8,128)S(1)}, u32[]{:S(2)}, u32[]{:S(2)}) collective-permute-start(f32[32,128]{1,0:T(8,128)S(1)} %get-tuple-element.42), channel_id=1, source_target_pairs={{32,1},{33,0},{64,33},{65,32},{96,65},{97,64},{128,97},{129,96},{1... | collective-permute-start | bytes 49160 | tf_op jit(solution)/shard_map/ppermute | solution.py:759
  71.8 9.2 %collective-permute-start.2 = (f32[2,32,128]{2,1,0:T(8,128)S(1)}, f32[2,32,128]{2,1,0:T(8,128)S(1)}, u32[]{:S(2)}, u32[]{:S(2)}) collective-permute-start(f32[2,32,128]{2,1,0:T(8,128)S(1)} %get-tuple-element.40), channel_id=1, source_target_pairs={{0,1},{1,0},{2,3},{3,2},{4,5},{5,4},{6,7},{7,6},{8,9},{9,8},{10,11... | collective-permute-start | bytes 98312 | tf_op jit(solution)/shard_map/ppermute | solution.py:751
  71.9 7.9 %collective-permute-start.1 = (f32[160,128]{1,0:T(8,128)S(1)}, f32[160,128]{1,0:T(8,128)S(1)}, u32[]{:S(2)}, u32[]{:S(2)}) collective-permute-start(f32[160,128]{1,0:T(8,128)S(1)} %get-tuple-element.39), channel_id=1, source_target_pairs={{32,0},{64,32},{96,64},{128,96},{160,128},{192,160},{224,192},{33,... | collective-permute-start | bytes 245768 | tf_op jit(solution)/shard_map/ppermute | solution.py:757
  82.3 8.1 %collective-permute-start.6 = (f32[46,8,128]{2,1,0:T(8,128)S(1)}, f32[46,8,128]{2,1,0:T(8,128)S(1)}, u32[]{:S(2)}, u32[]{:S(2)}) collective-permute-start(f32[46,8,128]{2,1,0:T(8,128)S(1)} %get-tuple-element.80), channel_id=1, source_target_pairs={{2,0},{4,2},{6,4},{8,6},{10,8},{12,10},{14,12},{16,14},{18,16},{20... | collective-permute-start | bytes 565256 | tf_op jit(solution)/shard_map/ppermute | solution.py:767
  84.4 8.1 %collective-permute-start.5 = (f32[46,8,128]{2,1,0:T(8,128)}, f32[46,8,128]{2,1,0:T(8,128)S(1)}, u32[]{:S(2)}, u32[]{:S(2)}) collective-permute-start(f32[46,8,128]{2,1,0:T(8,128)} %get-tuple-element.81), channel_id=1, source_target_pairs={{0,2},{2,4},{4,6},{6,8},{8,10},{10,12},{12,14},{14,16},{16,18},{18... | collective-permute-start | bytes 565256 | tf_op jit(solution)/shard_map/ppermute | solution.py:766
  94.2 11.5 %collective-permute-start.7 = (f32[160,128]{1,0:T(8,128)S(1)}, f32[160,128]{1,0:T(8,128)S(1)}, u32[]{:S(2)}, u32[]{:S(2)}) collective-permute-start(f32[160,128]{1,0:T(8,128)S(1)} %get-tuple-element.53), channel_id=1, source_target_pairs={{0,32},{32,64},{64,96},{96,128},{128,160},{160,192},{192,224},{1,3... | collective-permute-start | bytes 245768 | tf_op jit(solution)/shard_map/ppermute | solution.py:756
  97.1 13.6 %collective-permute-start.10 = (f32[32,128]{1,0:T(8,128)S(1)}, f32[32,128]{1,0:T(8,128)S(1)}, u32[]{:S(2)}, u32[]{:S(2)}) collective-permute-start(f32[32,128]{1,0:T(8,128)S(1)} %get-tuple-element.56), channel_id=1, source_target_pairs={{0,33},{1,32},{32,65},{33,64},{64,97},{65,96},{96,129},{97,128},{1... | collective-permute-start | bytes 49160 | tf_op jit(solution)/shard_map/ppermute | solution.py:758
  99.1 11.7 %collective-permute-start.11 = (f32[32,128]{1,0:T(8,128)S(1)}, f32[32,128]{1,0:T(8,128)S(1)}, u32[]{:S(2)}, u32[]{:S(2)}) collective-permute-start(f32[32,128]{1,0:T(8,128)S(1)} %get-tuple-element.57), channel_id=1, source_target_pairs={{32,1},{33,0},{64,33},{65,32},{96,65},{97,64},{128,97},{129,96},{1... | collective-permute-start | bytes 49160 | tf_op jit(solution)/shard_map/ppermute | solution.py:759
  102.7 8.1 %collective-permute-start.9 = (f32[2,32,128]{2,1,0:T(8,128)S(1)}, f32[2,32,128]{2,1,0:T(8,128)S(1)}, u32[]{:S(2)}, u32[]{:S(2)}) collective-permute-start(f32[2,32,128]{2,1,0:T(8,128)S(1)} %get-tuple-element.55), channel_id=1, source_target_pairs={{0,1},{1,0},{2,3},{3,2},{4,5},{5,4},{6,7},{7,6},{8,9},{9,8},{10,11... | collective-permute-start | bytes 98312 | tf_op jit(solution)/shard_map/ppermute | solution.py:751
  102.8 7.9 %collective-permute-start.8 = (f32[160,128]{1,0:T(8,128)S(1)}, f32[160,128]{1,0:T(8,128)S(1)}, u32[]{:S(2)}, u32[]{:S(2)}) collective-permute-start(f32[160,128]{1,0:T(8,128)S(1)} %get-tuple-element.54), channel_id=1, source_target_pairs={{32,0},{64,32},{96,64},{128,96},{160,128},{192,160},{224,192},{33,... | collective-permute-start | bytes 245768 | tf_op jit(solution)/shard_map/ppermute | solution.py:757
  110.8 8.2 %collective-permute-start.13 = (f32[46,8,128]{2,1,0:T(8,128)S(1)}, f32[46,8,128]{2,1,0:T(8,128)S(1)}, u32[]{:S(2)}, u32[]{:S(2)}) collective-permute-start(f32[46,8,128]{2,1,0:T(8,128)S(1)} %get-tuple-element.76), channel_id=1, source_target_pairs={{2,0},{4,2},{6,4},{8,6},{10,8},{12,10},{14,12},{16,14},{18,16},{20... | collective-permute-start | bytes 565256 | tf_op jit(solution)/shard_map/ppermute | solution.py:767
  112.7 8.2 %collective-permute-start.12 = (f32[46,8,128]{2,1,0:T(8,128)S(1)}, f32[46,8,128]{2,1,0:T(8,128)S(1)}, u32[]{:S(2)}, u32[]{:S(2)}) collective-permute-start(f32[46,8,128]{2,1,0:T(8,128)S(1)} %get-tuple-element.77), channel_id=1, source_target_pairs={{0,2},{2,4},{4,6},{6,8},{8,10},{10,12},{12,14},{14,16},{16,18},{18... | collective-permute-start | bytes 565256 | tf_op jit(solution)/shard_map/ppermute | solution.py:766
  140.8 48.7 %all-to-all-start.2 = ((f32[16,304,128]{2,1,0:T(8,128)}), f32[16,304,128]{2,1,0:T(8,128)S(1)}, u32[]{:S(2)}, u32[]{:S(2)}) async-start(f32[16,304,128]{2,1,0:T(8,128)} %get-tuple-element.58), calls=%async_computation.2 | async-start | bytes 4980736 | tf_op jit(solution)/shard_map/all_to_all | solution.py:821
  189.5 1.5 copy-start.2

commit v3 on v2

--- a/solution.py
+++ b/solution.py
@@ -17,6 +17,7 @@
 TILES = INNER // TILE
 PER_TILE = TILE // BOX
 ROWS = BOX * TILES
+PITCH = ROWS + 8
 RETURN_ROWS = PADDED * TILES + 4 * TILES
 STEP_DT = 0.25
 SHIFT_WEIGHT = 0.5
@@ -100,13 +101,13 @@
 
 def put_rows(ref, x, tiles):
     for q, tile in enumerate(tiles):
-        ref[pl.ds(x * TILES + q, 8, stride=ROWS), :] = tile
+        ref[pl.ds(x * TILES + q, 8, stride=PITCH), :] = tile
 
 
 def send_rows(slots, rows_ref, out_ref, sem, count):
     copies = [
         pltpu.make_async_copy(
-            rows_ref.at[pl.ds(pl.multiple_of(slots[d] * ROWS, ROWS), ROWS)],
+            rows_ref.at[pl.ds(pl.multiple_of(slots[d] * PITCH, 8), ROWS)],
             out_ref.at[d],
             sem.at[d],
         )
@@ -118,52 +119,98 @@
         copy.wait()
 
 
-def volume_kernel(slots, fraction, planes, rows, packed, tail, sem, *, lanes_by):
+def own_slots(table, own, lanes_by):
+    per_brick = table.shape[0] // lanes_by
+    count = jnp.int32(0)
+    slots = []
+    for d in range(lanes_by):
+        slot = jnp.int32(0)
+        for k in range(per_brick):
+            hit = jnp.where(table[d * per_brick + k] == own[0], 1, 0)
+            slot = slot + hit * count
+            count = count + hit
+        slots.append(slot)
+    return slots
+
+
+CHUNK = 8
+
+
+def fetched_until(x):
+    return x * PLANE // TILE * TILE + WIDE
+
+
+def volume_kernel(table, own, fraction, rows, cells, packed, sem_in, sem, *, lanes_by):
     lanes = lane_index()
+    fetches = []
+    begin = 0
+    for chunk in range(BOX // CHUNK):
+        end = fetched_until((chunk + 1) * CHUNK)
+        fetches.append(
+            pltpu.make_async_copy(
+                fraction.at[:, pl.ds(begin, end - begin)],
+                cells.at[:, pl.ds(begin, end - begin)],
+                sem_in.at[chunk],
+            )
+        )
+        begin = end
+    for fetch in fetches:
+        fetch.start()
+    slots = own_slots(table, own, lanes_by)
+
+    def send(chunk):
+        span = CHUNK * TILES
+        copies = [
+            pltpu.make_async_copy(
+                packed.at[pl.ds(pl.multiple_of(slots[d] * PITCH + chunk * span, 8), span)],
+                rows.at[d, pl.ds(chunk * span, span)],
+                sem.at[chunk, d],
+            )
+            for d in range(lanes_by)
+        ]
+        for copy in copies:
+            copy.start()
+        return copies
+
+    def body(x, carry):
+        tiles = aligned_plane(
+            lambda s: cells[:, pl.ds(s, WIDE)].astype(jnp.float32) * (1.0 / 256.0), x, lanes
+        )
+        put_rows(packed, x - 1, compact(jnp.concatenate(tiles, axis=1), 0, lanes))
+        return carry
+
+    copies = []
+    for chunk in range(BOX // CHUNK):
+        fetches[chunk].wait()
+        loop(chunk * CHUNK + 1, (chunk + 1) * CHUNK + 1, lambda x: body(x, 0), 4)
+        copies += send(chunk)
+    for copy in copies:
+        copy.wait()
+
+
+def flux_kernel(slots, velocity, fraction, planes, masses, rows, field, tail, carry_ref, packed, sem, *, lanes_by):
+    lanes = lane_index()
+    inside = inside_plane()
 
     def align(x):
         tiles = aligned_plane(
             lambda s: fraction[:, pl.ds(s, WIDE)].astype(jnp.float32) * (1.0 / 256.0), x, lanes
         )
         store_plane(planes, (x,), tiles)
-
-    def body(x, carry):
+        for c in range(3):
+            store_plane(field, (x, c), aligned_plane(lambda s: velocity[c, :, pl.ds(s, WIDE)], x, lanes))
+
+    def align_body(x, carry):
         align(x)
         return carry
 
-    lax.fori_loop(0, PADDED - 1, body, 0)
+    loop(0, PADDED - 1, align, 3)
     start = (PADDED - 1) * PLANE
     first = start // TILE * TILE
     span = PADDED * PLANE - first
     tail[...] = jnp.zeros_like(tail)
     tail[:, 0:span] = fraction[:, first : PADDED * PLANE].astype(jnp.float32) * (1.0 / 256.0)
     planes[PADDED - 1] = ahead(tail[...], start - first)
-
-    def pack(x, carry):
-        put_rows(packed, x, compact(planes[x + 1], 0, lanes))
-        return carry
-
-    lax.fori_loop(0, BOX, pack, 0)
-    send_rows(slots, packed, rows, sem, lanes_by)
-
-
-def flux_kernel(slots, velocity, planes, masses, rows, field, tail, carry_ref, packed, sem, *, lanes_by):
-    lanes = lane_index()
-    inside = inside_plane()
-
-    def align(x):
-        for c in range(3):
-            store_plane(field, (x, c), aligned_plane(lambda s: velocity[c, :, pl.ds(s, WIDE)], x, lanes))
-
-    def align_body(x, carry):
-        align(x)
-        return carry
-
-    lax.fori_loop(0, PADDED - 1, align_body, 0)
-    start = (PADDED - 1) * PLANE
-    first = start // TILE * TILE
-    span = PADDED * PLANE - first
-    tail[...] = jnp.zeros_like(tail)
     for c in range(3):
         tail[:, 0:span] = velocity[c, :, first : PADDED * PLANE]
         field[PADDED - 1, c] = ahead(tail[...], start - first)
@@ -218,7 +265,8 @@
             total = total + ahead(here, offset) + behind(here, offset)
         return total
 
-    def step(x, carry):
+    def step(i, carry):
+        x = pl.program_id(0) * STEP_X + i + 1
         volume = planes[x]
         weight = jnp.where(inside, volume, 0.0)
         below = jnp.where(inside & (x > 1), planes[x - 1], 0.0)
@@ -229,16 +277,16 @@
         for c in range(3):
             here = masses[x, c]
             spread = neighbours(here, masses[x - 1, c], masses[x + 1, c]) * inverse
-            put(updated, (x - 1, c), compact(jnp.where(cut, spread, here), 0, lanes))
-        put(apertures, (x - 1, 0), compact(jnp.minimum(volume, planes[x - 1]), 0, lanes))
-        put(apertures, (x - 1, 1), compact(jnp.minimum(volume, planes[x + 1]), 0, lanes))
+            put(updated, (i, c), compact(jnp.where(cut, spread, here), 0, lanes))
+        put(apertures, (i, 0), compact(jnp.minimum(volume, planes[x - 1]), 0, lanes))
+        put(apertures, (i, 1), compact(jnp.minimum(volume, planes[x + 1]), 0, lanes))
         for axis, offset in ((1, PADDED), (2, 1)):
             aperture = jnp.minimum(volume, ahead(volume, offset))
-            put(apertures, (x - 1, 2 * axis), compact(aperture, -offset, lanes))
-            put(apertures, (x - 1, 2 * axis + 1), compact(aperture, 0, lanes))
+            put(apertures, (i, 2 * axis), compact(aperture, -offset, lanes))
+            put(apertures, (i, 2 * axis + 1), compact(aperture, 0, lanes))
         return carry
 
-    lax.fori_loop(1, PADDED - 1, step, 0)
+    loop(0, STEP_X, lambda i: step(i, 0), 4)
 
 
 STEP_X = 4
@@ -306,45 +354,53 @@
     return jax.ShapeDtypeStruct(shape, jnp.float32)
 
 
-def volume_call(send_slot, fraction):
-    lanes_by = send_slot.shape[0]
+def volume_call(table, own, fraction, lanes_by):
     return pl.pallas_call(
         functools.partial(volume_kernel, lanes_by=lanes_by),
-        in_specs=[SMEM_SPEC, VMEM_SPEC],
-        out_specs=[VMEM_SPEC, HBM_SPEC],
-        out_shape=[struct(PADDED, 8, WIDE), struct(lanes_by, ROWS, TILE)],
+        in_specs=[SMEM_SPEC, SMEM_SPEC, ANY_SPEC],
+        out_specs=HBM_SPEC,
+        out_shape=struct(lanes_by, ROWS, TILE),
         scratch_shapes=[
-            pltpu.VMEM((8 * ROWS, TILE), jnp.float32),
-            pltpu.VMEM((8, WIDE), jnp.float32),
-            pltpu.SemaphoreType.DMA((lanes_by,)),
+            pltpu.VMEM((8, fetched_until(BOX)), jnp.int32),
+            pltpu.VMEM((8 * PITCH, TILE), jnp.float32),
+            pltpu.SemaphoreType.DMA((BOX // CHUNK,)),
+            pltpu.SemaphoreType.DMA((BOX // CHUNK, lanes_by)),
         ],
         name="volume_rows",
-    )(send_slot, fraction)
-
-
-def flux_call(send_slot, velocity, planes):
+    )(table, own, fraction)
+
+
+def flux_call(send_slot, velocity, fraction):
     lanes_by = send_slot.shape[0]
     return pl.pallas_call(
         functools.partial(flux_kernel, lanes_by=lanes_by),
         in_specs=[SMEM_SPEC, VMEM_SPEC, VMEM_SPEC],
-        out_specs=[VMEM_SPEC, HBM_SPEC],
-        out_shape=[struct(PADDED, 3, 8, WIDE), struct(lanes_by, ROWS, TILE)],
+        out_specs=[VMEM_SPEC, VMEM_SPEC, HBM_SPEC],
+        out_shape=[
+            struct(PADDED, 8, WIDE),
+            struct(PADDED, 3, 8, WIDE),
+            struct(lanes_by, ROWS, TILE),
+        ],
         scratch_shapes=[
             pltpu.VMEM((PADDED, 3, 8, WIDE), jnp.float32),
             pltpu.VMEM((8, WIDE), jnp.float32),
             pltpu.VMEM((4, 8, WIDE), jnp.float32),
-            pltpu.VMEM((8 * ROWS, TILE), jnp.float32),
+            pltpu.VMEM((8 * PITCH, TILE), jnp.float32),
             pltpu.SemaphoreType.DMA((lanes_by,)),
         ],
         name="flux_rows",
-    )(send_slot, velocity, planes)
+    )(send_slot, velocity, fraction)
 
 
 def update_call(masses, planes):
     return pl.pallas_call(
         update_kernel,
+        grid=(BOX // STEP_X,),
         in_specs=[VMEM_SPEC, VMEM_SPEC],
-        out_specs=[VMEM_SPEC, VMEM_SPEC],
+        out_specs=[
+            pl.BlockSpec((STEP_X, 3, 8, INNER), lambda i: (i, 0, 0, 0)),
+            pl.BlockSpec((STEP_X, 6, 8, INNER), lambda i: (i, 0, 0, 0)),
+        ],
         out_shape=[struct(BOX, 3, 8, INNER), struct(BOX, 6, 8, INNER)],
         name="updated",
     )(masses, planes)
@@ -823,9 +879,11 @@
 
 def local(velocity, fraction, placement):
     send_slot, slot_row, brick_table, box_of_row = routing(placement, velocity.shape[0])
-    planes, volume_rows = volume_call(send_slot, fraction)
+    own = lax.axis_index("by").reshape(1)
+    table = placement.reshape(-1)
+    volume_rows = volume_call(table, own, fraction, send_slot.shape[0])
     volume_recv = exchange(volume_rows)
-    masses, source_rows = flux_call(send_slot, jnp.swapaxes(velocity, 0, 1), planes)
+    planes, masses, source_rows = flux_call(send_slot, jnp.swapaxes(velocity, 0, 1), fraction)
     source_recv = exchange(source_rows)
     updated, apertures = update_call(masses, planes)
     side = lax.axis_index("bz").reshape(1)
@@ -833,7 +891,7 @@
     source_recv, volume = lax.optimization_barrier((source_recv, volume))
     source = halo(assemble_call(brick_table, side, source_recv))
     pressure, rows = solve_call(box_of_row, side, placement.shape[3], volume, source)
-    returned = exchange(pltpu.with_memory_space_constraint(rows, pltpu.HBM))
+    returned = exchange(rows)
     corrected = correct_call(slot_row, updated, apertures, returned)
     return (jnp.swapaxes(corrected, 0, 1), pressure)
 

time: 202 us -> 198 us (0.980); the launches traced: 201 us -> 194 us
  Pallas kernels: 104 us -> 97.6 us
    ppermute x2, waiting for transfers between devices: 9.31 us -> 0.01 us  [halo(): x_hi = lax.ppermute(first, 'bx', down)]
    ppermute x2, starting transfers between devices: 3.84 us -> 10.2 us  [halo(): z_lo = lax.ppermute(strip_last, ('bx', 'bz'), cross_up)]
    ppermute x2, waiting for transfers between devices: 0.01 us -> 5.45 us  [halo(): z_hi = lax.ppermute(strip_first, ('bx', 'bz'), cross_down)]
    pallas_call x1, Pallas kernels: 37 us -> 32.9 us  [update_call(): pl.pallas_call(update_kernel, grid=(BOX // STEP_X,), in_specs=[VMEM_SPEC,...]
    pallas_call x1, Pallas kernels: 10.3 us -> 6.61 us  [volume_call(): pl.pallas_call(functools.partial(volume_kernel, lanes_by=lanes_by), in_sp...]
    ppermute x2, starting transfers between devices: 7.28 us -> 3.84 us  [halo(): z_hi = lax.ppermute(strip_first, ('bx', 'bz'), cross_down)]
    all_to_all x3, starting transfers between devices: 27.2 us -> 23.9 us  [exchange(): return lax.all_to_all(rows, 'by', split_axis=0, concat_axis=0, tiled=True)]
    ppermute x2, waiting for transfers between devices: 4.49 us -> 7.55 us  [halo(): y_hi = lax.ppermute(edge(0), 'by', [(j, i) for i, j in y_up])]
  transfers between devices with their start and end apart: 17 -> 17, of which waited for: 7 -> 7; matrix products, arithmetic and copies ran while one was open for 2% -> 3% of each run, Pallas kernels for 31% -> 30%
where the time goes in v3:
time: 198 us; the launch traced here: 194 us
  Pallas kernels  97.6 us (49%)
  starting transfers between devices  62.7 us (32%)
  waiting for transfers between devices  22.1 us (11%)
  local copies, waits for them, and re-layouts  9.83 us (5%)
    pallas_call x1, Pallas kernels, update_call(): pl.pallas_call(update_kernel, grid=(BOX // STEP_X,), in_specs=[VMEM_SPEC,...  32.9 us
    all_to_all x3, starting transfers between devices, exchange(): return lax.all_to_all(rows, 'by', split_axis=0, concat_axis=0, tiled=True)  23.9 us
    pallas_call x1, Pallas kernels, flux_call(): pl.pallas_call(functools.partial(flux_kernel, lanes_by=lanes_by), in_spec...  22.9 us
    pallas_call x1, Pallas kernels, solve_call(): pl.pallas_call(functools.partial(solve_kernel, count=count, lanes_by=lane...  21.7 us
    ppermute x2, starting transfers between devices, halo(): z_lo = lax.ppermute(strip_last, ('bx', 'bz'), cross_up)  10.2 us
    pallas_call x1, Pallas kernels, correct_call(): pl.pallas_call(correct_kernel, grid=(BOX // STEP_X,), in_specs=[SMEM_SPEC...  10.2 us
    ppermute x2, starting transfers between devices, halo(): x_lo = lax.ppermute(last, 'bx', up)  8.74 us
    unnamed x21, local copies, waits for them, and re-layouts  8.27 us
  transfers between devices with their start and end apart: 17, of which 7 were waited for; matrix products, arithmetic and copies ran while one was open for 3% of the time, Pallas kernels for 30%

profile of v3, /device:TPU:98, one launch (start us, length us, event | category | flops | bytes accessed | tf_op | source)
XLA Modules:
  0.0 194.2 jit_solution(9657671924651076135)
XLA Ops:
  0.6 0.8 copy.9
  1.4 0.6 reshape_squeeze.3.table
  2.0 6.6 %volume_rows.1 = f32[16,256,128]{2,1,0:T(8,128)} custom-call(s32[64]{0:T(128)} %reshape_squeeze.3.table, s32[1]{0:T(128)} %bitcast.3.own, s32[8,39304]{1,0:T(8,128)} %fraction.3), custom_call_target="tpu_custom_call" | custom-call | tf_op jit(solution)/shard_map/volume_rows/pallas_call | solution.py:358
  8.6 0.0 copy-start.4
  8.6 0.0 copy-start.3
  8.6 7.5 %all-to-all-start.1 = ((f32[16,256,128]{2,1,0:T(8,128)}), f32[16,256,128]{2,1,0:T(8,128)S(1)}, u32[]{:S(2)}, u32[]{:S(2)}) async-start(f32[16,256,128]{2,1,0:T(8,128)} %volume_rows.1), calls=%async_computation.1 | async-start | bytes 4194304 | tf_op jit(solution)/shard_map/all_to_all | solution.py:877
  16.1 0.1 fusion
  16.2 0.1 reduce_window_sum.11
  16.3 0.2 select_reduce_fusion
  16.5 0.1 reshape.69
  16.6 0.1 copy.10
  16.7 0.5 select_reduce_fusion.3.slots
  17.2 22.9 %flux_rows.1 = (f32[34,8,1280]{2,1,0:T(8,128)}, f32[34,3,8,1280]{3,2,1,0:T(8,128)}, f32[16,256,128]{2,1,0:T(8,128)}) custom-call(s32[16]{0:T(128)} %select_reduce_fusion.3.slots, f32[3,8,39304]{2,1,0:T(8,128)} %bitcast.30, s32[8,39304]{1,0:T(8,128)} %fraction.3), custom_call_target="tpu_custom_call" | custom-call | tf_op jit(solution)/shard_map/flux_rows/pallas_call | solution.py:375
  40.1 3.2 %all-to-all-done.1.refs_0_.refs_1_.refs_2_.refs_3_ = f32[16,256,128]{2,1,0:T(8,128)S(1)} async-done(((f32[16,256,128]{2,1,0:T(8,128)}), f32[16,256,128]{2,1,0:T(8,128)S(1)}, u32[]{:S(2)}, u32[]{:S(2)}) %all-to-all-start.1) | async-done | bytes 2097184 | tf_op jit(solution)/shard_map/all_to_all | solution.py:877
  43.3 1.3 copy-done
  44.6 8.3 %all-to-all-start = ((f32[16,256,128]{2,1,0:T(8,128)}), f32[16,256,128]{2,1,0:T(8,128)S(1)}, u32[]{:S(2)}, u32[]{:S(2)}) async-start(f32[16,256,128]{2,1,0:T(8,128)} %get-tuple-element.34), calls=%async_computation | async-start | bytes 4194304 | tf_op jit(solution)/shard_map/all_to_all | solution.py:877
  52.9 0.2 dynamic-slice_reduce_fusion.table
  53.0 1.6 copy-done.1
  54.6 1.6 brick.2
  56.3 5.0 %collective-permute-start = (f32[160,128]{1,0:T(8,128)S(1)}, f32[160,128]{1,0:T(8,128)S(1)}, u32[]{:S(2)}, u32[]{:S(2)}) collective-permute-start(f32[160,128]{1,0:T(8,128)S(1)} %get-tuple-element.36), channel_id=1, source_target_pairs={{0,32},{32,64},{64,96},{96,128},{128,160},{160,192},{192,224},{1,3... | collective-permute-start | bytes 245768 | tf_op jit(solution)/shard_map/ppermute | solution.py:812
  61.3 1.9 collective-permute-start.1
  63.2 0.1 collective-permute-start.2
  63.3 5.2 %collective-permute-start.3 = (f32[32,128]{1,0:T(8,128)S(1)}, f32[32,128]{1,0:T(8,128)S(1)}, u32[]{:S(2)}, u32[]{:S(2)}) collective-permute-start(f32[32,128]{1,0:T(8,128)S(1)} %get-tuple-element.39), channel_id=1, source_target_pairs={{0,33},{1,32},{32,65},{33,64},{64,97},{65,96},{96,129},{97,128},{1... | collective-permute-start | bytes 49160 | tf_op jit(solution)/shard_map/ppermute | solution.py:814
  68.6 1.9 collective-permute-start.4
  70.5 0.0 collective-permute-done.refs_1_
  70.5 0.6 constant_dynamic-update-slice_fusion.9
  71.1 0.7 slice_dynamic-update-slice_fusion.2
  71.8 0.0 collective-permute-done.1.refs_2_
  71.8 0.6 constant_dynamic-update-slice_fusion.8
  72.4 0.0 collective-permute-done.3.refs_4_
  72.4 0.6 constant_dynamic-update-slice_fusion.7
  73.0 0.0 collective-permute-done.2.refs_3_
  73.0 0.6 constant_dynamic-update-slice_fusion.6
  73.6 1.2 collective-permute-done.4.refs_5_
  74.8 0.6 constant_dynamic-update-slice_fusion.5
  75.4 3.4 %collective-permute-start.5 = (f32[46,8,128]{2,1,0:T(8,128)}, f32[46,8,128]{2,1,0:T(8,128)S(1)}, u32[]{:S(2)}, u32[]{:S(2)}) collective-permute-start(f32[46,8,128]{2,1,0:T(8,128)} %get-tuple-element.79), channel_id=1, source_target_pairs={{0,2},{2,4},{4,6},{6,8},{8,10},{10,12},{12,14},{14,16},{16,18},{18... | collective-permute-start | bytes 565256 | tf_op jit(solution)/shard_map/ppermute | solution.py:822
  78.8 2.5 %collective-permute-start.6 = (f32[46,8,128]{2,1,0:T(8,128)S(1)}, f32[46,8,128]{2,1,0:T(8,128)S(1)}, u32[]{:S(2)}, u32[]{:S(2)}) collective-permute-start(f32[46,8,128]{2,1,0:T(8,128)S(1)} %get-tuple-element.78), channel_id=1, source_target_pairs={{2,0},{4,2},{6,4},{8,6},{10,8},{12,10},{14,12},{16,14},{18,16},{20... | collective-permute-start | bytes 565256 | tf_op jit(solution)/shard_map/ppermute | solution.py:823
  81.3 0.0 all-to-all-done.refs_0_.refs_1_.refs_2_.refs_3_
  81.3 3.2 %collective-permute-done.5.refs_6_ = f32[46,8,128]{2,1,0:T(8,128)S(1)} collective-permute-done((f32[46,8,128]{2,1,0:T(8,128)}, f32[46,8,128]{2,1,0:T(8,128)S(1)}, u32[]{:S(2)}, u32[]{:S(2)}) %collective-permute-start.5) | collective-permute-done | bytes 188448 | tf_op jit(solution)/shard_map/ppermute | solution.py:822
  84.5 2.9 %collective-permute-done.6.refs_7_ = f32[46,8,128]{2,1,0:T(8,128)S(1)} collective-permute-done((f32[46,8,128]{2,1,0:T(8,128)S(1)}, f32[46,8,128]{2,1,0:T(8,128)S(1)}, u32[]{:S(2)}, u32[]{:S(2)}) %collective-permute-start.6) | collective-permute-done | bytes 188448 | tf_op jit(solution)/shard_map/ppermute | solution.py:823
  87.4 1.6 brick.3
  89.0 3.7 %collective-permute-start.7 = (f32[160,128]{1,0:T(8,128)S(1)}, f32[160,128]{1,0:T(8,128)S(1)}, u32[]{:S(2)}, u32[]{:S(2)}) collective-permute-start(f32[160,128]{1,0:T(8,128)S(1)} %get-tuple-element.51), channel_id=1, source_target_pairs={{0,32},{32,64},{64,96},{96,128},{128,160},{160,192},{192,224},{1,3... | collective-permute-start | bytes 245768 | tf_op jit(solution)/shard_map/ppermute | solution.py:812
  92.7 2.1 %collective-permute-start.8 = (f32[160,128]{1,0:T(8,128)S(1)}, f32[160,128]{1,0:T(8,128)S(1)}, u32[]{:S(2)}, u32[]{:S(2)}) collective-permute-start(f32[160,128]{1,0:T(8,128)S(1)} %get-tuple-element.52), channel_id=1, source_target_pairs={{32,0},{64,32},{96,64},{128,96},{160,128},{192,160},{224,192},{33,... | collective-permute-start | bytes 245768 | tf_op jit(solution)/shard_map/ppermute | solution.py:813
  94.9 0.1 collective-permute-start.9
  95.0 5.0 %collective-permute-start.10 = (f32[32,128]{1,0:T(8,128)S(1)}, f32[32,128]{1,0:T(8,128)S(1)}, u32[]{:S(2)}, u32[]{:S(2)}) collective-permute-start(f32[32,128]{1,0:T(8,128)S(1)} %get-tuple-element.54), channel_id=1, source_target_pairs={{0,33},{1,32},{32,65},{33,64},{64,97},{65,96},{96,129},{97,128},{1... | collective-permute-start | bytes 49160 | tf_op jit(solution)/shard_map/ppermute | solution.py:814
  100.0 1.9 collective-permute-start.11
  101.9 0.0 collective-permute-done.7.refs_9_
  102.0 0.0 collective-permute-done.8.refs_10_
  102.0 0.0 collective-permute-done.10.refs_12_
  102.0 0.0 collective-permute-done.9.refs_11_
  102.0 4.2 %collective-permute-done.11.refs_13_ = f32[32,128]{1,0:T(8,128)S(1)} collective-permute-done((f32[32,128]{1,0:T(8,128)S(1)}, f32[32,128]{1,0:T(8,128)S(1)}, u32[]{:S(2)}, u32[]{:S(2)}) %collective-permute-start.11) | collective-permute-done | bytes 16416 | tf_op jit(solution)/shard_map/ppermute | solution.py:815
  106.3 3.1 %collective-permute-start.12 = (f32[46,8,128]{2,1,0:T(8,128)S(1)}, f32[46,8,128]{2,1,0:T(8,128)S(1)}, u32[]{:S(2)}, u32[]{:S(2)}) collective-permute-start(f32[46,8,128]{2,1,0:T(8,128)S(1)} %get-tuple-element.75), channel_id=1, source_target_pairs={{0,2},{2,4},{4,6},{6,8},{8,10},{10,12},{12,14},{14,16},{16,18},{18... | collective-permute-start | bytes 565256 | tf_op jit(solution)/shard_map/ppermute | solution.py:822
  109.3 2.8 %collective-permute-start.13 = (f32[46,8,128]{2,1,0:T(8,128)S(1)}, f32[46,8,128]{2,1,0:T(8,128)S(1)}, u32[]{:S(2)}, u32[]{:S(2)}) collective-permute-start(f32[46,8,128]{2,1,0:T(8,128)S(1)} %get-tuple-element.74), channel_id=1, source_target_pairs={{2,0},{4,2},{6,4},{8,6},{10,8},{12,10},{14,12},{16,14},{18,16},{20... | collective-permute-start | bytes 565256 | tf_op jit(solution)/shard_map/ppermute | solution.py:823
  112.1 0.1 select_reduce_fusion.2.box_of_row
  112.2 2.7 %collective-permute-done.12.refs_14_ = f32[46,8,128]{2,1,0:T(8,128)S(1)} collective-permute-done((f32[46,8,128]{2,1,0:T(8,128)S(1)}, f32[46,8,128]{2,1,0:T(8,128)S(1)}, u32[]{:S(2)}, u32[]{:S(2)}) %collective-permute-start.12) | collective-permute-done | bytes 188448 | tf_op jit(solution)/shard_map/ppermute | solution.py:822
  114.9 4.7 %collective-permute-done.13.refs_15_ = f32[46,8,128]{2,1,0:T(8,128)S(1)} collective-permute-done((f32[46,8,128]{2,1,0:T(8,128)S(1)}, f32[46,8,128]{2,1,0:T(8,128)S(1)}, u32[]{:S(2)}, u32[]{:S(2)}) %collective-permute-start.13) | collective-permute-done | bytes 188448 | tf_op jit(solution)/shard_map/ppermute | solution.py:823
  119.5 21.7 %solve.1 = (f32[32,32,128]{2,1,0:T(8,128)}, f32[16,304,128]{2,1,0:T(8,128)S(1)}) custom-call(s32[16]{0:T(128)S(1)} %select_reduce_fusion.2.box_of_row, s32[1]{0:T(128)} %bitcast.2.side, f32[1024,128]{1,0:T(8,128)S(1)} %get-tuple-element.41.refs_0_, f32[160,128]{1,0:T(8,128)S(1)} %collective-permute-done.refs_1_, ...), custom_call_target="tpu_custom_call" | custom-call | tf_op jit(solution)/shard_map/solve/pallas_call | solution.py:831
  141.2 0.0 copy-start.2
  141.3 1.4 copy-done.2
  142.7 8.2 %all-to-all-start.2 = ((f32[16,304,128]{2,1,0:T(8,128)}), f32[16,304,128]{2,1,0:T(8,128)S(1)}, u32[]{:S(2)}, u32[]{:S(2)}) async-start(f32[16,304,128]{2,1,0:T(8,128)} %copy-done.2), calls=%async_computation.2 | async-start | bytes 4980736 | tf_op jit(solution)/shard_map/all_to_all | solution.py:877
  150.9 32.9 %updated.1 = (f32[32,3,8,1024]{3,2,1,0:T(8,128)}, f32[32,6,8,1024]{3,2,1,0:T(8,128)}) custom-call(f32[34,3,8,1280]{3,2,1,0:T(8,128)} %get-tuple-element.30.masses, f32[34,8,1280]{2,1,0:T(8,128)} %get-tuple-element.31.planes), custom_call_target="tpu_custom_call" | custom-call | tf_op jit(solution)/shard_map/updated/pallas_call | solution.py:396
  183.8 0.1 select_reduce_fusion.1.rows
  183.9 0.0 all-to-all-done.2.returned
  183.9 10.2 %corrected.1 = f32[3,8,32768]{2,1,0:T(8,128)} custom-call(s32[8]{0:T(128)S(1)} %select_reduce_fusion.1.rows, f32[32,3,8,1024]{3,2,1,0:T(8,128)} %get-tuple-element.32.updated, f32[32,6,8,1024]{3,2,1,0:T(8,128)} %get-tuple-element.33.apertures, f32[16,304,128]{2,1,0:T(8,128)S(1)} %all-to-all-done.2.returned), custom_call_target="tpu_custom_call" | custom-call | tf_op jit(solution)/shard_map/corrected/pallas_call | solution.py:410
  (12 shorter events, 0.1 us)
Async XLA Ops:
  8.6 7.5 %copy-start.4 = (s32[64]{0:T(128)S(1)}, s32[64]{0:T(128)}, u32[]{:S(2)}) copy-start(s32[64]{0:T(128)} %reshape_squeeze.3.table) | copy-start | bytes 772
  8.6 8.0 %copy-start.3 = (s32[1,16,1,4]{1,3,2,0:T(4,128)S(1)}, s32[1,16,1,4]{1,3,2,0:T(4,128)}, u32[]{:S(2)}) copy-start(s32[1,16,1,4]{1,3,2,0:T(4,128)} %param.5) | copy-start | bytes 772
  8.6 34.6 %all-to-all-start.1 = ((f32[16,256,128]{2,1,0:T(8,128)}), f32[16,256,128]{2,1,0:T(8,128)S(1)}, u32[]{:S(2)}, u32[]{:S(2)}) async-start(f32[16,256,128]{2,1,0:T(8,128)} %volume_rows.1), calls=%async_computation.1 | async-start | bytes 4194304 | tf_op jit(solution)/shard_map/all_to_all | solution.py:877
  43.3 1.3 copy-start
  44.6 36.7 %all-to-all-start = ((f32[16,256,128]{2,1,0:T(8,128)}), f32[16,256,128]{2,1,0:T(8,128)S(1)}, u32[]{:S(2)}, u32[]{:S(2)}) async-start(f32[16,256,128]{2,1,0:T(8,128)} %get-tuple-element.34), calls=%async_computation | async-start | bytes 4194304 | tf_op jit(solution)/shard_map/all_to_all | solution.py:877
  53.0 1.6 copy-start.1
  56.3 14.2 %collective-permute-start = (f32[160,128]{1,0:T(8,128)S(1)}, f32[160,128]{1,0:T(8,128)S(1)}, u32[]{:S(2)}, u32[]{:S(2)}) collective-permute-start(f32[160,128]{1,0:T(8,128)S(1)} %get-tuple-element.36), channel_id=1, source_target_pairs={{0,32},{32,64},{64,96},{96,128},{128,160},{160,192},{192,224},{1,3... | collective-permute-start | bytes 245768 | tf_op jit(solution)/shard_map/ppermute | solution.py:812
  61.3 10.5 %collective-permute-start.1 = (f32[160,128]{1,0:T(8,128)S(1)}, f32[160,128]{1,0:T(8,128)S(1)}, u32[]{:S(2)}, u32[]{:S(2)}) collective-permute-start(f32[160,128]{1,0:T(8,128)S(1)} %get-tuple-element.37), channel_id=1, source_target_pairs={{32,0},{64,32},{96,64},{128,96},{160,128},{192,160},{224,192},{33,... | collective-permute-start | bytes 245768 | tf_op jit(solution)/shard_map/ppermute | solution.py:813
  63.2 9.8 %collective-permute-start.2 = (f32[2,32,128]{2,1,0:T(8,128)S(1)}, f32[2,32,128]{2,1,0:T(8,128)S(1)}, u32[]{:S(2)}, u32[]{:S(2)}) collective-permute-start(f32[2,32,128]{2,1,0:T(8,128)S(1)} %get-tuple-element.38), channel_id=1, source_target_pairs={{0,1},{1,0},{2,3},{3,2},{4,5},{5,4},{6,7},{7,6},{8,9},{9,8},{10,11... | collective-permute-start | bytes 98312 | tf_op jit(solution)/shard_map/ppermute | solution.py:807
  63.3 9.1 %collective-permute-start.3 = (f32[32,128]{1,0:T(8,128)S(1)}, f32[32,128]{1,0:T(8,128)S(1)}, u32[]{:S(2)}, u32[]{:S(2)}) collective-permute-start(f32[32,128]{1,0:T(8,128)S(1)} %get-tuple-element.39), channel_id=1, source_target_pairs={{0,33},{1,32},{32,65},{33,64},{64,97},{65,96},{96,129},{97,128},{1... | collective-permute-start | bytes 49160 | tf_op jit(solution)/shard_map/ppermute | solution.py:814
  68.6 6.3 %collective-permute-start.4 = (f32[32,128]{1,0:T(8,128)S(1)}, f32[32,128]{1,0:T(8,128)S(1)}, u32[]{:S(2)}, u32[]{:S(2)}) collective-permute-start(f32[32,128]{1,0:T(8,128)S(1)} %get-tuple-element.40), channel_id=1, source_target_pairs={{32,1},{33,0},{64,33},{65,32},{96,65},{97,64},{128,97},{129,96},{1... | collective-permute-start | bytes 49160 | tf_op jit(solution)/shard_map/ppermute | solution.py:815
  75.4 9.0 %collective-permute-start.5 = (f32[46,8,128]{2,1,0:T(8,128)}, f32[46,8,128]{2,1,0:T(8,128)S(1)}, u32[]{:S(2)}, u32[]{:S(2)}) collective-permute-start(f32[46,8,128]{2,1,0:T(8,128)} %get-tuple-element.79), channel_id=1, source_target_pairs={{0,2},{2,4},{4,6},{6,8},{8,10},{10,12},{12,14},{14,16},{16,18},{18... | collective-permute-start | bytes 565256 | tf_op jit(solution)/shard_map/ppermute | solution.py:822
  78.8 8.6 %collective-permute-start.6 = (f32[46,8,128]{2,1,0:T(8,128)S(1)}, f32[46,8,128]{2,1,0:T(8,128)S(1)}, u32[]{:S(2)}, u32[]{:S(2)}) collective-permute-start(f32[46,8,128]{2,1,0:T(8,128)S(1)} %get-tuple-element.78), channel_id=1, source_target_pairs={{2,0},{4,2},{6,4},{8,6},{10,8},{12,10},{14,12},{16,14},{18,16},{20... | collective-permute-start | bytes 565256 | tf_op jit(solution)/shard_map/ppermute | solution.py:823
  89.0 12.9 %collective-permute-start.7 = (f32[160,128]{1,0:T(8,128)S(1)}, f32[160,128]{1,0:T(8,128)S(1)}, u32[]{:S(2)}, u32[]{:S(2)}) collective-permute-start(f32[160,128]{1,0:T(8,128)S(1)} %get-tuple-element.51), channel_id=1, source_target_pairs={{0,32},{32,64},{64,96},{96,128},{128,160},{160,192},{192,224},{1,3... | collective-permute-start | bytes 245768 | tf_op jit(solution)/shard_map/ppermute | solution.py:812
  92.7 9.2 %collective-permute-start.8 = (f32[160,128]{1,0:T(8,128)S(1)}, f32[160,128]{1,0:T(8,128)S(1)}, u32[]{:S(2)}, u32[]{:S(2)}) collective-permute-start(f32[160,128]{1,0:T(8,128)S(1)} %get-tuple-element.52), channel_id=1, source_target_pairs={{32,0},{64,32},{96,64},{128,96},{160,128},{192,160},{224,192},{33,... | collective-permute-start | bytes 245768 | tf_op jit(solution)/shard_map/ppermute | solution.py:813
  94.9 7.1 %collective-permute-start.9 = (f32[2,32,128]{2,1,0:T(8,128)S(1)}, f32[2,32,128]{2,1,0:T(8,128)S(1)}, u32[]{:S(2)}, u32[]{:S(2)}) collective-permute-start(f32[2,32,128]{2,1,0:T(8,128)S(1)} %get-tuple-element.53), channel_id=1, source_target_pairs={{0,1},{1,0},{2,3},{3,2},{4,5},{5,4},{6,7},{7,6},{8,9},{9,8},{10,11... | collective-permute-start | bytes 98312 | tf_op jit(solution)/shard_map/ppermute | solution.py:807
  95.0 7.0 %collective-permute-start.10 = (f32[32,128]{1,0:T(8,128)S(1)}, f32[32,128]{1,0:T(8,128)S(1)}, u32[]{:S(2)}, u32[]{:S(2)}) collective-permute-start(f32[32,128]{1,0:T(8,128)S(1)} %get-tuple-element.54), channel_id=1, source_target_pairs={{0,33},{1,32},{32,65},{33,64},{64,97},{65,96},{96,129},{97,128},{1... | collective-permute-start | bytes 49160 | tf_op jit(solution)/shard_map/ppermute | solution.py:814
  100.0 6.3 %collective-permute-start.11 = (f32[32,128]{1,0:T(8,128)S(1)}, f32[32,128]{1,0:T(8,128)S(1)}, u32[]{:S(2)}, u32[]{:S(2)}) collective-permute-start(f32[32,128]{1,0:T(8,128)S(1)} %get-tuple-element.55), channel_id=1, source_target_pairs={{32,1},{33,0},{64,33},{65,32},{96,65},{97,64},{128,97},{129,96},{1... | collective-permute-start | bytes 49160 | tf_op jit(solution)/shard_map/ppermute | solution.py:815
  106.3 8.6 %collective-permute-start.12 = (f32[46,8,128]{2,1,0:T(8,128)S(1)}, f32[46,8,128]{2,1,0:T(8,128)S(1)}, u32[]{:S(2)}, u32[]{:S(2)}) collective-permute-start(f32[46,8,128]{2,1,0:T(8,128)S(1)} %get-tuple-element.75), channel_id=1, source_target_pairs={{0,2},{2,4},{4,6},{6,8},{8,10},{10,12},{12,14},{14,16},{16,18},{18... | collective-permute-start | bytes 565256 | tf_op jit(solution)/shard_map/ppermute | solution.py:822
  109.3 10.2 %collective-permute-start.13 = (f32[46,8,128]{2,1,0:T(8,128)S(1)}, f32[46,8,128]{2,1,0:T(8,128)S(1)}, u32[]{:S(2)}, u32[]{:S(2)}) collective-permute-start(f32[46,8,128]{2,1,0:T(8,128)S(1)} %get-tuple-element.74), channel_id=1, source_target_pairs={{2,0},{4,2},{6,4},{8,6},{10,8},{12,10},{14,12},{16,14},{18,16},{20... | collective-permute-start | bytes 565256 | tf_op jit(solution)/shard_map/ppermute | solution.py:823
  141.2 1.5 copy-start.2
  142.7 41.3 %all-to-all-start.2 = ((f32[16,304,128]{2,1,0:T(8,128)}), f32[16,304,128]{2,1,0:T(8,128)S(1)}, u32[]{:S(2)}, u32[]{:S(2)}) async-start(f32[16,304,128]{2,1,0:T(8,128)} %copy-done.2), calls=%async_computation.2 | async-start | bytes 4980736 | tf_op jit(solution)/shard_map/all_to_all | solution.py:877

commit v4 on v3

--- a/solution.py
+++ b/solution.py
@@ -455,7 +455,7 @@
 
 def assemble_kernel(table, side, *refs, count):
     boxes = refs[:count]
-    brick, first, last, strip, strip_first, strip_last = refs[count:]
+    brick, first, last, strip = refs[count:]
     step = pl.program_id(0)
     steps = BOX // STEP_BRICK
     lanes = lane_index()
@@ -495,14 +495,12 @@
     @pl.when(step == steps - 1)
     def _():
         last[...] = brick[(STEP_BRICK - HALO) * BOX : STEP_BRICK * BOX, :]
-        strip_first[...] = strip[0]
-        strip_last[...] = strip[BOX // GROUP - 1]
 
 
 def solve_kernel(box_of_row, side, *refs, count, lanes_by):
-    volume_in, source_in = refs[0:8], refs[8:16]
-    pressure, rows = refs[16:18]
-    scratch = refs[18:]
+    volume_in, source_in = refs[0:6], refs[6:12]
+    pressure, rows = refs[12:14]
+    scratch = refs[14:]
     (vol, ax, ay, azu, azl, diag, inv, res, sa, sb, total) = scratch[0:11]
     (hvol, hres, hsa, hsb, htotal, edge_a, edge_b, hcoef, turned, packed, sem) = scratch[11:]
     lane = lane_index()
@@ -528,27 +526,31 @@
         return g * ROWS_Y + 8
 
     def fill(ext, strips, parts):
-        brick, x_lo, x_hi, middle, z_lo, z_hi, y_lo, y_hi = parts
-
-        def rows_of(x):
-            ext[pl.ds(base(x), SIDE), :] = y_lo[x]
-            ext[pl.ds(base(x) + SIDE + BOX, SIDE), :] = y_hi[x]
+        brick, x_lo, x_hi, middle, y_lo, y_hi = parts
+        own = HALO + 1 + BOX
+        after = own + GROUPS - 2
+
+        def rows_of(x, source):
+            ext[pl.ds(base(x), SIDE), :] = y_lo[source]
+            ext[pl.ds(base(x) + SIDE + BOX, SIDE), :] = y_hi[source]
 
         def body(i):
             ext[pl.ds(base(i + HALO) + SIDE, BOX), :] = brick[pl.ds(pl.multiple_of(i * BOX, 8), BOX), :]
-            rows_of(i + HALO)
-
-        loop(0, BOX, body, 4)
+            rows_of(i + HALO, i + HALO + 1)
+
+        loop(0, BOX, body, 16)
         for i in range(HALO):
-            for x, part in ((i, x_lo), (HALO + BOX + i, x_hi)):
+            for x, part, source in ((i, x_lo, i), (HALO + BOX + i, x_hi, after + i)):
                 ext[x * ROWS_Y + SIDE : x * ROWS_Y + SIDE + BOX, :] = part[i * BOX : (i + 1) * BOX, :]
-                rows_of(x)
-        pieces = [z_lo[...]] + [middle[g] for g in range(GROUPS - 2)] + [z_hi[...]]
-        for g, piece in enumerate(pieces):
+                rows_of(x, source)
+        outer = slice(HALO * BOX, (HALO + 1) * BOX)
+        pieces = [x_lo[outer, :]] + [middle[g] for g in range(GROUPS - 2)] + [x_hi[outer, :]]
+        sources = [HALO] + [own + g for g in range(GROUPS - 2)] + [after + HALO]
+        for g, (piece, source) in enumerate(zip(pieces, sources)):
             start = strip_base(g)
-            strips[start : start + SIDE, :] = y_lo[EXT + g]
+            strips[start : start + SIDE, :] = y_lo[source]
             strips[start + SIDE : start + SIDE + BOX, :] = piece
-            strips[start + SIDE + BOX : start + ROWS_Y, :] = y_hi[EXT + g]
+            strips[start + SIDE + BOX : start + ROWS_Y, :] = y_hi[source]
 
     fill(vol, hvol, volume_in)
     fill(res, hres, source_in)
@@ -592,7 +594,7 @@
         for t in row_tiles:
             to_edge(edge_a, start, t, where, tile(vol, base(x), t))
 
-    loop(1, EXT - 1, volume_edge, 4)
+    loop(1, EXT - 1, volume_edge, 8)
     center = 0.5 * (UPPER_BOUND + LOWER_BOUND)
     halfwidth = 0.5 * (UPPER_BOUND - LOWER_BOUND)
     spread = center / halfwidth
@@ -631,7 +633,7 @@
             put(total, here, t, search)
             to_edge(edge_b, start, t, where, search)
 
-    loop(1, EXT - 1, prepare, 2)
+    loop(1, EXT - 1, prepare, 4)
     for g in range(GROUPS):
         for t in row_tiles:
             v = tile(hvol, strip_base(g), t)
@@ -676,7 +678,7 @@
 
         if iteration == ITERS - 2:
             iterate = functools.partial(iterate, edge_next=None)
-        loop(1, EXT - 1, iterate, 2)
+        loop(1, EXT - 1, iterate, 4)
         for g in range(GROUPS):
             for t in row_tiles:
                 rows_here = slice(g * ROWS_Y + 8 * t, g * ROWS_Y + 8 * t + 8)
@@ -707,12 +709,12 @@
         pieces = [total[pl.ds(start + r, TILES, stride=PER_TILE), :] for r in range(PER_TILE)]
         spread_boxes(pieces, i * TILES)
 
-    loop(0, PADDED, core, 2)
+    loop(0, PADDED, core, 17)
 
     def output(i):
         pressure[i] = total[pl.ds(base(i + HALO) + SIDE, BOX), :]
 
-    loop(0, BOX, output, 4)
+    loop(0, BOX, output, 8)
     for f, y in enumerate((SIDE - 1, SIDE + BOX)):
         pieces = [
             total[pl.ds((HALO + r) * ROWS_Y + y, TILES, stride=PER_TILE * ROWS_Y), :]
@@ -775,8 +777,6 @@
         (HALO * BOX, TILE),
         (HALO * BOX, TILE),
         (BOX // GROUP, BOX, TILE),
-        (BOX, TILE),
-        (BOX, TILE),
     ]
 
     def box_spec(k):
@@ -801,19 +801,15 @@
 
 
 def halo(parts):
-    brick, first, last, strip, strip_first, strip_last = parts
+    brick, first, last, strip = parts
     nx, ny = lax.axis_size("bx"), lax.axis_size("by")
     nz = lax.axis_size("bz")
     middle = lax.ppermute(strip, "bz", [(i, nz - 1 - i) for i in range(nz)])
     up = [(i, i + 1) for i in range(nx - 1)]
     down = [(j, i) for i, j in up]
-    cross_up = [(i * nz + z, j * nz + nz - 1 - z) for i, j in up for z in range(nz)]
-    cross_down = [(i * nz + z, j * nz + nz - 1 - z) for i, j in down for z in range(nz)]
-    x_lo = lax.ppermute(last, "bx", up)
-    x_hi = lax.ppermute(first, "bx", down)
-    z_lo = lax.ppermute(strip_last, ("bx", "bz"), cross_up)
-    z_hi = lax.ppermute(strip_first, ("bx", "bz"), cross_down)
-    cubes = [v.reshape(-1, BOX, TILE) for v in (x_lo, brick, x_hi, z_lo, middle, z_hi)]
+    x_lo = lax.ppermute(jnp.concatenate([last, middle[-1]], axis=0), "bx", up)
+    x_hi = lax.ppermute(jnp.concatenate([first, middle[0]], axis=0), "bx", down)
+    cubes = [v.reshape(-1, BOX, TILE) for v in (x_lo, brick, middle, x_hi)]
 
     def edge(start):
         return jnp.concatenate([v[:, start : start + SIDE] for v in cubes], axis=0)
@@ -821,7 +817,7 @@
     y_up = [(i, i + 1) for i in range(ny - 1)]
     y_lo = lax.ppermute(edge(BOX - SIDE), "by", y_up)
     y_hi = lax.ppermute(edge(0), "by", [(j, i) for i, j in y_up])
-    return brick, x_lo, x_hi, middle, z_lo, z_hi, y_lo, y_hi
+    return brick, x_lo, x_hi, middle, y_lo, y_hi
 
 
 def solve_call(box_of_row, side, count, volume, source):
@@ -830,7 +826,7 @@
     narrow = pltpu.VMEM((GROUPS * ROWS_Y + 16, TILE), jnp.float32)
     return pl.pallas_call(
         functools.partial(solve_kernel, count=count, lanes_by=lanes_by),
-        in_specs=[SMEM_SPEC, SMEM_SPEC] + [VMEM_SPEC] * 16,
+        in_specs=[SMEM_SPEC, SMEM_SPEC] + [VMEM_SPEC] * 12,
         out_specs=[VMEM_SPEC, HBM_SPEC],
         out_shape=[struct(BOX, BOX, count * BOX), struct(lanes_by, RETURN_ROWS, TILE)],
         scratch_shapes=[wide] * 11

time: 198 us -> 181 us (0.914); the launches traced: 194 us -> 180 us
  starting transfers between devices: 62.7 us -> 51.2 us
  waiting for transfers between devices: 22.1 us -> 27.8 us
  Pallas kernels: 97.6 us -> 92.3 us
  local copies, waits for them, and re-layouts: 9.83 us -> 6.18 us
    ppermute x8 -> x4, starting transfers between devices: 26.9 us -> 13.9 us  [the longest x2 10.1 us: halo(): x_lo = lax.ppermute(jnp.concatenate([last, middle[-1]], axis=0), 'bx', up)]
    ppermute x8 -> x4, waiting for transfers between devices: 5.47 us -> 11.6 us  [the longest x2 11.6 us: halo(): x_hi = lax.ppermute(jnp.concatenate([first, middle[0]], axis=0), 'bx', down)]
    pallas_call x1, Pallas kernels: 21.7 us -> 16.1 us  [solve_call(): pl.pallas_call(functools.partial(solve_kernel, count=count, lanes_by=lane...]
    ppermute x2, waiting for transfers between devices: 7.55 us -> 4.42 us  [halo(): y_hi = lax.ppermute(edge(0), 'by', [(j, i) for i, j in y_up])]
    unnamed x21 -> x11, local copies, waits for them, and re-layouts: 8.27 us -> 5.15 us
    all_to_all x3, waiting for transfers between devices: 3.18 us -> 5.74 us  [exchange(): return lax.all_to_all(rows, 'by', split_axis=0, concat_axis=0, tiled=True)]
    ppermute x2, waiting for transfers between devices: 0.01 us -> 2.33 us  [halo(): middle = lax.ppermute(strip, 'bz', [(i, nz - 1 - i) for i in range(nz)])]
    ppermute x2, waiting for transfers between devices: 5.87 us -> 3.78 us  [halo(): y_lo = lax.ppermute(edge(BOX - SIDE), 'by', y_up)]
  transfers between devices with their start and end apart: 17 -> 13, of which waited for: 7 -> 10; matrix products, arithmetic and copies ran while one was open for 3% -> 1% of each run, Pallas kernels for 30% -> 32%
where the time goes in v4:
time: 181 us; the launch traced here: 180 us
  Pallas kernels  92.3 us (51%)
  starting transfers between devices  51.2 us (28%)
  waiting for transfers between devices  27.8 us (15%)
  local copies, waits for them, and re-layouts  6.18 us (3%)
  other arithmetic  1.87 us (1%)
    pallas_call x1, Pallas kernels, update_call(): pl.pallas_call(update_kernel, grid=(BOX // STEP_X,), in_specs=[VMEM_SPEC,...  33 us
    all_to_all x3, starting transfers between devices, exchange(): return lax.all_to_all(rows, 'by', split_axis=0, concat_axis=0, tiled=True)  25.4 us
    pallas_call x1, Pallas kernels, flux_call(): pl.pallas_call(functools.partial(flux_kernel, lanes_by=lanes_by), in_spec...  23 us
    pallas_call x1, Pallas kernels, solve_call(): pl.pallas_call(functools.partial(solve_kernel, count=count, lanes_by=lane...  16.1 us
    ppermute x2, waiting for transfers between devices, halo(): x_hi = lax.ppermute(jnp.concatenate([first, middle[0]], axis=0), 'bx', down)  11.6 us
    pallas_call x1, Pallas kernels, correct_call(): pl.pallas_call(correct_kernel, grid=(BOX // STEP_X,), in_specs=[SMEM_SPEC...  10.4 us
    ppermute x2, starting transfers between devices, halo(): x_lo = lax.ppermute(jnp.concatenate([last, middle[-1]], axis=0), 'bx', up)  10.1 us
    ppermute x2, starting transfers between devices, halo(): y_lo = lax.ppermute(edge(BOX - SIDE), 'by', y_up)  6.76 us
  transfers between devices with their start and end apart: 13, of which 10 were waited for; matrix products, arithmetic and copies ran while one was open for 1% of the time, Pallas kernels for 32%

profile of v4, /device:TPU:98, one launch (start us, length us, event | category | flops | bytes accessed | tf_op | source)
XLA Modules:
  0.0 180.3 jit_solution(9918810151358523066)
XLA Ops:
  0.6 0.8 copy.9
  1.4 0.6 reshape_squeeze.3.table
  2.0 6.6 %volume_rows.1 = f32[16,256,128]{2,1,0:T(8,128)} custom-call(s32[64]{0:T(128)} %reshape_squeeze.3.table, s32[1]{0:T(128)} %bitcast.3.own, s32[8,39304]{1,0:T(8,128)} %fraction.3), custom_call_target="tpu_custom_call" | custom-call | tf_op jit(solution)/shard_map/volume_rows/pallas_call | solution.py:358
  8.6 0.0 copy-start.4
  8.6 0.0 copy-start.3
  8.6 7.5 %all-to-all-start.1 = ((f32[16,256,128]{2,1,0:T(8,128)}), f32[16,256,128]{2,1,0:T(8,128)S(1)}, u32[]{:S(2)}, u32[]{:S(2)}) async-start(f32[16,256,128]{2,1,0:T(8,128)} %volume_rows.1), calls=%async_computation.1 | async-start | bytes 4194304 | tf_op jit(solution)/shard_map/all_to_all | solution.py:873
  16.1 0.0 copy-done.4
  16.1 0.1 fusion
  16.2 0.1 reduce_window_sum.11
  16.3 0.2 select_reduce_fusion
  16.5 0.1 reshape.57
  16.5 0.1 copy.10
  16.6 0.0 copy-done.3
  16.6 0.5 select_reduce_fusion.3.slots
  17.2 23.0 %flux_rows.1 = (f32[34,8,1280]{2,1,0:T(8,128)}, f32[34,3,8,1280]{3,2,1,0:T(8,128)}, f32[16,256,128]{2,1,0:T(8,128)}) custom-call(s32[16]{0:T(128)} %select_reduce_fusion.3.slots, f32[3,8,39304]{2,1,0:T(8,128)} %bitcast.30, s32[8,39304]{1,0:T(8,128)} %fraction.3), custom_call_target="tpu_custom_call" | custom-call | tf_op jit(solution)/shard_map/flux_rows/pallas_call | solution.py:375
  40.1 3.1 %all-to-all-done.1.refs_0_.refs_1_.refs_2_.refs_3_ = f32[16,256,128]{2,1,0:T(8,128)S(1)} async-done(((f32[16,256,128]{2,1,0:T(8,128)}), f32[16,256,128]{2,1,0:T(8,128)S(1)}, u32[]{:S(2)}, u32[]{:S(2)}) %all-to-all-start.1) | async-done | bytes 2097184 | tf_op jit(solution)/shard_map/all_to_all | solution.py:873
  43.2 0.0 copy-start
  43.2 1.3 copy-done
  44.6 8.3 %all-to-all-start = ((f32[16,256,128]{2,1,0:T(8,128)}), f32[16,256,128]{2,1,0:T(8,128)S(1)}, u32[]{:S(2)}, u32[]{:S(2)}) async-start(f32[16,256,128]{2,1,0:T(8,128)} %get-tuple-element.28), calls=%async_computation | async-start | bytes 4194304 | tf_op jit(solution)/shard_map/all_to_all | solution.py:873
  52.8 0.2 dynamic-slice_reduce_fusion.table
  53.0 0.0 copy-start.1
  53.0 1.6 copy-done.1
  54.6 1.6 brick.2
  56.2 0.1 collective-permute-start
  56.4 1.2 collective-permute-done.refs_3_
  57.5 5.0 %collective-permute-start.1 = (f32[192,128]{1,0:T(8,128)S(1)}, f32[192,128]{1,0:T(8,128)S(1)}, u32[]{:S(2)}, u32[]{:S(2)}) collective-permute-start(f32[192,128]{1,0:T(8,128)S(1)} %pad_maximum_fusion.4), channel_id=1, source_target_pairs={{0,32},{32,64},{64,96},{96,128},{128,160},{160,192},{192,224},{1,3... | collective-permute-start | bytes 294920 | tf_op jit(solution)/shard_map/ppermute | solution.py:810
  62.6 1.9 %collective-permute-start.2 = (f32[192,128]{1,0:T(8,128)S(1)}, f32[192,128]{1,0:T(8,128)S(1)}, u32[]{:S(2)}, u32[]{:S(2)}) collective-permute-start(f32[192,128]{1,0:T(8,128)S(1)} %pad_maximum_fusion.5), channel_id=1, source_target_pairs={{32,0},{64,32},{96,64},{128,96},{160,128},{192,160},{224,192},{33,... | collective-permute-start | bytes 294920 | tf_op jit(solution)/shard_map/ppermute | solution.py:811
  64.5 5.8 %collective-permute-done.2.refs_2_ = f32[192,128]{1,0:T(8,128)S(1)} collective-permute-done((f32[192,128]{1,0:T(8,128)S(1)}, f32[192,128]{1,0:T(8,128)S(1)}, u32[]{:S(2)}, u32[]{:S(2)}) %collective-permute-start.2) | collective-permute-done | bytes 98336 | tf_op jit(solution)/shard_map/ppermute | solution.py:811
  70.3 0.0 collective-permute-done.1.refs_1_
  70.4 3.4 %collective-permute-start.3 = (f32[46,8,128]{2,1,0:T(8,128)S(1)}, f32[46,8,128]{2,1,0:T(8,128)S(1)}, u32[]{:S(2)}, u32[]{:S(2)}) collective-permute-start(f32[46,8,128]{2,1,0:T(8,128)S(1)} %pad_maximum_fusion), channel_id=1, source_target_pairs={{0,2},{2,4},{4,6},{6,8},{8,10},{10,12},{12,14},{14,16},{16,18},{18... | collective-permute-start | bytes 565256 | tf_op jit(solution)/shard_map/ppermute | solution.py:818
  73.8 0.7 pad_maximum_fusion.1
  74.4 2.5 %collective-permute-start.4 = (f32[46,8,128]{2,1,0:T(8,128)}, f32[46,8,128]{2,1,0:T(8,128)S(1)}, u32[]{:S(2)}, u32[]{:S(2)}) collective-permute-start(f32[46,8,128]{2,1,0:T(8,128)} %pad_maximum_fusion.1), channel_id=1, source_target_pairs={{2,0},{4,2},{6,4},{8,6},{10,8},{12,10},{14,12},{16,14},{18,16},{20... | collective-permute-start | bytes 565256 | tf_op jit(solution)/shard_map/ppermute | solution.py:819
  76.9 2.7 %all-to-all-done.refs_0_.refs_1_.refs_2_.refs_3_ = f32[16,256,128]{2,1,0:T(8,128)S(1)} async-done(((f32[16,256,128]{2,1,0:T(8,128)}), f32[16,256,128]{2,1,0:T(8,128)S(1)}, u32[]{:S(2)}, u32[]{:S(2)}) %all-to-all-start) | async-done | bytes 2097184 | tf_op jit(solution)/shard_map/all_to_all | solution.py:873
  79.6 2.3 %collective-permute-done.3.refs_4_ = f32[46,8,128]{2,1,0:T(8,128)S(1)} collective-permute-done((f32[46,8,128]{2,1,0:T(8,128)S(1)}, f32[46,8,128]{2,1,0:T(8,128)S(1)}, u32[]{:S(2)}, u32[]{:S(2)}) %collective-permute-start.3) | collective-permute-done | bytes 188448 | tf_op jit(solution)/shard_map/ppermute | solution.py:818
  81.9 1.0 collective-permute-done.4.refs_5_
  82.9 1.6 brick.3
  84.5 0.1 collective-permute-start.5
  84.6 1.2 collective-permute-done.5.refs_9_
  85.8 5.0 %collective-permute-start.6 = (f32[192,128]{1,0:T(8,128)S(1)}, f32[192,128]{1,0:T(8,128)S(1)}, u32[]{:S(2)}, u32[]{:S(2)}) collective-permute-start(f32[192,128]{1,0:T(8,128)S(1)} %pad_maximum_fusion.6), channel_id=1, source_target_pairs={{0,32},{32,64},{64,96},{96,128},{128,160},{160,192},{192,224},{1,3... | collective-permute-start | bytes 294920 | tf_op jit(solution)/shard_map/ppermute | solution.py:810
  90.9 1.9 %collective-permute-start.7 = (f32[192,128]{1,0:T(8,128)S(1)}, f32[192,128]{1,0:T(8,128)S(1)}, u32[]{:S(2)}, u32[]{:S(2)}) collective-permute-start(f32[192,128]{1,0:T(8,128)S(1)} %pad_maximum_fusion.7), channel_id=1, source_target_pairs={{32,0},{64,32},{96,64},{128,96},{160,128},{192,160},{224,192},{33,... | collective-permute-start | bytes 294920 | tf_op jit(solution)/shard_map/ppermute | solution.py:811
  92.8 5.8 %collective-permute-done.7.refs_8_ = f32[192,128]{1,0:T(8,128)S(1)} collective-permute-done((f32[192,128]{1,0:T(8,128)S(1)}, f32[192,128]{1,0:T(8,128)S(1)}, u32[]{:S(2)}, u32[]{:S(2)}) %collective-permute-start.7) | collective-permute-done | bytes 98336 | tf_op jit(solution)/shard_map/ppermute | solution.py:811
  98.6 0.0 collective-permute-done.6.refs_7_
  98.6 3.4 %collective-permute-start.8 = (f32[46,8,128]{2,1,0:T(8,128)S(1)}, f32[46,8,128]{2,1,0:T(8,128)S(1)}, u32[]{:S(2)}, u32[]{:S(2)}) collective-permute-start(f32[46,8,128]{2,1,0:T(8,128)S(1)} %pad_maximum_fusion.2), channel_id=1, source_target_pairs={{0,2},{2,4},{4,6},{6,8},{8,10},{10,12},{12,14},{14,16},{16,18},{18... | collective-permute-start | bytes 565256 | tf_op jit(solution)/shard_map/ppermute | solution.py:818
  102.1 2.5 %collective-permute-start.9 = (f32[46,8,128]{2,1,0:T(8,128)S(1)}, f32[46,8,128]{2,1,0:T(8,128)S(1)}, u32[]{:S(2)}, u32[]{:S(2)}) collective-permute-start(f32[46,8,128]{2,1,0:T(8,128)S(1)} %pad_maximum_fusion.3), channel_id=1, source_target_pairs={{2,0},{4,2},{6,4},{8,6},{10,8},{12,10},{14,12},{16,14},{18,16},{20... | collective-permute-start | bytes 565256 | tf_op jit(solution)/shard_map/ppermute | solution.py:819
  104.5 0.1 select_reduce_fusion.2.box_of_row
  104.6 1.5 collective-permute-done.8.refs_10_
  106.1 3.4 %collective-permute-done.9.refs_11_ = f32[46,8,128]{2,1,0:T(8,128)S(1)} collective-permute-done((f32[46,8,128]{2,1,0:T(8,128)S(1)}, f32[46,8,128]{2,1,0:T(8,128)S(1)}, u32[]{:S(2)}, u32[]{:S(2)}) %collective-permute-start.9) | collective-permute-done | bytes 188448 | tf_op jit(solution)/shard_map/ppermute | solution.py:819
  109.5 16.1 %solve.1 = (f32[32,32,128]{2,1,0:T(8,128)}, f32[16,304,128]{2,1,0:T(8,128)S(1)}) custom-call(s32[16]{0:T(128)S(1)} %select_reduce_fusion.2.box_of_row, s32[1]{0:T(128)} %bitcast.2.side, f32[1024,128]{1,0:T(8,128)S(1)} %get-tuple-element.33.refs_0_, f32[192,128]{1,0:T(8,128)S(1)} %collective-permute-done.1.refs_1_, ...), custom_call_target="tpu_custom_call" | custom-call | tf_op jit(solution)/shard_map/solve/pallas_call | solution.py:827
  125.7 0.0 copy-start.2
  125.7 1.4 copy-done.2
  127.1 9.7 %all-to-all-start.2 = ((f32[16,304,128]{2,1,0:T(8,128)}), f32[16,304,128]{2,1,0:T(8,128)S(1)}, u32[]{:S(2)}, u32[]{:S(2)}) async-start(f32[16,304,128]{2,1,0:T(8,128)} %copy-done.2), calls=%async_computation.2 | async-start | bytes 4980736 | tf_op jit(solution)/shard_map/all_to_all | solution.py:873
  136.8 33.0 %updated.1 = (f32[32,3,8,1024]{3,2,1,0:T(8,128)}, f32[32,6,8,1024]{3,2,1,0:T(8,128)}) custom-call(f32[34,3,8,1280]{3,2,1,0:T(8,128)} %get-tuple-element.24.masses, f32[34,8,1280]{2,1,0:T(8,128)} %get-tuple-element.25.planes), custom_call_target="tpu_custom_call" | custom-call | tf_op jit(solution)/shard_map/updated/pallas_call | solution.py:396
  169.8 0.1 select_reduce_fusion.1.rows
  169.9 0.0 all-to-all-done.2.returned
  169.9 10.4 %corrected.1 = f32[3,8,32768]{2,1,0:T(8,128)} custom-call(s32[8]{0:T(128)S(1)} %select_reduce_fusion.1.rows, f32[32,3,8,1024]{3,2,1,0:T(8,128)} %get-tuple-element.26.updated, f32[32,6,8,1024]{3,2,1,0:T(8,128)} %get-tuple-element.27.apertures, f32[16,304,128]{2,1,0:T(8,128)S(1)} %all-to-all-done.2.returned), custom_call_target="tpu_custom_call" | custom-call | tf_op jit(solution)/shard_map/corrected/pallas_call | solution.py:410
  (19 shorter events, 0.2 us)
Async XLA Ops:
  8.6 7.5 %copy-start.4 = (s32[64]{0:T(128)S(1)}, s32[64]{0:T(128)}, u32[]{:S(2)}) copy-start(s32[64]{0:T(128)} %reshape_squeeze.3.table) | copy-start | bytes 772
  8.6 8.0 %copy-start.3 = (s32[1,16,1,4]{1,3,2,0:T(4,128)S(1)}, s32[1,16,1,4]{1,3,2,0:T(4,128)}, u32[]{:S(2)}) copy-start(s32[1,16,1,4]{1,3,2,0:T(4,128)} %param.5) | copy-start | bytes 772
  8.6 34.6 %all-to-all-start.1 = ((f32[16,256,128]{2,1,0:T(8,128)}), f32[16,256,128]{2,1,0:T(8,128)S(1)}, u32[]{:S(2)}, u32[]{:S(2)}) async-start(f32[16,256,128]{2,1,0:T(8,128)} %volume_rows.1), calls=%async_computation.1 | async-start | bytes 4194304 | tf_op jit(solution)/shard_map/all_to_all | solution.py:873
  43.2 1.3 copy-start
  44.6 35.0 %all-to-all-start = ((f32[16,256,128]{2,1,0:T(8,128)}), f32[16,256,128]{2,1,0:T(8,128)S(1)}, u32[]{:S(2)}, u32[]{:S(2)}) async-start(f32[16,256,128]{2,1,0:T(8,128)} %get-tuple-element.28), calls=%async_computation | async-start | bytes 4194304 | tf_op jit(solution)/shard_map/all_to_all | solution.py:873
  53.0 1.6 copy-start.1
  56.2 1.3 collective-permute-start
  57.5 12.8 %collective-permute-start.1 = (f32[192,128]{1,0:T(8,128)S(1)}, f32[192,128]{1,0:T(8,128)S(1)}, u32[]{:S(2)}, u32[]{:S(2)}) collective-permute-start(f32[192,128]{1,0:T(8,128)S(1)} %pad_maximum_fusion.4), channel_id=1, source_target_pairs={{0,32},{32,64},{64,96},{96,128},{128,160},{160,192},{192,224},{1,3... | collective-permute-start | bytes 294920 | tf_op jit(solution)/shard_map/ppermute | solution.py:810
  62.6 7.7 %collective-permute-start.2 = (f32[192,128]{1,0:T(8,128)S(1)}, f32[192,128]{1,0:T(8,128)S(1)}, u32[]{:S(2)}, u32[]{:S(2)}) collective-permute-start(f32[192,128]{1,0:T(8,128)S(1)} %pad_maximum_fusion.5), channel_id=1, source_target_pairs={{32,0},{64,32},{96,64},{128,96},{160,128},{192,160},{224,192},{33,... | collective-permute-start | bytes 294920 | tf_op jit(solution)/shard_map/ppermute | solution.py:811
  70.4 11.5 %collective-permute-start.3 = (f32[46,8,128]{2,1,0:T(8,128)S(1)}, f32[46,8,128]{2,1,0:T(8,128)S(1)}, u32[]{:S(2)}, u32[]{:S(2)}) collective-permute-start(f32[46,8,128]{2,1,0:T(8,128)S(1)} %pad_maximum_fusion), channel_id=1, source_target_pairs={{0,2},{2,4},{4,6},{6,8},{8,10},{10,12},{12,14},{14,16},{16,18},{18... | collective-permute-start | bytes 565256 | tf_op jit(solution)/shard_map/ppermute | solution.py:818
  74.4 8.4 %collective-permute-start.4 = (f32[46,8,128]{2,1,0:T(8,128)}, f32[46,8,128]{2,1,0:T(8,128)S(1)}, u32[]{:S(2)}, u32[]{:S(2)}) collective-permute-start(f32[46,8,128]{2,1,0:T(8,128)} %pad_maximum_fusion.1), channel_id=1, source_target_pairs={{2,0},{4,2},{6,4},{8,6},{10,8},{12,10},{14,12},{16,14},{18,16},{20... | collective-permute-start | bytes 565256 | tf_op jit(solution)/shard_map/ppermute | solution.py:819
  84.5 1.3 collective-permute-start.5
  85.8 12.8 %collective-permute-start.6 = (f32[192,128]{1,0:T(8,128)S(1)}, f32[192,128]{1,0:T(8,128)S(1)}, u32[]{:S(2)}, u32[]{:S(2)}) collective-permute-start(f32[192,128]{1,0:T(8,128)S(1)} %pad_maximum_fusion.6), channel_id=1, source_target_pairs={{0,32},{32,64},{64,96},{96,128},{128,160},{160,192},{192,224},{1,3... | collective-permute-start | bytes 294920 | tf_op jit(solution)/shard_map/ppermute | solution.py:810
  90.9 7.7 %collective-permute-start.7 = (f32[192,128]{1,0:T(8,128)S(1)}, f32[192,128]{1,0:T(8,128)S(1)}, u32[]{:S(2)}, u32[]{:S(2)}) collective-permute-start(f32[192,128]{1,0:T(8,128)S(1)} %pad_maximum_fusion.7), channel_id=1, source_target_pairs={{32,0},{64,32},{96,64},{128,96},{160,128},{192,160},{224,192},{33,... | collective-permute-start | bytes 294920 | tf_op jit(solution)/shard_map/ppermute | solution.py:811
  98.6 7.5 %collective-permute-start.8 = (f32[46,8,128]{2,1,0:T(8,128)S(1)}, f32[46,8,128]{2,1,0:T(8,128)S(1)}, u32[]{:S(2)}, u32[]{:S(2)}) collective-permute-start(f32[46,8,128]{2,1,0:T(8,128)S(1)} %pad_maximum_fusion.2), channel_id=1, source_target_pairs={{0,2},{2,4},{4,6},{6,8},{8,10},{10,12},{12,14},{14,16},{16,18},{18... | collective-permute-start | bytes 565256 | tf_op jit(solution)/shard_map/ppermute | solution.py:818
  102.1 7.5 %collective-permute-start.9 = (f32[46,8,128]{2,1,0:T(8,128)S(1)}, f32[46,8,128]{2,1,0:T(8,128)S(1)}, u32[]{:S(2)}, u32[]{:S(2)}) collective-permute-start(f32[46,8,128]{2,1,0:T(8,128)S(1)} %pad_maximum_fusion.3), channel_id=1, source_target_pairs={{2,0},{4,2},{6,4},{8,6},{10,8},{12,10},{14,12},{16,14},{18,16},{20... | collective-permute-start | bytes 565256 | tf_op jit(solution)/shard_map/ppermute | solution.py:819
  125.7 1.5 copy-start.2
  127.1 42.8 %all-to-all-start.2 = ((f32[16,304,128]{2,1,0:T(8,128)}), f32[16,304,128]{2,1,0:T(8,128)S(1)}, u32[]{:S(2)}, u32[]{:S(2)}) async-start(f32[16,304,128]{2,1,0:T(8,128)} %copy-done.2), calls=%async_computation.2 | async-start | bytes 4980736 | tf_op jit(solution)/shard_map/all_to_all | solution.py:873

commit v5 on v4

--- a/solution.py
+++ b/solution.py
@@ -525,14 +525,22 @@
     def strip_base(g):
         return g * ROWS_Y + 8
 
-    def fill(ext, strips, parts):
+    def fill(ext, strips, parts, depth):
         brick, x_lo, x_hi, middle, y_lo, y_hi = parts
         own = HALO + 1 + BOX
         after = own + GROUPS - 2
 
         def rows_of(x, source):
-            ext[pl.ds(base(x), SIDE), :] = y_lo[source]
-            ext[pl.ds(base(x) + SIDE + BOX, SIDE), :] = y_hi[source]
+            ext[pl.ds(base(x), SIDE), :] = low_rows(source)
+            ext[pl.ds(base(x) + SIDE + BOX, SIDE), :] = high_rows(source)
+
+        rest = jnp.zeros((SIDE - depth, TILE), jnp.float32) if depth < SIDE else None
+
+        def low_rows(source):
+            return y_lo[source] if rest is None else jnp.concatenate([rest, y_lo[source]], axis=0)
+
+        def high_rows(source):
+            return y_hi[source] if rest is None else jnp.concatenate([y_hi[source], rest], axis=0)
 
         def body(i):
             ext[pl.ds(base(i + HALO) + SIDE, BOX), :] = brick[pl.ds(pl.multiple_of(i * BOX, 8), BOX), :]
@@ -548,12 +556,12 @@
         sources = [HALO] + [own + g for g in range(GROUPS - 2)] + [after + HALO]
         for g, (piece, source) in enumerate(zip(pieces, sources)):
             start = strip_base(g)
-            strips[start : start + SIDE, :] = y_lo[source]
+            strips[start : start + SIDE, :] = low_rows(source)
             strips[start + SIDE : start + SIDE + BOX, :] = piece
-            strips[start + SIDE + BOX : start + ROWS_Y, :] = y_hi[source]
-
-    fill(vol, hvol, volume_in)
-    fill(res, hres, source_in)
+            strips[start + SIDE + BOX : start + ROWS_Y, :] = high_rows(source)
+
+    fill(vol, hvol, volume_in, SIDE)
+    fill(res, hres, source_in, ITERS)
     guard = jnp.zeros((8, TILE), jnp.float32)
     for ref in (hvol, hsa, hsb):
         ref[0:8, :] = guard
@@ -800,7 +808,7 @@
     )(table, side, *([recv] * count))
 
 
-def halo(parts):
+def halo(parts, depth):
     brick, first, last, strip = parts
     nx, ny = lax.axis_size("bx"), lax.axis_size("by")
     nz = lax.axis_size("bz")
@@ -812,10 +820,10 @@
     cubes = [v.reshape(-1, BOX, TILE) for v in (x_lo, brick, middle, x_hi)]
 
     def edge(start):
-        return jnp.concatenate([v[:, start : start + SIDE] for v in cubes], axis=0)
+        return jnp.concatenate([v[:, start : start + depth] for v in cubes], axis=0)
 
     y_up = [(i, i + 1) for i in range(ny - 1)]
-    y_lo = lax.ppermute(edge(BOX - SIDE), "by", y_up)
+    y_lo = lax.ppermute(edge(BOX - depth), "by", y_up)
     y_hi = lax.ppermute(edge(0), "by", [(j, i) for i, j in y_up])
     return brick, x_lo, x_hi, middle, y_lo, y_hi
 
@@ -883,9 +891,9 @@
     source_recv = exchange(source_rows)
     updated, apertures = update_call(masses, planes)
     side = lax.axis_index("bz").reshape(1)
-    volume = halo(assemble_call(brick_table, side, volume_recv))
+    volume = halo(assemble_call(brick_table, side, volume_recv), SIDE)
     source_recv, volume = lax.optimization_barrier((source_recv, volume))
-    source = halo(assemble_call(brick_table, side, source_recv))
+    source = halo(assemble_call(brick_table, side, source_recv), ITERS)
     pressure, rows = solve_call(box_of_row, side, placement.shape[3], volume, source)
     returned = exchange(rows)
     corrected = correct_call(slot_row, updated, apertures, returned)

time: 181 us -> 180 us (level)
  no operation moved by 1% of the time
where the time goes in v5:
time: 180 us; the launch traced here: 179 us
  Pallas kernels  92.3 us (51%)
  starting transfers between devices  51.2 us (28%)
  waiting for transfers between devices  26.8 us (15%)
  local copies, waits for them, and re-layouts  6.19 us (3%)
  other arithmetic  1.89 us (1%)
    pallas_call x1, Pallas kernels, update_call(): pl.pallas_call(update_kernel, grid=(BOX // STEP_X,), in_specs=[VMEM_SPEC,...  33 us
    all_to_all x3, starting transfers between devices, exchange(): return lax.all_to_all(rows, 'by', split_axis=0, concat_axis=0, tiled=True)  25.4 us
    pallas_call x1, Pallas kernels, flux_call(): pl.pallas_call(functools.partial(flux_kernel, lanes_by=lanes_by), in_spec...  23 us
    pallas_call x1, Pallas kernels, solve_call(): pl.pallas_call(functools.partial(solve_kernel, count=count, lanes_by=lane...  16.1 us
    ppermute x2, waiting for transfers between devices, halo(): x_hi = lax.ppermute(jnp.concatenate([first, middle[0]], axis=0), 'bx', down)  11.6 us
    pallas_call x1, Pallas kernels, correct_call(): pl.pallas_call(correct_kernel, grid=(BOX // STEP_X,), in_specs=[SMEM_SPEC...  10.4 us
    ppermute x2, starting transfers between devices, halo(): x_lo = lax.ppermute(jnp.concatenate([last, middle[-1]], axis=0), 'bx', up)  10.1 us
    ppermute x2, starting transfers between devices, halo(): y_lo = lax.ppermute(edge(BOX - depth), 'by', y_up)  6.76 us
  transfers between devices with their start and end apart: 13, of which 10 were waited for; matrix products, arithmetic and copies ran while one was open for 1% of the time, Pallas kernels for 32%

profile of v5, /device:TPU:98, one launch (start us, length us, event | category | flops | bytes accessed | tf_op | source)
XLA Modules:
  0.0 179.3 jit_solution(1737894957925924336)
XLA Ops:
  0.6 0.8 copy.9
  1.4 0.6 reshape_squeeze.3.table
  2.0 6.6 %volume_rows.1 = f32[16,256,128]{2,1,0:T(8,128)} custom-call(s32[64]{0:T(128)} %reshape_squeeze.3.table, s32[1]{0:T(128)} %bitcast.3.own, s32[8,39304]{1,0:T(8,128)} %fraction.3), custom_call_target="tpu_custom_call" | custom-call | tf_op jit(solution)/shard_map/volume_rows/pallas_call | solution.py:358
  8.6 0.0 copy-start.4
  8.6 0.0 copy-start.3
  8.6 7.5 %all-to-all-start.1 = ((f32[16,256,128]{2,1,0:T(8,128)}), f32[16,256,128]{2,1,0:T(8,128)S(1)}, u32[]{:S(2)}, u32[]{:S(2)}) async-start(f32[16,256,128]{2,1,0:T(8,128)} %volume_rows.1), calls=%async_computation.1 | async-start | bytes 4194304 | tf_op jit(solution)/shard_map/all_to_all | solution.py:881
  16.1 0.0 copy-done.4
  16.1 0.1 fusion
  16.2 0.1 reduce_window_sum.11
  16.3 0.2 select_reduce_fusion
  16.5 0.1 reshape.57
  16.5 0.1 copy.10
  16.6 0.0 copy-done.3
  16.6 0.5 select_reduce_fusion.3.slots
  17.2 23.0 %flux_rows.1 = (f32[34,8,1280]{2,1,0:T(8,128)}, f32[34,3,8,1280]{3,2,1,0:T(8,128)}, f32[16,256,128]{2,1,0:T(8,128)}) custom-call(s32[16]{0:T(128)} %select_reduce_fusion.3.slots, f32[3,8,39304]{2,1,0:T(8,128)} %bitcast.30, s32[8,39304]{1,0:T(8,128)} %fraction.3), custom_call_target="tpu_custom_call" | custom-call | tf_op jit(solution)/shard_map/flux_rows/pallas_call | solution.py:375
  40.1 3.1 %all-to-all-done.1.refs_0_.refs_1_.refs_2_.refs_3_ = f32[16,256,128]{2,1,0:T(8,128)S(1)} async-done(((f32[16,256,128]{2,1,0:T(8,128)}), f32[16,256,128]{2,1,0:T(8,128)S(1)}, u32[]{:S(2)}, u32[]{:S(2)}) %all-to-all-start.1) | async-done | bytes 2097184 | tf_op jit(solution)/shard_map/all_to_all | solution.py:881
  43.2 0.0 copy-start
  43.2 1.3 copy-done
  44.6 8.3 %all-to-all-start = ((f32[16,256,128]{2,1,0:T(8,128)}), f32[16,256,128]{2,1,0:T(8,128)S(1)}, u32[]{:S(2)}, u32[]{:S(2)}) async-start(f32[16,256,128]{2,1,0:T(8,128)} %get-tuple-element.28), calls=%async_computation | async-start | bytes 4194304 | tf_op jit(solution)/shard_map/all_to_all | solution.py:881
  52.8 0.2 dynamic-slice_reduce_fusion.table
  53.0 0.0 copy-start.1
  53.0 1.6 copy-done.1
  54.6 1.6 brick.2
  56.2 0.1 collective-permute-start
  56.4 1.2 collective-permute-done.refs_3_
  57.5 5.0 %collective-permute-start.1 = (f32[192,128]{1,0:T(8,128)S(1)}, f32[192,128]{1,0:T(8,128)S(1)}, u32[]{:S(2)}, u32[]{:S(2)}) collective-permute-start(f32[192,128]{1,0:T(8,128)S(1)} %pad_maximum_fusion.2), channel_id=1, source_target_pairs={{0,32},{32,64},{64,96},{96,128},{128,160},{160,192},{192,224},{1,3... | collective-permute-start | bytes 294920 | tf_op jit(solution)/shard_map/ppermute | solution.py:818
  62.6 1.9 %collective-permute-start.2 = (f32[192,128]{1,0:T(8,128)S(1)}, f32[192,128]{1,0:T(8,128)S(1)}, u32[]{:S(2)}, u32[]{:S(2)}) collective-permute-start(f32[192,128]{1,0:T(8,128)S(1)} %pad_maximum_fusion.3), channel_id=1, source_target_pairs={{32,0},{64,32},{96,64},{128,96},{160,128},{192,160},{224,192},{33,... | collective-permute-start | bytes 294920 | tf_op jit(solution)/shard_map/ppermute | solution.py:819
  64.5 5.8 %collective-permute-done.2.refs_2_ = f32[192,128]{1,0:T(8,128)S(1)} collective-permute-done((f32[192,128]{1,0:T(8,128)S(1)}, f32[192,128]{1,0:T(8,128)S(1)}, u32[]{:S(2)}, u32[]{:S(2)}) %collective-permute-start.2) | collective-permute-done | bytes 98336 | tf_op jit(solution)/shard_map/ppermute | solution.py:819
  70.3 0.0 collective-permute-done.1.refs_1_
  70.4 3.4 %collective-permute-start.3 = (f32[46,8,128]{2,1,0:T(8,128)S(1)}, f32[46,8,128]{2,1,0:T(8,128)S(1)}, u32[]{:S(2)}, u32[]{:S(2)}) collective-permute-start(f32[46,8,128]{2,1,0:T(8,128)S(1)} %pad_maximum_fusion), channel_id=1, source_target_pairs={{0,2},{2,4},{4,6},{6,8},{8,10},{10,12},{12,14},{14,16},{16,18},{18... | collective-permute-start | bytes 565256 | tf_op jit(solution)/shard_map/ppermute | solution.py:826
  73.8 0.7 pad_maximum_fusion.1
  74.4 2.5 %collective-permute-start.4 = (f32[46,8,128]{2,1,0:T(8,128)}, f32[46,8,128]{2,1,0:T(8,128)S(1)}, u32[]{:S(2)}, u32[]{:S(2)}) collective-permute-start(f32[46,8,128]{2,1,0:T(8,128)} %pad_maximum_fusion.1), channel_id=1, source_target_pairs={{2,0},{4,2},{6,4},{8,6},{10,8},{12,10},{14,12},{16,14},{18,16},{20... | collective-permute-start | bytes 565256 | tf_op jit(solution)/shard_map/ppermute | solution.py:827
  76.9 2.7 %all-to-all-done.refs_0_.refs_1_.refs_2_.refs_3_ = f32[16,256,128]{2,1,0:T(8,128)S(1)} async-done(((f32[16,256,128]{2,1,0:T(8,128)}), f32[16,256,128]{2,1,0:T(8,128)S(1)}, u32[]{:S(2)}, u32[]{:S(2)}) %all-to-all-start) | async-done | bytes 2097184 | tf_op jit(solution)/shard_map/all_to_all | solution.py:881
  79.6 2.3 %collective-permute-done.3.refs_4_ = f32[46,8,128]{2,1,0:T(8,128)S(1)} collective-permute-done((f32[46,8,128]{2,1,0:T(8,128)S(1)}, f32[46,8,128]{2,1,0:T(8,128)S(1)}, u32[]{:S(2)}, u32[]{:S(2)}) %collective-permute-start.3) | collective-permute-done | bytes 188448 | tf_op jit(solution)/shard_map/ppermute | solution.py:826
  81.9 1.0 collective-permute-done.4.refs_5_
  82.9 1.6 brick.3
  84.5 0.1 collective-permute-start.5
  84.6 1.2 collective-permute-done.5.refs_9_
  85.8 5.0 %collective-permute-start.6 = (f32[192,128]{1,0:T(8,128)S(1)}, f32[192,128]{1,0:T(8,128)S(1)}, u32[]{:S(2)}, u32[]{:S(2)}) collective-permute-start(f32[192,128]{1,0:T(8,128)S(1)} %pad_maximum_fusion.4), channel_id=1, source_target_pairs={{0,32},{32,64},{64,96},{96,128},{128,160},{160,192},{192,224},{1,3... | collective-permute-start | bytes 294920 | tf_op jit(solution)/shard_map/ppermute | solution.py:818
  90.9 1.9 %collective-permute-start.7 = (f32[192,128]{1,0:T(8,128)S(1)}, f32[192,128]{1,0:T(8,128)S(1)}, u32[]{:S(2)}, u32[]{:S(2)}) collective-permute-start(f32[192,128]{1,0:T(8,128)S(1)} %pad_maximum_fusion.5), channel_id=1, source_target_pairs={{32,0},{64,32},{96,64},{128,96},{160,128},{192,160},{224,192},{33,... | collective-permute-start | bytes 294920 | tf_op jit(solution)/shard_map/ppermute | solution.py:819
  92.8 5.8 %collective-permute-done.7.refs_8_ = f32[192,128]{1,0:T(8,128)S(1)} collective-permute-done((f32[192,128]{1,0:T(8,128)S(1)}, f32[192,128]{1,0:T(8,128)S(1)}, u32[]{:S(2)}, u32[]{:S(2)}) %collective-permute-start.7) | collective-permute-done | bytes 98336 | tf_op jit(solution)/shard_map/ppermute | solution.py:819
  98.6 0.0 collective-permute-done.6.refs_7_
  98.7 3.4 %collective-permute-start.8 = (f32[46,4,128]{2,1,0:T(4,128)S(1)}, f32[46,4,128]{2,1,0:T(4,128)S(1)}, u32[]{:S(2)}, u32[]{:S(2)}) collective-permute-start(f32[46,4,128]{2,1,0:T(4,128)S(1)} %pad_maximum_fusion.6), channel_id=1, source_target_pairs={{0,2},{2,4},{4,6},{6,8},{8,10},{10,12},{12,14},{14,16},{16,18},{18... | collective-permute-start | bytes 282632 | tf_op jit(solution)/shard_map/ppermute | solution.py:826
  102.1 2.5 %collective-permute-start.9 = (f32[46,4,128]{2,1,0:T(4,128)S(1)}, f32[46,4,128]{2,1,0:T(4,128)S(1)}, u32[]{:S(2)}, u32[]{:S(2)}) collective-permute-start(f32[46,4,128]{2,1,0:T(4,128)S(1)} %pad_maximum_fusion.7), channel_id=1, source_target_pairs={{2,0},{4,2},{6,4},{8,6},{10,8},{12,10},{14,12},{16,14},{18,16},{20... | collective-permute-start | bytes 282632 | tf_op jit(solution)/shard_map/ppermute | solution.py:827
  104.5 0.1 select_reduce_fusion.2.box_of_row
  104.6 0.5 collective-permute-done.8.refs_10_
  105.1 3.4 %collective-permute-done.9.refs_11_ = f32[46,4,128]{2,1,0:T(4,128)S(1)} collective-permute-done((f32[46,4,128]{2,1,0:T(4,128)S(1)}, f32[46,4,128]{2,1,0:T(4,128)S(1)}, u32[]{:S(2)}, u32[]{:S(2)}) %collective-permute-start.9) | collective-permute-done | bytes 94240 | tf_op jit(solution)/shard_map/ppermute | solution.py:827
  108.5 16.1 %solve.1 = (f32[32,32,128]{2,1,0:T(8,128)}, f32[16,304,128]{2,1,0:T(8,128)S(1)}) custom-call(s32[16]{0:T(128)S(1)} %select_reduce_fusion.2.box_of_row, s32[1]{0:T(128)} %bitcast.2.side, f32[1024,128]{1,0:T(8,128)S(1)} %get-tuple-element.33.refs_0_, f32[192,128]{1,0:T(8,128)S(1)} %collective-permute-done.1.refs_1_, ...), custom_call_target="tpu_custom_call" | custom-call | tf_op jit(solution)/shard_map/solve/pallas_call | solution.py:835
  124.7 0.0 copy-start.2
  124.7 1.4 copy-done.2
  126.1 9.7 %all-to-all-start.2 = ((f32[16,304,128]{2,1,0:T(8,128)}), f32[16,304,128]{2,1,0:T(8,128)S(1)}, u32[]{:S(2)}, u32[]{:S(2)}) async-start(f32[16,304,128]{2,1,0:T(8,128)} %copy-done.2), calls=%async_computation.2 | async-start | bytes 4980736 | tf_op jit(solution)/shard_map/all_to_all | solution.py:881
  135.8 33.0 %updated.1 = (f32[32,3,8,1024]{3,2,1,0:T(8,128)}, f32[32,6,8,1024]{3,2,1,0:T(8,128)}) custom-call(f32[34,3,8,1280]{3,2,1,0:T(8,128)} %get-tuple-element.24.masses, f32[34,8,1280]{2,1,0:T(8,128)} %get-tuple-element.25.planes), custom_call_target="tpu_custom_call" | custom-call | tf_op jit(solution)/shard_map/updated/pallas_call | solution.py:396
  168.8 0.1 select_reduce_fusion.1.rows
  168.9 0.0 all-to-all-done.2.returned
  169.0 10.4 %corrected.1 = f32[3,8,32768]{2,1,0:T(8,128)} custom-call(s32[8]{0:T(128)S(1)} %select_reduce_fusion.1.rows, f32[32,3,8,1024]{3,2,1,0:T(8,128)} %get-tuple-element.26.updated, f32[32,6,8,1024]{3,2,1,0:T(8,128)} %get-tuple-element.27.apertures, f32[16,304,128]{2,1,0:T(8,128)S(1)} %all-to-all-done.2.returned), custom_call_target="tpu_custom_call" | custom-call | tf_op jit(solution)/shard_map/corrected/pallas_call | solution.py:410
  (19 shorter events, 0.2 us)
Async XLA Ops:
  8.6 7.5 %copy-start.4 = (s32[64]{0:T(128)S(1)}, s32[64]{0:T(128)}, u32[]{:S(2)}) copy-start(s32[64]{0:T(128)} %reshape_squeeze.3.table) | copy-start | bytes 772
  8.6 8.0 %copy-start.3 = (s32[1,16,1,4]{1,3,2,0:T(4,128)S(1)}, s32[1,16,1,4]{1,3,2,0:T(4,128)}, u32[]{:S(2)}) copy-start(s32[1,16,1,4]{1,3,2,0:T(4,128)} %param.5) | copy-start | bytes 772
  8.6 34.6 %all-to-all-start.1 = ((f32[16,256,128]{2,1,0:T(8,128)}), f32[16,256,128]{2,1,0:T(8,128)S(1)}, u32[]{:S(2)}, u32[]{:S(2)}) async-start(f32[16,256,128]{2,1,0:T(8,128)} %volume_rows.1), calls=%async_computation.1 | async-start | bytes 4194304 | tf_op jit(solution)/shard_map/all_to_all | solution.py:881
  43.2 1.3 copy-start
  44.6 35.0 %all-to-all-start = ((f32[16,256,128]{2,1,0:T(8,128)}), f32[16,256,128]{2,1,0:T(8,128)S(1)}, u32[]{:S(2)}, u32[]{:S(2)}) async-start(f32[16,256,128]{2,1,0:T(8,128)} %get-tuple-element.28), calls=%async_computation | async-start | bytes 4194304 | tf_op jit(solution)/shard_map/all_to_all | solution.py:881
  53.0 1.6 copy-start.1
  56.2 1.3 collective-permute-start
  57.5 12.8 %collective-permute-start.1 = (f32[192,128]{1,0:T(8,128)S(1)}, f32[192,128]{1,0:T(8,128)S(1)}, u32[]{:S(2)}, u32[]{:S(2)}) collective-permute-start(f32[192,128]{1,0:T(8,128)S(1)} %pad_maximum_fusion.2), channel_id=1, source_target_pairs={{0,32},{32,64},{64,96},{96,128},{128,160},{160,192},{192,224},{1,3... | collective-permute-start | bytes 294920 | tf_op jit(solution)/shard_map/ppermute | solution.py:818
  62.6 7.7 %collective-permute-start.2 = (f32[192,128]{1,0:T(8,128)S(1)}, f32[192,128]{1,0:T(8,128)S(1)}, u32[]{:S(2)}, u32[]{:S(2)}) collective-permute-start(f32[192,128]{1,0:T(8,128)S(1)} %pad_maximum_fusion.3), channel_id=1, source_target_pairs={{32,0},{64,32},{96,64},{128,96},{160,128},{192,160},{224,192},{33,... | collective-permute-start | bytes 294920 | tf_op jit(solution)/shard_map/ppermute | solution.py:819
  70.4 11.5 %collective-permute-start.3 = (f32[46,8,128]{2,1,0:T(8,128)S(1)}, f32[46,8,128]{2,1,0:T(8,128)S(1)}, u32[]{:S(2)}, u32[]{:S(2)}) collective-permute-start(f32[46,8,128]{2,1,0:T(8,128)S(1)} %pad_maximum_fusion), channel_id=1, source_target_pairs={{0,2},{2,4},{4,6},{6,8},{8,10},{10,12},{12,14},{14,16},{16,18},{18... | collective-permute-start | bytes 565256 | tf_op jit(solution)/shard_map/ppermute | solution.py:826
  74.4 8.4 %collective-permute-start.4 = (f32[46,8,128]{2,1,0:T(8,128)}, f32[46,8,128]{2,1,0:T(8,128)S(1)}, u32[]{:S(2)}, u32[]{:S(2)}) collective-permute-start(f32[46,8,128]{2,1,0:T(8,128)} %pad_maximum_fusion.1), channel_id=1, source_target_pairs={{2,0},{4,2},{6,4},{8,6},{10,8},{12,10},{14,12},{16,14},{18,16},{20... | collective-permute-start | bytes 565256 | tf_op jit(solution)/shard_map/ppermute | solution.py:827
  84.5 1.3 collective-permute-start.5
  85.8 12.8 %collective-permute-start.6 = (f32[192,128]{1,0:T(8,128)S(1)}, f32[192,128]{1,0:T(8,128)S(1)}, u32[]{:S(2)}, u32[]{:S(2)}) collective-permute-start(f32[192,128]{1,0:T(8,128)S(1)} %pad_maximum_fusion.4), channel_id=1, source_target_pairs={{0,32},{32,64},{64,96},{96,128},{128,160},{160,192},{192,224},{1,3... | collective-permute-start | bytes 294920 | tf_op jit(solution)/shard_map/ppermute | solution.py:818
  90.9 7.7 %collective-permute-start.7 = (f32[192,128]{1,0:T(8,128)S(1)}, f32[192,128]{1,0:T(8,128)S(1)}, u32[]{:S(2)}, u32[]{:S(2)}) collective-permute-start(f32[192,128]{1,0:T(8,128)S(1)} %pad_maximum_fusion.5), channel_id=1, source_target_pairs={{32,0},{64,32},{96,64},{128,96},{160,128},{192,160},{224,192},{33,... | collective-permute-start | bytes 294920 | tf_op jit(solution)/shard_map/ppermute | solution.py:819
  98.7 6.5 %collective-permute-start.8 = (f32[46,4,128]{2,1,0:T(4,128)S(1)}, f32[46,4,128]{2,1,0:T(4,128)S(1)}, u32[]{:S(2)}, u32[]{:S(2)}) collective-permute-start(f32[46,4,128]{2,1,0:T(4,128)S(1)} %pad_maximum_fusion.6), channel_id=1, source_target_pairs={{0,2},{2,4},{4,6},{6,8},{8,10},{10,12},{12,14},{14,16},{16,18},{18... | collective-permute-start | bytes 282632 | tf_op jit(solution)/shard_map/ppermute | solution.py:826
  102.1 6.5 %collective-permute-start.9 = (f32[46,4,128]{2,1,0:T(4,128)S(1)}, f32[46,4,128]{2,1,0:T(4,128)S(1)}, u32[]{:S(2)}, u32[]{:S(2)}) collective-permute-start(f32[46,4,128]{2,1,0:T(4,128)S(1)} %pad_maximum_fusion.7), channel_id=1, source_target_pairs={{2,0},{4,2},{6,4},{8,6},{10,8},{12,10},{14,12},{16,14},{18,16},{20... | collective-permute-start | bytes 282632 | tf_op jit(solution)/shard_map/ppermute | solution.py:827
  124.7 1.5 copy-start.2
  126.1 42.8 %all-to-all-start.2 = ((f32[16,304,128]{2,1,0:T(8,128)}), f32[16,304,128]{2,1,0:T(8,128)S(1)}, u32[]{:S(2)}, u32[]{:S(2)}) async-start(f32[16,304,128]{2,1,0:T(8,128)} %copy-done.2), calls=%async_computation.2 | async-start | bytes 4980736 | tf_op jit(solution)/shard_map/all_to_all | solution.py:881

commit v6 on v5

--- a/solution.py
+++ b/solution.py
@@ -265,7 +265,7 @@
             total = total + ahead(here, offset) + behind(here, offset)
         return total
 
-    def step(i, carry):
+    def step(i, lower):
         x = pl.program_id(0) * STEP_X + i + 1
         volume = planes[x]
         weight = jnp.where(inside, volume, 0.0)
@@ -278,15 +278,20 @@
             here = masses[x, c]
             spread = neighbours(here, masses[x - 1, c], masses[x + 1, c]) * inverse
             put(updated, (i, c), compact(jnp.where(cut, spread, here), 0, lanes))
-        put(apertures, (i, 0), compact(jnp.minimum(volume, planes[x - 1]), 0, lanes))
-        put(apertures, (i, 1), compact(jnp.minimum(volume, planes[x + 1]), 0, lanes))
+        if lower is None:
+            lower = compact(jnp.minimum(volume, planes[x - 1]), 0, lanes)
+        upper = compact(jnp.minimum(volume, planes[x + 1]), 0, lanes)
+        put(apertures, (i, 0), lower)
+        put(apertures, (i, 1), upper)
         for axis, offset in ((1, PADDED), (2, 1)):
             aperture = jnp.minimum(volume, ahead(volume, offset))
             put(apertures, (i, 2 * axis), compact(aperture, -offset, lanes))
             put(apertures, (i, 2 * axis + 1), compact(aperture, 0, lanes))
-        return carry
-
-    loop(0, STEP_X, lambda i: step(i, 0), 4)
+        return upper
+
+    lower = None
+    for i in range(STEP_X):
+        lower = step(i, lower)
 
 
 STEP_X = 4

time: 180 us -> 179 us (level)
  no operation moved by 1% of the time
where the time goes in v6:
time: 179 us; the launch traced here: 178 us
  Pallas kernels  91.3 us (51%)
  starting transfers between devices  51.2 us (29%)
  waiting for transfers between devices  26.8 us (15%)
  local copies, waits for them, and re-layouts  6.19 us (3%)
  other arithmetic  1.89 us (1%)
    pallas_call x1, Pallas kernels, update_call(): pl.pallas_call(update_kernel, grid=(BOX // STEP_X,), in_specs=[VMEM_SPEC,...  32 us
    all_to_all x3, starting transfers between devices, exchange(): return lax.all_to_all(rows, 'by', split_axis=0, concat_axis=0, tiled=True)  25.4 us
    pallas_call x1, Pallas kernels, flux_call(): pl.pallas_call(functools.partial(flux_kernel, lanes_by=lanes_by), in_spec...  23 us
    pallas_call x1, Pallas kernels, solve_call(): pl.pallas_call(functools.partial(solve_kernel, count=count, lanes_by=lane...  16.1 us
    ppermute x2, waiting for transfers between devices, halo(): x_hi = lax.ppermute(jnp.concatenate([first, middle[0]], axis=0), 'bx', down)  11.6 us
    pallas_call x1, Pallas kernels, correct_call(): pl.pallas_call(correct_kernel, grid=(BOX // STEP_X,), in_specs=[SMEM_SPEC...  10.4 us
    ppermute x2, starting transfers between devices, halo(): x_lo = lax.ppermute(jnp.concatenate([last, middle[-1]], axis=0), 'bx', up)  10.1 us
    ppermute x2, starting transfers between devices, halo(): y_lo = lax.ppermute(edge(BOX - depth), 'by', y_up)  6.76 us
  transfers between devices with their start and end apart: 13, of which 10 were waited for; matrix products, arithmetic and copies ran while one was open for 1% of the time, Pallas kernels for 32%

profile of v6, /device:TPU:98, one launch (start us, length us, event | category | flops | bytes accessed | tf_op | source)
XLA Modules:
  0.0 178.3 jit_solution(12347055699006703923)
XLA Ops:
  0.6 0.8 copy.9
  1.4 0.6 reshape_squeeze.3.table
  2.0 6.6 %volume_rows.1 = f32[16,256,128]{2,1,0:T(8,128)} custom-call(s32[64]{0:T(128)} %reshape_squeeze.3.table, s32[1]{0:T(128)} %bitcast.3.own, s32[8,39304]{1,0:T(8,128)} %fraction.3), custom_call_target="tpu_custom_call" | custom-call | tf_op jit(solution)/shard_map/volume_rows/pallas_call | solution.py:363
  8.6 0.0 copy-start.4
  8.6 0.0 copy-start.3
  8.6 7.5 %all-to-all-start.1 = ((f32[16,256,128]{2,1,0:T(8,128)}), f32[16,256,128]{2,1,0:T(8,128)S(1)}, u32[]{:S(2)}, u32[]{:S(2)}) async-start(f32[16,256,128]{2,1,0:T(8,128)} %volume_rows.1), calls=%async_computation.1 | async-start | bytes 4194304 | tf_op jit(solution)/shard_map/all_to_all | solution.py:886
  16.1 0.0 copy-done.4
  16.1 0.1 fusion
  16.2 0.1 reduce_window_sum.11
  16.3 0.2 select_reduce_fusion
  16.5 0.1 reshape.57
  16.5 0.1 copy.10
  16.6 0.0 copy-done.3
  16.6 0.5 select_reduce_fusion.3.slots
  17.2 23.0 %flux_rows.1 = (f32[34,8,1280]{2,1,0:T(8,128)}, f32[34,3,8,1280]{3,2,1,0:T(8,128)}, f32[16,256,128]{2,1,0:T(8,128)}) custom-call(s32[16]{0:T(128)} %select_reduce_fusion.3.slots, f32[3,8,39304]{2,1,0:T(8,128)} %bitcast.30, s32[8,39304]{1,0:T(8,128)} %fraction.3), custom_call_target="tpu_custom_call" | custom-call | tf_op jit(solution)/shard_map/flux_rows/pallas_call | solution.py:380
  40.1 3.1 %all-to-all-done.1.refs_0_.refs_1_.refs_2_.refs_3_ = f32[16,256,128]{2,1,0:T(8,128)S(1)} async-done(((f32[16,256,128]{2,1,0:T(8,128)}), f32[16,256,128]{2,1,0:T(8,128)S(1)}, u32[]{:S(2)}, u32[]{:S(2)}) %all-to-all-start.1) | async-done | bytes 2097184 | tf_op jit(solution)/shard_map/all_to_all | solution.py:886
  43.2 0.0 copy-start
  43.2 1.3 copy-done
  44.6 8.3 %all-to-all-start = ((f32[16,256,128]{2,1,0:T(8,128)}), f32[16,256,128]{2,1,0:T(8,128)S(1)}, u32[]{:S(2)}, u32[]{:S(2)}) async-start(f32[16,256,128]{2,1,0:T(8,128)} %get-tuple-element.28), calls=%async_computation | async-start | bytes 4194304 | tf_op jit(solution)/shard_map/all_to_all | solution.py:886
  52.8 0.2 dynamic-slice_reduce_fusion.table
  53.0 0.0 copy-start.1
  53.0 1.6 copy-done.1
  54.6 1.6 brick.2
  56.2 0.1 collective-permute-start
  56.4 1.2 collective-permute-done.refs_3_
  57.5 5.0 %collective-permute-start.1 = (f32[192,128]{1,0:T(8,128)S(1)}, f32[192,128]{1,0:T(8,128)S(1)}, u32[]{:S(2)}, u32[]{:S(2)}) collective-permute-start(f32[192,128]{1,0:T(8,128)S(1)} %pad_maximum_fusion.2), channel_id=1, source_target_pairs={{0,32},{32,64},{64,96},{96,128},{128,160},{160,192},{192,224},{1,3... | collective-permute-start | bytes 294920 | tf_op jit(solution)/shard_map/ppermute | solution.py:823
  62.6 1.9 %collective-permute-start.2 = (f32[192,128]{1,0:T(8,128)S(1)}, f32[192,128]{1,0:T(8,128)S(1)}, u32[]{:S(2)}, u32[]{:S(2)}) collective-permute-start(f32[192,128]{1,0:T(8,128)S(1)} %pad_maximum_fusion.3), channel_id=1, source_target_pairs={{32,0},{64,32},{96,64},{128,96},{160,128},{192,160},{224,192},{33,... | collective-permute-start | bytes 294920 | tf_op jit(solution)/shard_map/ppermute | solution.py:824
  64.5 5.8 %collective-permute-done.2.refs_2_ = f32[192,128]{1,0:T(8,128)S(1)} collective-permute-done((f32[192,128]{1,0:T(8,128)S(1)}, f32[192,128]{1,0:T(8,128)S(1)}, u32[]{:S(2)}, u32[]{:S(2)}) %collective-permute-start.2) | collective-permute-done | bytes 98336 | tf_op jit(solution)/shard_map/ppermute | solution.py:824
  70.3 0.0 collective-permute-done.1.refs_1_
  70.4 3.4 %collective-permute-start.3 = (f32[46,8,128]{2,1,0:T(8,128)S(1)}, f32[46,8,128]{2,1,0:T(8,128)S(1)}, u32[]{:S(2)}, u32[]{:S(2)}) collective-permute-start(f32[46,8,128]{2,1,0:T(8,128)S(1)} %pad_maximum_fusion), channel_id=1, source_target_pairs={{0,2},{2,4},{4,6},{6,8},{8,10},{10,12},{12,14},{14,16},{16,18},{18... | collective-permute-start | bytes 565256 | tf_op jit(solution)/shard_map/ppermute | solution.py:831
  73.8 0.7 pad_maximum_fusion.1
  74.4 2.5 %collective-permute-start.4 = (f32[46,8,128]{2,1,0:T(8,128)}, f32[46,8,128]{2,1,0:T(8,128)S(1)}, u32[]{:S(2)}, u32[]{:S(2)}) collective-permute-start(f32[46,8,128]{2,1,0:T(8,128)} %pad_maximum_fusion.1), channel_id=1, source_target_pairs={{2,0},{4,2},{6,4},{8,6},{10,8},{12,10},{14,12},{16,14},{18,16},{20... | collective-permute-start | bytes 565256 | tf_op jit(solution)/shard_map/ppermute | solution.py:832
  76.9 2.7 %all-to-all-done.refs_0_.refs_1_.refs_2_.refs_3_ = f32[16,256,128]{2,1,0:T(8,128)S(1)} async-done(((f32[16,256,128]{2,1,0:T(8,128)}), f32[16,256,128]{2,1,0:T(8,128)S(1)}, u32[]{:S(2)}, u32[]{:S(2)}) %all-to-all-start) | async-done | bytes 2097184 | tf_op jit(solution)/shard_map/all_to_all | solution.py:886
  79.6 2.3 %collective-permute-done.3.refs_4_ = f32[46,8,128]{2,1,0:T(8,128)S(1)} collective-permute-done((f32[46,8,128]{2,1,0:T(8,128)S(1)}, f32[46,8,128]{2,1,0:T(8,128)S(1)}, u32[]{:S(2)}, u32[]{:S(2)}) %collective-permute-start.3) | collective-permute-done | bytes 188448 | tf_op jit(solution)/shard_map/ppermute | solution.py:831
  81.9 1.0 collective-permute-done.4.refs_5_
  82.9 1.6 brick.3
  84.5 0.1 collective-permute-start.5
  84.6 1.2 collective-permute-done.5.refs_9_
  85.8 5.0 %collective-permute-start.6 = (f32[192,128]{1,0:T(8,128)S(1)}, f32[192,128]{1,0:T(8,128)S(1)}, u32[]{:S(2)}, u32[]{:S(2)}) collective-permute-start(f32[192,128]{1,0:T(8,128)S(1)} %pad_maximum_fusion.4), channel_id=1, source_target_pairs={{0,32},{32,64},{64,96},{96,128},{128,160},{160,192},{192,224},{1,3... | collective-permute-start | bytes 294920 | tf_op jit(solution)/shard_map/ppermute | solution.py:823
  90.9 1.9 %collective-permute-start.7 = (f32[192,128]{1,0:T(8,128)S(1)}, f32[192,128]{1,0:T(8,128)S(1)}, u32[]{:S(2)}, u32[]{:S(2)}) collective-permute-start(f32[192,128]{1,0:T(8,128)S(1)} %pad_maximum_fusion.5), channel_id=1, source_target_pairs={{32,0},{64,32},{96,64},{128,96},{160,128},{192,160},{224,192},{33,... | collective-permute-start | bytes 294920 | tf_op jit(solution)/shard_map/ppermute | solution.py:824
  92.8 5.8 %collective-permute-done.7.refs_8_ = f32[192,128]{1,0:T(8,128)S(1)} collective-permute-done((f32[192,128]{1,0:T(8,128)S(1)}, f32[192,128]{1,0:T(8,128)S(1)}, u32[]{:S(2)}, u32[]{:S(2)}) %collective-permute-start.7) | collective-permute-done | bytes 98336 | tf_op jit(solution)/shard_map/ppermute | solution.py:824
  98.6 0.0 collective-permute-done.6.refs_7_
  98.7 3.4 %collective-permute-start.8 = (f32[46,4,128]{2,1,0:T(4,128)S(1)}, f32[46,4,128]{2,1,0:T(4,128)S(1)}, u32[]{:S(2)}, u32[]{:S(2)}) collective-permute-start(f32[46,4,128]{2,1,0:T(4,128)S(1)} %pad_maximum_fusion.6), channel_id=1, source_target_pairs={{0,2},{2,4},{4,6},{6,8},{8,10},{10,12},{12,14},{14,16},{16,18},{18... | collective-permute-start | bytes 282632 | tf_op jit(solution)/shard_map/ppermute | solution.py:831
  102.1 2.5 %collective-permute-start.9 = (f32[46,4,128]{2,1,0:T(4,128)S(1)}, f32[46,4,128]{2,1,0:T(4,128)S(1)}, u32[]{:S(2)}, u32[]{:S(2)}) collective-permute-start(f32[46,4,128]{2,1,0:T(4,128)S(1)} %pad_maximum_fusion.7), channel_id=1, source_target_pairs={{2,0},{4,2},{6,4},{8,6},{10,8},{12,10},{14,12},{16,14},{18,16},{20... | collective-permute-start | bytes 282632 | tf_op jit(solution)/shard_map/ppermute | solution.py:832
  104.5 0.1 select_reduce_fusion.2.box_of_row
  104.6 0.5 collective-permute-done.8.refs_10_
  105.1 3.4 %collective-permute-done.9.refs_11_ = f32[46,4,128]{2,1,0:T(4,128)S(1)} collective-permute-done((f32[46,4,128]{2,1,0:T(4,128)S(1)}, f32[46,4,128]{2,1,0:T(4,128)S(1)}, u32[]{:S(2)}, u32[]{:S(2)}) %collective-permute-start.9) | collective-permute-done | bytes 94240 | tf_op jit(solution)/shard_map/ppermute | solution.py:832
  108.5 16.1 %solve.1 = (f32[32,32,128]{2,1,0:T(8,128)}, f32[16,304,128]{2,1,0:T(8,128)S(1)}) custom-call(s32[16]{0:T(128)S(1)} %select_reduce_fusion.2.box_of_row, s32[1]{0:T(128)} %bitcast.2.side, f32[1024,128]{1,0:T(8,128)S(1)} %get-tuple-element.33.refs_0_, f32[192,128]{1,0:T(8,128)S(1)} %collective-permute-done.1.refs_1_, ...), custom_call_target="tpu_custom_call" | custom-call | tf_op jit(solution)/shard_map/solve/pallas_call | solution.py:840
  124.7 0.0 copy-start.2
  124.7 1.4 copy-done.2
  126.1 9.7 %all-to-all-start.2 = ((f32[16,304,128]{2,1,0:T(8,128)}), f32[16,304,128]{2,1,0:T(8,128)S(1)}, u32[]{:S(2)}, u32[]{:S(2)}) async-start(f32[16,304,128]{2,1,0:T(8,128)} %copy-done.2), calls=%async_computation.2 | async-start | bytes 4980736 | tf_op jit(solution)/shard_map/all_to_all | solution.py:886
  135.8 32.0 %updated.1 = (f32[32,3,8,1024]{3,2,1,0:T(8,128)}, f32[32,6,8,1024]{3,2,1,0:T(8,128)}) custom-call(f32[34,3,8,1280]{3,2,1,0:T(8,128)} %get-tuple-element.24.masses, f32[34,8,1280]{2,1,0:T(8,128)} %get-tuple-element.25.planes), custom_call_target="tpu_custom_call" | custom-call | tf_op jit(solution)/shard_map/updated/pallas_call | solution.py:401
  167.8 0.1 select_reduce_fusion.1.rows
  167.9 0.0 all-to-all-done.2.returned
  167.9 10.4 %corrected.1 = f32[3,8,32768]{2,1,0:T(8,128)} custom-call(s32[8]{0:T(128)S(1)} %select_reduce_fusion.1.rows, f32[32,3,8,1024]{3,2,1,0:T(8,128)} %get-tuple-element.26.updated, f32[32,6,8,1024]{3,2,1,0:T(8,128)} %get-tuple-element.27.apertures, f32[16,304,128]{2,1,0:T(8,128)S(1)} %all-to-all-done.2.returned), custom_call_target="tpu_custom_call" | custom-call | tf_op jit(solution)/shard_map/corrected/pallas_call | solution.py:415
  (19 shorter events, 0.2 us)
Async XLA Ops:
  8.6 7.5 %copy-start.4 = (s32[64]{0:T(128)S(1)}, s32[64]{0:T(128)}, u32[]{:S(2)}) copy-start(s32[64]{0:T(128)} %reshape_squeeze.3.table) | copy-start | bytes 772
  8.6 8.0 %copy-start.3 = (s32[1,16,1,4]{1,3,2,0:T(4,128)S(1)}, s32[1,16,1,4]{1,3,2,0:T(4,128)}, u32[]{:S(2)}) copy-start(s32[1,16,1,4]{1,3,2,0:T(4,128)} %param.5) | copy-start | bytes 772
  8.6 34.6 %all-to-all-start.1 = ((f32[16,256,128]{2,1,0:T(8,128)}), f32[16,256,128]{2,1,0:T(8,128)S(1)}, u32[]{:S(2)}, u32[]{:S(2)}) async-start(f32[16,256,128]{2,1,0:T(8,128)} %volume_rows.1), calls=%async_computation.1 | async-start | bytes 4194304 | tf_op jit(solution)/shard_map/all_to_all | solution.py:886
  43.2 1.3 copy-start
  44.6 35.0 %all-to-all-start = ((f32[16,256,128]{2,1,0:T(8,128)}), f32[16,256,128]{2,1,0:T(8,128)S(1)}, u32[]{:S(2)}, u32[]{:S(2)}) async-start(f32[16,256,128]{2,1,0:T(8,128)} %get-tuple-element.28), calls=%async_computation | async-start | bytes 4194304 | tf_op jit(solution)/shard_map/all_to_all | solution.py:886
  53.0 1.6 copy-start.1
  56.2 1.3 collective-permute-start
  57.5 12.8 %collective-permute-start.1 = (f32[192,128]{1,0:T(8,128)S(1)}, f32[192,128]{1,0:T(8,128)S(1)}, u32[]{:S(2)}, u32[]{:S(2)}) collective-permute-start(f32[192,128]{1,0:T(8,128)S(1)} %pad_maximum_fusion.2), channel_id=1, source_target_pairs={{0,32},{32,64},{64,96},{96,128},{128,160},{160,192},{192,224},{1,3... | collective-permute-start | bytes 294920 | tf_op jit(solution)/shard_map/ppermute | solution.py:823
  62.6 7.7 %collective-permute-start.2 = (f32[192,128]{1,0:T(8,128)S(1)}, f32[192,128]{1,0:T(8,128)S(1)}, u32[]{:S(2)}, u32[]{:S(2)}) collective-permute-start(f32[192,128]{1,0:T(8,128)S(1)} %pad_maximum_fusion.3), channel_id=1, source_target_pairs={{32,0},{64,32},{96,64},{128,96},{160,128},{192,160},{224,192},{33,... | collective-permute-start | bytes 294920 | tf_op jit(solution)/shard_map/ppermute | solution.py:824
  70.4 11.5 %collective-permute-start.3 = (f32[46,8,128]{2,1,0:T(8,128)S(1)}, f32[46,8,128]{2,1,0:T(8,128)S(1)}, u32[]{:S(2)}, u32[]{:S(2)}) collective-permute-start(f32[46,8,128]{2,1,0:T(8,128)S(1)} %pad_maximum_fusion), channel_id=1, source_target_pairs={{0,2},{2,4},{4,6},{6,8},{8,10},{10,12},{12,14},{14,16},{16,18},{18... | collective-permute-start | bytes 565256 | tf_op jit(solution)/shard_map/ppermute | solution.py:831
  74.4 8.4 %collective-permute-start.4 = (f32[46,8,128]{2,1,0:T(8,128)}, f32[46,8,128]{2,1,0:T(8,128)S(1)}, u32[]{:S(2)}, u32[]{:S(2)}) collective-permute-start(f32[46,8,128]{2,1,0:T(8,128)} %pad_maximum_fusion.1), channel_id=1, source_target_pairs={{2,0},{4,2},{6,4},{8,6},{10,8},{12,10},{14,12},{16,14},{18,16},{20... | collective-permute-start | bytes 565256 | tf_op jit(solution)/shard_map/ppermute | solution.py:832
  84.5 1.3 collective-permute-start.5
  85.8 12.8 %collective-permute-start.6 = (f32[192,128]{1,0:T(8,128)S(1)}, f32[192,128]{1,0:T(8,128)S(1)}, u32[]{:S(2)}, u32[]{:S(2)}) collective-permute-start(f32[192,128]{1,0:T(8,128)S(1)} %pad_maximum_fusion.4), channel_id=1, source_target_pairs={{0,32},{32,64},{64,96},{96,128},{128,160},{160,192},{192,224},{1,3... | collective-permute-start | bytes 294920 | tf_op jit(solution)/shard_map/ppermute | solution.py:823
  90.9 7.7 %collective-permute-start.7 = (f32[192,128]{1,0:T(8,128)S(1)}, f32[192,128]{1,0:T(8,128)S(1)}, u32[]{:S(2)}, u32[]{:S(2)}) collective-permute-start(f32[192,128]{1,0:T(8,128)S(1)} %pad_maximum_fusion.5), channel_id=1, source_target_pairs={{32,0},{64,32},{96,64},{128,96},{160,128},{192,160},{224,192},{33,... | collective-permute-start | bytes 294920 | tf_op jit(solution)/shard_map/ppermute | solution.py:824
  98.7 6.5 %collective-permute-start.8 = (f32[46,4,128]{2,1,0:T(4,128)S(1)}, f32[46,4,128]{2,1,0:T(4,128)S(1)}, u32[]{:S(2)}, u32[]{:S(2)}) collective-permute-start(f32[46,4,128]{2,1,0:T(4,128)S(1)} %pad_maximum_fusion.6), channel_id=1, source_target_pairs={{0,2},{2,4},{4,6},{6,8},{8,10},{10,12},{12,14},{14,16},{16,18},{18... | collective-permute-start | bytes 282632 | tf_op jit(solution)/shard_map/ppermute | solution.py:831
  102.1 6.5 %collective-permute-start.9 = (f32[46,4,128]{2,1,0:T(4,128)S(1)}, f32[46,4,128]{2,1,0:T(4,128)S(1)}, u32[]{:S(2)}, u32[]{:S(2)}) collective-permute-start(f32[46,4,128]{2,1,0:T(4,128)S(1)} %pad_maximum_fusion.7), channel_id=1, source_target_pairs={{2,0},{4,2},{6,4},{8,6},{10,8},{12,10},{14,12},{16,14},{18,16},{20... | collective-permute-start | bytes 282632 | tf_op jit(solution)/shard_map/ppermute | solution.py:832
  124.7 1.5 copy-start.2
  126.1 41.8 %all-to-all-start.2 = ((f32[16,304,128]{2,1,0:T(8,128)}), f32[16,304,128]{2,1,0:T(8,128)S(1)}, u32[]{:S(2)}, u32[]{:S(2)}) async-start(f32[16,304,128]{2,1,0:T(8,128)} %copy-done.2), calls=%async_computation.2 | async-start | bytes 4980736 | tf_op jit(solution)/shard_map/all_to_all | solution.py:886
